TPU v7x, 32 devices: a whole 2x2x4 slice. The times are simulated.
32 devices in a mesh: group: 2 (over y), ctx: 4 (over z), feat: 2 (over x), ex: 2 (over core).
Axes of the slice: x: 2, y: 2, z: 4, core: 2. Of those that a mesh axis runs over, the one named last changes fastest.
Arguments:
- hidden: bfloat16 [8, 512, 8192], P(('group', 'feat', 'ex'), 'ctx'), parts along dimension 0, may hold values from -6 to 6
- cotangent: bfloat16 [8, 512, 1024], P(('group', 'feat', 'ex'), 'ctx'), parts along dimension 0, may hold values from -6 to 6
- adapter_down_factor: bfloat16 [8192, 16], replicated, may hold values from -0.0625 to 0.0625
- projection: bfloat16 [16384, 8192], P('ctx', 'feat'), may hold values from -6 to 6
- lengths: int32 [8], P(('group', 'feat', 'ex')), parts along dimension 0, may hold values from 128 to 512, as said below
- slot_example_order: int32 [8], P('group'), parts along dimension 0, may hold values from 0 to 3, each once
Outputs:
- features: float32 [8, 8192], P(('group', 'ex'), 'feat'), parts along dimension 0
There are 2 independent parts, one for each index of `group`. A program takes and returns all parts, laid end to end along the dimension named above; an argument that names none is the same for every part. Nothing has to cross between parts.
Inputs may be any that keep to these rules, and one draw needn't show every extreme that they name: `lengths`: some example has exactly 512 valid positions and some exactly one quarter of 512.
All inputs are finite; a program needn't handle non-finite values.
Results may differ from a plain program's by a relative error of at most 0.0042.
Values may be sent and summed in bfloat16 or wider, within the bound.
No kernel may reach another device: no remote copies, remote signals or barrier semaphores. Data moves between devices by JAX's collectives and lax.ppermute only.
A program may use at most 64 MiB of HBM per device.

v0:
```python
import jax
import jax.numpy as jnp
from jax import lax
from jax.sharding import PartitionSpec as P

FEATS = 8192


def per_device(hidden, cotangent, adapter_down_factor, projection, lengths, slot_example_order):
    ctx_count = lax.axis_size("ctx")
    feat_count = lax.axis_size("feat")
    example_groups = lax.axis_size("ex")
    example_count, token_count, model_width = hidden.shape
    down_factor_rows = jnp.dot(
        hidden.reshape(example_count * token_count, model_width),
        adapter_down_factor,
        preferred_element_type=jnp.float32,
    )
    down_factor_rows = down_factor_rows.astype(jnp.bfloat16).reshape(example_count, token_count, -1)
    position = lax.axis_index("ctx") * token_count + lax.iota(jnp.int32, token_count)
    retain_mask = (position[None, :] < lengths[:, None]).astype(jnp.bfloat16)
    down_factor_rows = down_factor_rows * retain_mask[:, :, None]
    partial_value = jnp.einsum(
        "etr,etj->erj", down_factor_rows, cotangent, preferred_element_type=jnp.float32
    )
    partial_value = partial_value.reshape(example_count, -1)
    block_size = partial_value.shape[1] // ctx_count
    summed_all = lax.psum(partial_value, "ctx")
    owned_rows = lax.dynamic_slice_in_dim(
        summed_all, lax.axis_index("ctx") * block_size, block_size, 1
    )
    grad_rows = owned_rows.astype(jnp.bfloat16)
    projected = jnp.dot(
        lax.all_gather(grad_rows, "feat", axis=0, tiled=True),
        projection,
        preferred_element_type=jnp.float32,
    )
    summed = lax.psum(projected, "ctx")
    squares = lax.psum(jnp.sum(summed * summed, axis=1), "feat")
    scaled = summed / jnp.sqrt(squares / FEATS + 1e-06)[:, None]
    everything = lax.all_gather(scaled, "ex", axis=0, tiled=True)
    arranged = jnp.transpose(
        slot_example_order.reshape(feat_count, example_groups, example_count), (1, 0, 2)
    ).reshape(-1)
    own_rows = everything.shape[0] // example_groups
    wanted = lax.axis_index("ex") * own_rows + lax.iota(jnp.int32, own_rows)
    select = (arranged[None, :] == wanted[:, None]).astype(jnp.float32)
    return jnp.dot(
        select, everything, precision=lax.Precision.HIGHEST, preferred_element_type=jnp.float32
    )


def solution(mesh):
    in_specs = (
        P(("group", "feat", "ex"), "ctx", None),
        P(("group", "feat", "ex"), "ctx", None),
        P(),
        P("ctx", "feat"),
        P(("group", "feat", "ex")),
        P("group"),
    )
    out_specs = P(("group", "ex"), "feat")
    return jax.shard_map(
        per_device, mesh=mesh, in_specs=in_specs, out_specs=out_specs, check_vma=False
    )
```

profile of v0, /device:TPU:0, one launch (start us, length us, event | category | flops | bytes accessed | tf_op | source)
XLA Modules:
  0.0 76.8 jit_solution(9681998552901455173)
XLA Ops:
  0.0 0.0 copy-start
  0.8 0.8 %copy-done = bf16[1,128,8192]{2,1,0:T(8,128)(2,1)S(1)} copy-done((bf16[1,128,8192]{2,1,0:T(8,128)(2,1)S(1)}, bf16[1,128,8192]{2,1,0:T(8,128)(2,1)}, u32[]{:S(2)}) %copy-start) | copy-done | bytes 2097176
  1.6 1.9 %convolution_bitcast_fusion = f32[1,1,16,1024]{3,2,1,0:T(8,128)S(1)} fusion(bf16[8192,16]{0,1:T(8,128)(2,1)} %param.8, bf16[1,128,8192]{2,1,0:T(8,128)(2,1)S(1)} %copy-done, bf16[1,128,1024]{2,1,0:T(8,128)(2,1)} %param.7, bf16[128]{0:T(256)(128)(2,1)S(1)} %compare_convert_fusion), kind=kOutput, calls=%fused_computation.2 | convolution fusion | flops 37752832 | bytes 2687232 | tf_op jit(solution)/shard_map/etr,etj->erj/dot_general | solution.py:23
  3.5 0.1 copy.11
  3.6 32.0 %psum.21 = bf16[1,16384]{1,0:T(2,128)(2,1)S(1)} all-reduce(f32[1,16384]{1,0:T(1,128)S(1)} %bitcast.31), channel_id=1, replica_groups=mesh['group'=2,'ctx'=4,'feat'=2,'ex'=2] {'ctx'}, use_global_device_ids=true, to_apply=%region_0.0 | all-reduce | flops 16384 | bytes 98304 | tf_op jit(solution)/shard_map/psum | solution.py:28
  35.6 4.4 %all-gather = bf16[2,1,4096]{2,1,0:T(2,128)(2,1)S(1)} all-gather(bf16[1,1,4096]{2,1,0:T(2,128)(2,1)S(1)} %convert_bitcast_fusion), channel_id=1, replica_groups=mesh['group'=2,'ctx'=4,'feat'=2,'ex'=2] {'feat'}, dimensions={0}, use_global_device_ids=true | all-gather | bytes 24576 | tf_op jit(solution)/shard_map/all_gather | solution.py:34
  40.0 0.0 copy-start.1
  40.0 12.8 %fusion.11 = f32[2,4096]{1,0:T(2,128)S(1)} fusion(bf16[4096,4096]{1,0:T(8,128)(2,1)} %param.9, bf16[2,1,4096]{2,1,0:T(2,128)(2,1)S(1)} %all-gather), kind=kOutput, calls=%fused_computation.8 | convolution fusion | flops 67108864 | bytes 33603584 | tf_op jit(solution)/shard_map/dot_general | solution.py:33
  52.8 15.8 %psum.22 = f32[2,4096]{1,0:T(2,128)S(1)} all-reduce(f32[2,4096]{1,0:T(2,128)S(1)} %fusion.11), channel_id=1, replica_groups=mesh['group'=2,'ctx'=4,'feat'=2,'ex'=2] {'ctx'}, use_global_device_ids=true, to_apply=%region_1.0 | all-reduce | flops 8192 | bytes 65536 | tf_op jit(solution)/shard_map/psum | solution.py:38
  68.6 0.1 multiply_reduce_fusion
  68.7 4.9 %psum.23 = f32[2]{0:T(128)S(1)} all-reduce(f32[2]{0:T(128)S(1)} %multiply_reduce_fusion), channel_id=1, replica_groups=mesh['group'=2,'ctx'=4,'feat'=2,'ex'=2] {'feat'}, use_global_device_ids=true, to_apply=%region_3.0 | all-reduce | flops 2 | bytes 16 | tf_op jit(solution)/shard_map/psum | solution.py:39
  73.7 0.1 divide_bitcast_fusion
  73.8 1.9 %all-gather.1 = f32[2,2,4096]{2,1,0:T(2,128)S(1)} all-gather(f32[1,2,4096]{2,1,0:T(2,128)S(1)} %divide_bitcast_fusion), channel_id=1, replica_groups=mesh['group'=2,'ctx'=4,'feat'=2,'ex'=2] {'ex'}, dimensions={0}, use_global_device_ids=true | all-gather | bytes 98304 | tf_op jit(solution)/shard_map/all_gather | solution.py:41
  75.6 0.1 reshape.45
  75.7 0.0 copy-done.1
  75.7 0.1 reshape.38
  75.8 0.1 copy.9
  75.9 0.1 eq.15
  76.0 0.9 %fusion.15 = f32[2,4096]{1,0:T(2,128)} fusion(f32[4,4096]{1,0:T(4,128)S(1)} %reshape.45, s32[4]{0:T(128)S(1)} %eq.15, s32[2]{0:T(128)S(1)} %iota_add_fusion), kind=kOutput, calls=%fused_computation.14 | convolution fusion | flops 393224 | bytes 98328 | tf_op jit(solution)/shard_map/dot_general | solution.py:48
  (4 shorter events, 0.0 us)
Async XLA Ops:
  0.0 1.6 %copy-start = (bf16[1,128,8192]{2,1,0:T(8,128)(2,1)S(1)}, bf16[1,128,8192]{2,1,0:T(8,128)(2,1)}, u32[]{:S(2)}) copy-start(bf16[1,128,8192]{2,1,0:T(8,128)(2,1)} %param.6) | copy-start | bytes 6291460
  40.0 35.7 %copy-start.1 = (s32[4]{0:T(128)S(1)}, s32[4]{0:T(128)}, u32[]{:S(2)}) copy-start(s32[4]{0:T(128)} %param.11) | copy-start | bytes 52
where the time goes:
time: 77.1 us; the launch traced here: 76.8 us
  blocking collectives  58.9 us (76%)
  matrix products  15.6 us (20%)
  local copies, waits for them, and re-layouts  1.22 us (2%)
  between operations  0.88 us (1%)
    psum x1, blocking collectives, per_device(): summed_all = lax.psum(partial_value, 'ctx')  32 us
    psum x1, blocking collectives, per_device(): summed = lax.psum(projected, 'ctx')  15.8 us
    dot_general x1, matrix products, per_device(): jnp.dot(lax.all_gather(grad_rows, 'feat', axis=0, tiled=True), projection...  12.8 us
    psum x1, blocking collectives, per_device(): squares = lax.psum(jnp.sum(summed * summed, axis=1), 'feat')  4.93 us
    all_gather x1, blocking collectives, per_device(): lax.all_gather(grad_rows, 'feat', axis=0, tiled=True)  4.41 us
    dot_general x1, matrix products, per_device(): jnp.einsum('etr,etj->erj', down_factor_rows, cotangent, preferred_element...  1.87 us
    all_gather x1, blocking collectives, per_device(): everything = lax.all_gather(scaled, 'ex', axis=0, tiled=True)  1.85 us

commit v1 on v0

v1 whole, which is shorter than its diff:
```python
import jax
import jax.numpy as jnp
from jax import lax
from jax.experimental import pallas as pl
from jax.experimental.pallas import tpu as pltpu
from jax.sharding import PartitionSpec as P

FEATS = 8192


def partner_pairs(count, step):
    if count & (count - 1) == 0:
        return [(i, i ^ step) for i in range(count)]
    return [(i, (i + step) % count) for i in range(count)]


def target_of(index, count, step):
    if count & (count - 1) == 0:
        return index ^ step
    return lax.rem(index + step, count)


def source_of(index, count, step):
    if count & (count - 1) == 0:
        return index ^ step
    return lax.rem(index + count - step, count)


def swap(value, axis, count, step):
    return lax.ppermute(value, axis, partner_pairs(count, step))


def project_body(half_ref, rows_ref, projection_ref, out_ref):
    part = jnp.dot(rows_ref[...], projection_ref[...], preferred_element_type=jnp.float32)

    @pl.when(pl.program_id(0) == 0)
    def _():
        out_ref[...] = part

    @pl.when(pl.program_id(0) > 0)
    def _():
        out_ref[...] += part


def project(rows, projection, part_index, parts):
    depth, width = projection.shape
    own_width = width // parts
    block = min(512, depth)
    return pl.pallas_call(
        project_body,
        out_shape=jax.ShapeDtypeStruct((rows.shape[0], own_width), jnp.float32),
        grid_spec=pltpu.PrefetchScalarGridSpec(
            num_scalar_prefetch=1,
            grid=(depth // block,),
            in_specs=[
                pl.BlockSpec((rows.shape[0], block), lambda k, part: (0, k)),
                pl.BlockSpec((block, own_width), lambda k, part: (k, part[0])),
            ],
            out_specs=pl.BlockSpec((rows.shape[0], own_width), lambda k, part: (0, 0)),
        ),
    )(part_index, rows, projection)


def per_device(hidden, cotangent, adapter_down_factor, projection, lengths, slot_example_order):
    ctx_count = lax.axis_size("ctx")
    feat_count = lax.axis_size("feat")
    ex_count = lax.axis_size("ex")
    ctx, feat, ex = lax.axis_index("ctx"), lax.axis_index("feat"), lax.axis_index("ex")
    own, token_count, model_width = hidden.shape
    down_rows = jnp.dot(
        hidden.reshape(own * token_count, model_width),
        adapter_down_factor,
        preferred_element_type=jnp.float32,
    )
    down_rows = down_rows.astype(jnp.bfloat16).reshape(own, token_count, -1)
    position = ctx * token_count + lax.iota(jnp.int32, token_count)
    retain_mask = (position[None, :] < lengths[:, None]).astype(jnp.bfloat16)
    down_rows = down_rows * retain_mask[:, :, None]
    partial = jnp.einsum("etr,etj->erj", down_rows, cotangent, preferred_element_type=jnp.float32)

    blocks = partial.reshape(own, ctx_count, -1)
    block = lambda index: lax.dynamic_index_in_dim(blocks, index, 1, keepdims=False)
    grad = block(ctx)
    for step in range(1, ctx_count):
        grad = grad + swap(block(target_of(ctx, ctx_count, step)), "ctx", ctx_count, step)
    grad_rows = grad.astype(jnp.bfloat16)

    slots = slot_example_order.reshape(feat_count, ex_count, own)
    ex_parts = [grad_rows]
    ex_places = [ex]
    for step in range(1, ex_count):
        ex_parts.append(swap(grad_rows, "ex", ex_count, step))
        ex_places.append(source_of(ex, ex_count, step))
    of_chip = jnp.concatenate(ex_parts, axis=0)
    parts, ids = [of_chip], [jnp.concatenate([slots[feat, e] for e in ex_places])]
    for step in range(1, feat_count):
        parts.append(swap(of_chip, "feat", feat_count, step))
        place = source_of(feat, feat_count, step)
        ids.append(jnp.concatenate([slots[place, e] for e in ex_places]))
    everything = jnp.concatenate(parts, axis=0)
    held = jnp.concatenate(ids)
    count = everything.shape[0]
    select = (held[None, :] == lax.iota(jnp.int32, count)[:, None]).astype(jnp.bfloat16)
    ordered = jnp.dot(select, everything, preferred_element_type=jnp.float32).astype(jnp.bfloat16)

    product = project(ordered, projection, ex.astype(jnp.int32)[None], ex_count)
    per_ex = product.reshape(ex_count, count // ex_count, -1)
    row_part = lambda index: lax.dynamic_index_in_dim(per_ex, index, 0, keepdims=False)
    column_parts, column_places = [row_part(ex)], [ex]
    for step in range(1, ex_count):
        column_parts.append(swap(row_part(target_of(ex, ex_count, step)), "ex", ex_count, step))
        column_places.append(source_of(ex, ex_count, step))
    mine = jnp.stack(column_parts, axis=1)
    summed = mine
    for step in range(1, ctx_count):
        summed = summed + swap(mine, "ctx", ctx_count, step)
    own_squares = jnp.sum(summed * summed, axis=(1, 2))
    squares = own_squares
    for step in range(1, feat_count):
        squares = squares + swap(own_squares, "feat", feat_count, step)
    scaled = summed / jnp.sqrt(squares / FEATS + 1e-06)[:, None, None]
    placed = jnp.stack(column_places)
    ordered_columns = sum(
        jnp.where((placed[k] == lax.iota(jnp.int32, ex_count))[None, :, None], scaled[:, k : k + 1], 0.0)
        for k in range(ex_count)
    )
    return ordered_columns.reshape(scaled.shape[0], -1)


def solution(mesh):
    in_specs = (
        P(("group", "feat", "ex"), "ctx", None),
        P(("group", "feat", "ex"), "ctx", None),
        P(),
        P("ctx", "feat"),
        P(("group", "feat", "ex")),
        P("group"),
    )
    out_specs = P(("group", "ex"), "feat")
    return jax.shard_map(
        per_device, mesh=mesh, in_specs=in_specs, out_specs=out_specs, check_vma=False
    )
```

time: 77.1 us -> 44.7 us (0.58)
  blocking collectives: 58.9 us -> 0 us
  starting transfers between devices: 0 us -> 13 us
  matrix products: 15.6 us -> 2.72 us
  waiting for transfers between devices: 0 us -> 11.6 us
  Pallas kernels: 0 us -> 9.7 us
  other arithmetic: 0.26 us -> 3.68 us
  local copies, waits for them, and re-layouts: 1.22 us -> 2.74 us
    psum x3 -> x0, blocking collectives: 52.6 us -> none  [the longest x1 32 us: per_device(): summed_all = lax.psum(partial_value, 'ctx')]
    ppermute x0 -> x10, starting transfers between devices: none -> 13 us  [swap(): return lax.ppermute(value, axis, partner_pairs(count, step))]
    dot_general x3 -> x2, matrix products: 15.6 us -> 2.72 us  [the longest x1 1.93 us: per_device(): jnp.einsum('etr,etj->erj', down_rows, cotangent, preferred_element_type=j...]
    ppermute x0 -> x10, waiting for transfers between devices: none -> 11.6 us  [swap(): return lax.ppermute(value, axis, partner_pairs(count, step))]
    pallas_call x0 -> x1, Pallas kernels: none -> 9.7 us  [project(): pl.pallas_call(project_body, out_shape=jax.ShapeDtypeStruct((rows.shape[0...]
    all_gather x2 -> x0, blocking collectives: 6.26 us -> none  [the longest x1 4.41 us: per_device(): lax.all_gather(grad_rows, 'feat', axis=0, tiled=True)]
    concatenate x0 -> x2, other arithmetic: none -> 2.7 us  [the longest x1 2.66 us: per_device(): held = jnp.concatenate(ids)]
    reshape x1 -> x3, local copies, waits for them, and re-layouts: 0.08 us -> 0.92 us  [the longest x1 0.79 us: per_device(): per_ex = product.reshape(ex_count, count // ex_count, -1)]
  transfers between devices with their start and end apart: 0 -> 10, of which waited for: 0 -> 7; matrix products, arithmetic and copies ran while one was open for 0% -> 8% of each run, Pallas kernels for 0% -> 0%
where the time goes in v1:
time: 44.7 us; the launch traced here: 44.4 us
  starting transfers between devices  13 us (29%)
  waiting for transfers between devices  11.6 us (26%)
  Pallas kernels  9.7 us (22%)
  other arithmetic  3.68 us (8%)
  local copies, waits for them, and re-layouts  2.74 us (6%)
  matrix products  2.72 us (6%)
  between operations  0.97 us (2%)
    ppermute x10, starting transfers between devices, swap(): return lax.ppermute(value, axis, partner_pairs(count, step))  13 us
    ppermute x10, waiting for transfers between devices, swap(): return lax.ppermute(value, axis, partner_pairs(count, step))  11.6 us
    pallas_call x1, Pallas kernels, project(): pl.pallas_call(project_body, out_shape=jax.ShapeDtypeStruct((rows.shape[0...  9.7 us
    concatenate x1, other arithmetic, per_device(): held = jnp.concatenate(ids)  2.66 us
    dot_general x1, matrix products, per_device(): jnp.einsum('etr,etj->erj', down_rows, cotangent, preferred_element_type=j...  1.93 us
  transfers between devices with their start and end apart: 10, of which 7 were waited for; matrix products, arithmetic and copies ran while one was open for 8% of the time, Pallas kernels for 0%

profile of v1, /device:TPU:0, one launch (start us, length us, event | category | flops | bytes accessed | tf_op | source)
XLA Modules:
  0.0 44.4 jit_solution(13644861241695501876)
XLA Ops:
  0.8 0.8 %copy-done = bf16[1,128,8192]{2,1,0:T(8,128)(2,1)S(1)} copy-done((bf16[1,128,8192]{2,1,0:T(8,128)(2,1)S(1)}, bf16[1,128,8192]{2,1,0:T(8,128)(2,1)}, u32[]{:S(2)}) %copy-start) | copy-done | bytes 2097176
  1.6 1.9 %fusion.9 = f32[16,1024]{1,0:T(8,128)S(1)} fusion(bf16[8192,16]{0,1:T(8,128)(2,1)} %param.8, bf16[1,128,8192]{2,1,0:T(8,128)(2,1)S(1)} %copy-done, bf16[1,128,1024]{2,1,0:T(8,128)(2,1)} %param.7, bf16[128]{0:T(256)(128)(2,1)S(1)} %compare_convert_fusion), kind=kOutput, calls=%fused_computation.5 | convolution fusion | flops 37752832 | bytes 2687232 | tf_op jit(solution)/shard_map/etr,etj->erj/dot_general | solution.py:79
  3.7 3.1 %collective-permute-start = (f32[1,4096]{1,0:T(1,128)S(1)}, f32[1,4096]{1,0:T(1,128)S(1)}, u32[]{:S(2)}, u32[]{:S(2)}) collective-permute-start(f32[1,4096]{1,0:T(1,128)S(1)} %get-tuple-element.7), channel_id=1, source_target_pairs={{0,4},{4,0},{8,12},{12,8},{1,5},{5,1},{9,13},{13,9},{2,6},{6,2},{1... | collective-permute-start | bytes 49160 | tf_op jit(solution)/shard_map/ppermute | solution.py:30
  6.8 2.6 %collective-permute-start.1 = (f32[1,4096]{1,0:T(1,128)S(1)}, f32[1,4096]{1,0:T(1,128)S(1)}, u32[]{:S(2)}, u32[]{:S(2)}) collective-permute-start(f32[1,4096]{1,0:T(1,128)S(1)} %get-tuple-element.9), channel_id=1, source_target_pairs={{0,8},{4,12},{8,0},{12,4},{1,9},{5,13},{9,1},{13,5},{2,10},{6,14},... | collective-permute-start | bytes 49160 | tf_op jit(solution)/shard_map/ppermute | solution.py:30
  9.4 2.1 %collective-permute-done.1 = f32[1,4096]{1,0:T(1,128)S(1)} collective-permute-done((f32[1,4096]{1,0:T(1,128)S(1)}, f32[1,4096]{1,0:T(1,128)S(1)}, u32[]{:S(2)}, u32[]{:S(2)}) %collective-permute-start.1) | collective-permute-done | bytes 16416 | tf_op jit(solution)/shard_map/ppermute | solution.py:30
  11.5 3.4 %collective-permute-done.2 = f32[1,4096]{1,0:T(1,128)S(1)} collective-permute-done((f32[1,4096]{1,0:T(1,128)S(1)}, f32[1,4096]{1,0:T(1,128)S(1)}, u32[]{:S(2)}, u32[]{:S(2)}) %collective-permute-start.2) | collective-permute-done | bytes 16416 | tf_op jit(solution)/shard_map/ppermute | solution.py:30
  15.1 0.1 reshape.51
  15.1 0.7 %constant_dynamic-slice_fusion.3 = (s32[1,1,1]{1,0,2:T(1,128)}, s32[1,1,1]{1,0,2:T(1,128)}, s32[1,1,1]{1,0,2:T(1,128)}, s32[1,1,1]{1,0,2:T(1,128)}) fusion(s32[2,2,1]{1,0,2:T(2,128)S(1)} %reshape.51, s32[]{:T(128)S(6)} %select_n.41, s32[]{:T(128)S(6)} %select_n.42, s32[]{:T(128)S(6)} %select_n.44, s32[]{:T(128)S(6)} %select_n.43), kind=kLoop, calls=%fused_computation.35 | loop fusion | bytes 48 | tf_op jit(solution)/shard_map/dynamic_slice | solution.py:95
  15.8 0.4 collective-permute-done.3
  16.3 1.6 %collective-permute-start.4 = (bf16[2,4096]{1,0:T(2,128)(2,1)S(1)}, bf16[2,4096]{1,0:T(2,128)(2,1)S(1)}, u32[]{:S(2)}, u32[]{:S(2)}) collective-permute-start(bf16[2,4096]{1,0:T(2,128)(2,1)S(1)} %pad_maximum_fusion.1), channel_id=1, source_target_pairs={{0,2},{2,0},{1,3},{3,1},{4,6},{6,4},{5,7},{7,5},{8,10},{10,8},{9,1... | collective-permute-start | bytes 49160 | tf_op jit(solution)/shard_map/ppermute | solution.py:30
  17.8 2.7 %pad_add_fusion = s32[4]{0:T(128)S(1)} fusion(s32[1]{0:T(128)} %bitcast.4, s32[1]{0:T(128)} %bitcast.3, s32[1]{0:T(128)} %bitcast.2, s32[1]{0:T(128)} %bitcast.1), kind=kLoop, calls=%fused_computation.39 | loop fusion | flops 12 | bytes 32 | tf_op jit(solution)/shard_map/concatenate | solution.py:101
  20.5 0.8 %convolution_convert_fusion.rows_ref = bf16[4,4096]{1,0:T(4,128)(2,1)} fusion(bf16[2,4096]{1,0:T(2,128)(2,1)S(1)} %collective-permute-done.4, bf16[1,4096]{1,0:T(2,128)(2,1)S(1)} %collective-permute-done.3, bf16[1,4096]{1,0:T(2,128)(2,1)S(1)} %fusion.20, s32[4]{0:T(128)S(1)} %pad_add_fusion), kind=kOutput, calls=%fused_computation | convolution fusion | flops 245776 | bytes 65552 | tf_op jit(solution)/shard_map/dot_general | solution.py:104
  21.3 9.7 %shard_map.64 = f32[4,2048]{1,0:T(4,128)} custom-call(s32[1]{0:T(128)} %bitcast.half_ref, bf16[4,4096]{1,0:T(4,128)(2,1)} %convolution_convert_fusion.rows_ref, bf16[4096,4096]{1,0:T(8,128)(2,1)} %projection_ref.1), custom_call_target="tpu_custom_call" | custom-call | tf_op jit(solution)/shard_map/pallas_call | solution.py:49
  31.0 0.8 %reshape.55 = f32[2,2,2048]{2,1,0:T(2,128)S(1)} reshape(f32[4,2048]{1,0:T(4,128)} %shard_map.64) | data formatting | bytes 65536 | tf_op jit(solution)/shard_map/reshape | solution.py:107
  31.9 1.2 %collective-permute-done.5 = f32[2,2048]{1,0:T(2,128)S(1)} collective-permute-done((f32[2,2048]{1,0:T(2,128)S(1)}, f32[2,2048]{1,0:T(2,128)S(1)}, u32[]{:S(2)}, u32[]{:S(2)}) %collective-permute-start.5) | collective-permute-done | bytes 16416 | tf_op jit(solution)/shard_map/ppermute | solution.py:30
  33.1 0.8 %collective-permute-start.7 = (f32[2,2,2048]{2,0,1:T(2,128)S(1)}, f32[2,2,2048]{2,0,1:T(2,128)S(1)}, u32[]{:S(2)}, u32[]{:S(2)}) collective-permute-start(f32[2,2,2048]{2,0,1:T(2,128)S(1)} %pad_maximum_fusion), channel_id=1, source_target_pairs={{0,8},{4,12},{8,0},{12,4},{1,9},{5,13},{9,1},{13,5},{2,10},{6,14},... | collective-permute-start | bytes 98312 | tf_op jit(solution)/shard_map/ppermute | solution.py:30
  33.9 3.6 %collective-permute-start.8 = (f32[2,2,2048]{2,0,1:T(2,128)S(1)}, f32[2,2,2048]{2,0,1:T(2,128)S(1)}, u32[]{:S(2)}, u32[]{:S(2)}) collective-permute-start(f32[2,2,2048]{2,0,1:T(2,128)S(1)} %pad_maximum_fusion), channel_id=1, source_target_pairs={{0,12},{4,8},{8,4},{12,0},{1,13},{5,9},{9,5},{13,1},{2,14},{6,10},... | collective-permute-start | bytes 98312 | tf_op jit(solution)/shard_map/ppermute | solution.py:30
  37.7 0.3 collective-permute-done.7
  38.0 1.7 %collective-permute-done.8 = f32[2,2,2048]{2,0,1:T(2,128)S(1)} collective-permute-done((f32[2,2,2048]{2,0,1:T(2,128)S(1)}, f32[2,2,2048]{2,0,1:T(2,128)S(1)}, u32[]{:S(2)}, u32[]{:S(2)}) %collective-permute-start.8) | collective-permute-done | bytes 32800 | tf_op jit(solution)/shard_map/ppermute | solution.py:30
  39.7 0.2 multiply_reduce_fusion
  39.9 1.1 %collective-permute-start.9 = (f32[2]{0:T(128)S(1)}, f32[2]{0:T(128)S(1)}, u32[]{:S(2)}, u32[]{:S(2)}) collective-permute-start(f32[2]{0:T(128)S(1)} %get-tuple-element.5), channel_id=1, source_target_pairs={{0,2},{2,0},{1,3},{3,1},{4,6},{6,4},{5,7},{7,5},{8,10},{10,8},{9,1... | collective-permute-start | bytes 32 | tf_op jit(solution)/shard_map/ppermute | solution.py:30
  41.0 2.5 %collective-permute-done.9 = f32[2]{0:T(128)S(1)} collective-permute-done((f32[2]{0:T(128)S(1)}, f32[2]{0:T(128)S(1)}, u32[]{:S(2)}, u32[]{:S(2)}) %collective-permute-start.9) | collective-permute-done | bytes 40 | tf_op jit(solution)/shard_map/ppermute | solution.py:30
  43.5 0.1 broadcast_divide_fusion
  43.7 0.7 %select_add_fusion = f32[2,4096]{1,0:T(2,128)} fusion(f32[2,4096]{1,0:T(2,128)S(1)} %bitcast.50, f32[2,4096]{1,0:T(2,128)S(1)} %bitcast.49, pred[4096]{0:T(1024)(128)(4,1)S(1)} %broadcast_in_dim.67, pred[4096]{0:T(1024)(128)(4,1)S(1)} %broadcast_in_dim.59), kind=kLoop, calls=%fused_computation.13 | loop fusion | flops 24576 | bytes 106496 | tf_op jit(solution)/shard_map/add | solution.py:123
  (28 shorter events, 0.8 us)
Async XLA Ops:
  0.0 1.6 %copy-start = (bf16[1,128,8192]{2,1,0:T(8,128)(2,1)S(1)}, bf16[1,128,8192]{2,1,0:T(8,128)(2,1)}, u32[]{:S(2)}) copy-start(bf16[1,128,8192]{2,1,0:T(8,128)(2,1)} %param.6) | copy-start | bytes 6291460
  0.0 15.1 %copy-start.1 = (s32[4]{0:T(128)S(1)}, s32[4]{0:T(128)}, u32[]{:S(2)}) copy-start(s32[4]{0:T(128)} %param.11) | copy-start | bytes 52
  3.7 5.7 %collective-permute-start = (f32[1,4096]{1,0:T(1,128)S(1)}, f32[1,4096]{1,0:T(1,128)S(1)}, u32[]{:S(2)}, u32[]{:S(2)}) collective-permute-start(f32[1,4096]{1,0:T(1,128)S(1)} %get-tuple-element.7), channel_id=1, source_target_pairs={{0,4},{4,0},{8,12},{12,8},{1,5},{5,1},{9,13},{13,9},{2,6},{6,2},{1... | collective-permute-start | bytes 49160 | tf_op jit(solution)/shard_map/ppermute | solution.py:30
  6.8 4.7 %collective-permute-start.1 = (f32[1,4096]{1,0:T(1,128)S(1)}, f32[1,4096]{1,0:T(1,128)S(1)}, u32[]{:S(2)}, u32[]{:S(2)}) collective-permute-start(f32[1,4096]{1,0:T(1,128)S(1)} %get-tuple-element.9), channel_id=1, source_target_pairs={{0,8},{4,12},{8,0},{12,4},{1,9},{5,13},{9,1},{13,5},{2,10},{6,14},... | collective-permute-start | bytes 49160 | tf_op jit(solution)/shard_map/ppermute | solution.py:30
  9.4 5.5 %collective-permute-start.2 = (f32[1,4096]{1,0:T(1,128)S(1)}, f32[1,4096]{1,0:T(1,128)S(1)}, u32[]{:S(2)}, u32[]{:S(2)}) collective-permute-start(f32[1,4096]{1,0:T(1,128)S(1)} %get-tuple-element.8), channel_id=1, source_target_pairs={{0,12},{4,8},{8,4},{12,0},{1,13},{5,9},{9,5},{13,1},{2,14},{6,10},... | collective-permute-start | bytes 49160 | tf_op jit(solution)/shard_map/ppermute | solution.py:30
  15.0 1.2 %collective-permute-start.3 = (bf16[1,4096]{1,0:T(2,128)(2,1)S(1)}, bf16[1,4096]{1,0:T(2,128)(2,1)S(1)}, u32[]{:S(2)}, u32[]{:S(2)}) collective-permute-start(bf16[1,4096]{1,0:T(2,128)(2,1)S(1)} %fusion.20), channel_id=1, source_target_pairs={{0,1},{1,0},{2,3},{3,2},{4,5},{5,4},{6,7},{7,6},{8,9},{9,8},{10,11... | collective-permute-start | bytes 24584 | tf_op jit(solution)/shard_map/ppermute | solution.py:30
  16.3 4.2 %collective-permute-start.4 = (bf16[2,4096]{1,0:T(2,128)(2,1)S(1)}, bf16[2,4096]{1,0:T(2,128)(2,1)S(1)}, u32[]{:S(2)}, u32[]{:S(2)}) collective-permute-start(bf16[2,4096]{1,0:T(2,128)(2,1)S(1)} %pad_maximum_fusion.1), channel_id=1, source_target_pairs={{0,2},{2,0},{1,3},{3,1},{4,6},{6,4},{5,7},{7,5},{8,10},{10,8},{9,1... | collective-permute-start | bytes 49160 | tf_op jit(solution)/shard_map/ppermute | solution.py:30
  31.8 1.2 %collective-permute-start.5 = (f32[2,2048]{1,0:T(2,128)S(1)}, f32[2,2048]{1,0:T(2,128)S(1)}, u32[]{:S(2)}, u32[]{:S(2)}) collective-permute-start(f32[2,2048]{1,0:T(2,128)S(1)} %get-tuple-element.13), channel_id=1, source_target_pairs={{0,1},{1,0},{2,3},{3,2},{4,5},{5,4},{6,7},{7,6},{8,9},{9,8},{10,11... | collective-permute-start | bytes 49160 | tf_op jit(solution)/shard_map/ppermute | solution.py:30
  33.0 4.7 %collective-permute-start.6 = (f32[2,2,2048]{2,0,1:T(2,128)S(1)}, f32[2,2,2048]{2,0,1:T(2,128)S(1)}, u32[]{:S(2)}, u32[]{:S(2)}) collective-permute-start(f32[2,2,2048]{2,0,1:T(2,128)S(1)} %pad_maximum_fusion), channel_id=1, source_target_pairs={{0,4},{4,0},{8,12},{12,8},{1,5},{5,1},{9,13},{13,9},{2,6},{6,2},{1... | collective-permute-start | bytes 98312 | tf_op jit(solution)/shard_map/ppermute | solution.py:30
  33.1 4.9 %collective-permute-start.7 = (f32[2,2,2048]{2,0,1:T(2,128)S(1)}, f32[2,2,2048]{2,0,1:T(2,128)S(1)}, u32[]{:S(2)}, u32[]{:S(2)}) collective-permute-start(f32[2,2,2048]{2,0,1:T(2,128)S(1)} %pad_maximum_fusion), channel_id=1, source_target_pairs={{0,8},{4,12},{8,0},{12,4},{1,9},{5,13},{9,1},{13,5},{2,10},{6,14},... | collective-permute-start | bytes 98312 | tf_op jit(solution)/shard_map/ppermute | solution.py:30
  33.9 5.8 %collective-permute-start.8 = (f32[2,2,2048]{2,0,1:T(2,128)S(1)}, f32[2,2,2048]{2,0,1:T(2,128)S(1)}, u32[]{:S(2)}, u32[]{:S(2)}) collective-permute-start(f32[2,2,2048]{2,0,1:T(2,128)S(1)} %pad_maximum_fusion), channel_id=1, source_target_pairs={{0,12},{4,8},{8,4},{12,0},{1,13},{5,9},{9,5},{13,1},{2,14},{6,10},... | collective-permute-start | bytes 98312 | tf_op jit(solution)/shard_map/ppermute | solution.py:30
  39.9 3.6 %collective-permute-start.9 = (f32[2]{0:T(128)S(1)}, f32[2]{0:T(128)S(1)}, u32[]{:S(2)}, u32[]{:S(2)}) collective-permute-start(f32[2]{0:T(128)S(1)} %get-tuple-element.5), channel_id=1, source_target_pairs={{0,2},{2,0},{1,3},{3,1},{4,6},{6,4},{5,7},{7,5},{8,10},{10,8},{9,1... | collective-permute-start | bytes 32 | tf_op jit(solution)/shard_map/ppermute | solution.py:30

commit v2 on v0

v2 whole, which is shorter than its diff:
```python
import functools
import itertools

import jax
import jax.numpy as jnp
from jax import lax
from jax.experimental import pallas as pl
from jax.experimental.pallas import tpu as pltpu
from jax.sharding import PartitionSpec as P

MIB = 1 << 20
SHARES = (1, 3, 2, 2)
VMEM = pl.BlockSpec(memory_space=pltpu.VMEM)
HBM = pl.BlockSpec(memory_space=pltpu.HBM)


def is_power(count):
    return count & (count - 1) == 0


def place_at(index, count, step, sign=1):
    if is_power(count):
        return index ^ step
    return (index + sign * step + count) % count


def step_to(index, target, count):
    if is_power(count):
        return index ^ target
    return lax.rem(target - index + count, count)


def swap(value, axes, steps):
    sizes = [lax.axis_size(a) for a in axes]
    flat = lambda place: functools.reduce(lambda total, p: total * p[1] + p[0], zip(place, sizes), 0)
    pairs = [
        (flat(place), flat([place_at(i, n, s) for i, n, s in zip(place, sizes, steps)]))
        for place in itertools.product(*map(range, sizes))
    ]
    return lax.ppermute(value, tuple(axes) if len(axes) > 1 else axes[0], pairs)


def params(mib, **more):
    return pltpu.CompilerParams(vmem_limit_bytes=mib * MIB, **more)


def lane_dot(a, b):
    return lax.dot_general(a, b, (((1,), (1,)), ((), ())), preferred_element_type=jnp.float32)


def hbm(value):
    return pltpu.with_memory_space_constraint(value, pltpu.HBM)


def share_rows(depth, number):
    eighth = depth // sum(SHARES)
    return sum(SHARES[:number]) * eighth, SHARES[number] * eighth


def share_copy(projection_hbm, buffer, sem, number):
    first, rows = share_rows(projection_hbm.shape[0], number)
    width = buffer.shape[1]
    columns = pl.ds(pl.multiple_of(lax.axis_index("ex") * width, 128), width)
    return pltpu.make_async_copy(projection_hbm.at[pl.ds(first, rows), columns], buffer, sem)


def share_shape(projection, number, ex_count):
    depth, width = projection.shape
    return share_rows(depth, number)[1], width // ex_count


def load_body(number, after_ref, projection_hbm, buffer, sem):
    copy = share_copy(projection_hbm, buffer, sem, number)
    copy.start()
    copy.wait()


def load(projection, number, ex_count, after):
    return pl.pallas_call(
        functools.partial(load_body, number),
        out_shape=pltpu.VMEM(share_shape(projection, number, ex_count), projection.dtype),
        in_specs=[VMEM, HBM],
        out_specs=VMEM,
        scratch_shapes=[pltpu.SemaphoreType.DMA],
        compiler_params=params(2),
    )(after, hbm(projection))


def gradient_body(chunks, counts, hidden_hbm, factor_hbm, cotangent_hbm, projection_hbm, lengths, order_hbm, *refs):
    ctx_count, feat_count, ex_count = counts
    outs, ranks_ref, share_ref = refs[:ctx_count], refs[ctx_count], refs[ctx_count + 1]
    hidden, factor, cotangent, blocks, order, sems, order_sem = refs[ctx_count + 2 :]
    own, tokens, width = hidden.shape
    part = width // chunks
    order_copy = pltpu.make_async_copy(order_hbm, order, order_sem)
    order_copy.start()
    copies = [pltpu.make_async_copy(factor_hbm, factor, sems.at[0])]
    for k in range(chunks):
        columns = pl.ds(k * part, part)
        copies.append(
            pltpu.make_async_copy(hidden_hbm.at[:, :, columns], hidden.at[:, :, columns], sems.at[1 + k])
        )
    copies.append(pltpu.make_async_copy(cotangent_hbm, cotangent, sems.at[1 + chunks]))
    copies.append(share_copy(projection_hbm, share_ref, sems.at[2 + chunks], 0))
    for copy in copies:
        copy.start()
    copies[0].wait()
    down = [None] * own
    for k in range(chunks):
        copies[1 + k].wait()
        for e in range(own):
            product = lane_dot(factor[:, k * part : (k + 1) * part], hidden[e, :, k * part : (k + 1) * part])
            down[e] = product if k == 0 else down[e] + product
    copies[-2].wait()
    order_copy.wait()
    place = lax.axis_index("ctx")
    for e in range(own):
        rows = down[e].astype(jnp.bfloat16)
        position = place * tokens + lax.broadcasted_iota(jnp.int32, rows.shape, 1)
        rows = jnp.where(position < lengths[e], rows.astype(jnp.float32), 0.0).astype(jnp.bfloat16)
        grad = jnp.dot(rows, cotangent[e], preferred_element_type=jnp.float32)
        share = grad.shape[0] // ctx_count
        for c in range(ctx_count):
            blocks[c, e] = grad[c * share : (c + 1) * share]
    for step in range(ctx_count):
        outs[step][...] = blocks[place_at(place, ctx_count, step)]
    feat, ex = lax.axis_index("feat"), lax.axis_index("ex")
    per_ex = own * feat_count
    for k, steps in enumerate(itertools.product(range(feat_count), range(ex_count))):
        from_feat, from_ex = place_at(feat, feat_count, steps[0], -1), place_at(ex, ex_count, steps[1], -1)
        for e in range(own):
            wanted = order[(from_feat * ex_count + from_ex) * own + e]
            rank = step_to(ex, lax.div(wanted, per_ex), ex_count) * per_ex + lax.rem(wanted, per_ex)
            ranks_ref[pl.ds(k * own + e, 1), :] = jnp.full((1, 128), rank, jnp.int32)
    copies[-1].wait()


def gradient(hidden, factor, cotangent, projection, lengths, order, counts):
    ctx_count, feat_count, ex_count = counts
    own, tokens, width = hidden.shape
    rank, model = factor.shape[0], cotangent.shape[2]
    shape = (own, rank // ctx_count, model)
    chunks = 4
    return pl.pallas_call(
        functools.partial(gradient_body, chunks, counts),
        out_shape=[jax.ShapeDtypeStruct(shape, jnp.float32)] * ctx_count
        + [
            jax.ShapeDtypeStruct((own * feat_count * ex_count, 128), jnp.int32),
            pltpu.VMEM(share_shape(projection, 0, ex_count), projection.dtype),
        ],
        in_specs=[HBM] * 4 + [pl.BlockSpec(memory_space=pltpu.SMEM), HBM],
        out_specs=[VMEM] * (ctx_count + 2),
        scratch_shapes=[
            pltpu.VMEM(hidden.shape, hidden.dtype),
            pltpu.VMEM(factor.shape, factor.dtype),
            pltpu.VMEM(cotangent.shape, cotangent.dtype),
            pltpu.VMEM((ctx_count,) + shape, jnp.float32),
            pltpu.SMEM(order.shape, order.dtype),
            pltpu.SemaphoreType.DMA((chunks + 3,)),
            pltpu.SemaphoreType.DMA,
        ],
        compiler_params=params(8),
    )(*map(hbm, (hidden, factor, cotangent, projection)), lengths, hbm(order))


def sum_body(*refs):
    total = refs[0][...]
    for ref in refs[1:-2]:
        total = total + ref[...]
    refs[-1][...] = total.astype(refs[-1].dtype)


def sum_rows(parts, dtype, after):
    return pl.pallas_call(
        sum_body,
        out_shape=jax.ShapeDtypeStruct(parts[0].shape, dtype),
        in_specs=[VMEM] * (len(parts) + 1),
        out_specs=VMEM,
        compiler_params=params(2),
    )(*parts, pltpu.with_memory_space_constraint(after, pltpu.VMEM))


def project_body(source_count, ranks_ref, projection_hbm, *refs):
    sources, shares, (out, last_share, rows_ref, sem) = refs[:source_count], refs[source_count:-4], refs[-4:]
    copy = share_copy(projection_hbm, last_share, sem, len(shares))
    copy.start()
    padded, width = out.shape
    own, share, model = sources[0].shape
    row = lax.broadcasted_iota(jnp.int32, (padded, model), 0)
    ranks = ranks_ref[...][:, :1]
    for r in range(share):
        rows = jnp.zeros((padded, model), jnp.float32)
        for k, source in enumerate(sources):
            for e in range(own):
                values = source[e, r : r + 1].astype(jnp.float32)
                rows = rows + jnp.where(row == ranks[k * own + e : k * own + e + 1], values, 0.0)
        rows_ref[:, r * model : (r + 1) * model] = rows.astype(jnp.bfloat16)
    for number, weights in enumerate((*shares, last_share)):
        first, depth = share_rows(projection_hbm.shape[0], number)
        if number == len(shares):
            copy.wait()
        part = jnp.dot(rows_ref[:, first : first + depth], weights[...], preferred_element_type=jnp.float32)
        if number == 0:
            out[...] = part
        else:
            out[...] += part


def project(sources, ranks, projection, shares, ex_count):
    depth, width = projection.shape
    padded = max(8, ranks.shape[0])
    return pl.pallas_call(
        functools.partial(project_body, len(sources)),
        out_shape=jax.ShapeDtypeStruct((padded, width // ex_count), jnp.float32),
        in_specs=[VMEM, HBM] + [VMEM] * (len(sources) + len(shares)),
        out_specs=VMEM,
        scratch_shapes=[
            pltpu.VMEM(share_shape(projection, len(shares), ex_count), projection.dtype),
            pltpu.VMEM((padded, depth), jnp.bfloat16),
            pltpu.SemaphoreType.DMA,
        ],
        compiler_params=params(8),
    )(ranks, hbm(projection), *sources, *[pltpu.with_memory_space_constraint(v, pltpu.VMEM) for v in shares])


def total_body(per_ex, ex_count, *refs):
    parts, outs = refs[: -2 * ex_count], refs[-2 * ex_count :]
    total = parts[0][...]
    for part in parts[1:]:
        total = total + part[...]
    squares = jnp.sum(total * total, axis=1, keepdims=True)
    for step in range(ex_count):
        rows = slice(step * per_ex, (step + 1) * per_ex)
        outs[2 * step][...] = total[rows]
        outs[2 * step + 1][...] = jnp.broadcast_to(squares[rows], (per_ex, 128))


def totals(parts, count, ex_count):
    per_ex, width = count // ex_count, parts[0].shape[1]
    shapes = [jax.ShapeDtypeStruct((per_ex, width), jnp.float32), jax.ShapeDtypeStruct((per_ex, 128), jnp.float32)]
    return pl.pallas_call(
        functools.partial(total_body, per_ex, ex_count),
        out_shape=shapes * ex_count,
        in_specs=[VMEM] * len(parts),
        out_specs=[VMEM] * (2 * ex_count),
        compiler_params=params(8),
    )(*parts)


def scale_body(ex_count, columns, *refs):
    rows, squares, out = refs[:ex_count], refs[ex_count:-1], refs[-1]
    width = rows[0].shape[1]
    total = squares[0][...]
    for square in squares[1:]:
        total = total + square[...]
    norm = jnp.sqrt(total[:, :1] / columns + 1e-06)
    for step in range(ex_count):
        place = place_at(lax.axis_index("ex"), ex_count, step, -1)
        out[:, pl.ds(pl.multiple_of(place * width, 128), width)] = rows[step][...] / norm


def scale(rows, squares, columns):
    per_ex, width = rows[0].shape
    return pl.pallas_call(
        functools.partial(scale_body, len(rows), columns),
        out_shape=jax.ShapeDtypeStruct((per_ex, width * len(rows)), jnp.float32),
        in_specs=[VMEM] * (len(rows) + len(squares)),
        out_specs=VMEM,
        compiler_params=params(8),
    )(*rows, *squares)


def per_device(hidden, cotangent, adapter_down_factor, projection, lengths, slot_example_order):
    counts = ctx_count, feat_count, ex_count = tuple(map(lax.axis_size, ("ctx", "feat", "ex")))
    count = hidden.shape[0] * feat_count * ex_count
    ctx_steps = range(1, ctx_count)
    chip_steps = list(itertools.product(range(feat_count), range(ex_count)))[1:]

    *blocks, ranks, share = gradient(
        hidden, adapter_down_factor.T, cotangent, projection, lengths, slot_example_order, counts
    )
    shares = [share, load(projection, 1, ex_count, ranks)]
    grad_rows = sum_rows(
        [blocks[0]] + [swap(blocks[s], ("ctx",), (s,)) for s in ctx_steps], jnp.bfloat16, shares[1]
    )
    shares.append(load(projection, 2, ex_count, grad_rows))
    sources = [grad_rows] + [swap(grad_rows, ("feat", "ex"), steps) for steps in chip_steps]
    product = project(sources, ranks, projection, shares, ex_count)
    outs = totals([product] + [swap(product, ("ctx",), (s,)) for s in ctx_steps], count, ex_count)
    rows = [outs[0]] + [swap(outs[2 * s], ("ex",), (s,)) for s in range(1, ex_count)]
    squares = [outs[1]] + [swap(outs[2 * s[1] + 1], ("feat", "ex"), s) for s in chip_steps]
    return scale(rows, squares, projection.shape[1] * feat_count)


def solution(mesh):
    in_specs = (
        P(("group", "feat", "ex"), "ctx", None),
        P(("group", "feat", "ex"), "ctx", None),
        P(),
        P("ctx", "feat"),
        P(("group", "feat", "ex")),
        P("group"),
    )
    out_specs = P(("group", "ex"), "feat")
    return jax.shard_map(
        per_device, mesh=mesh, in_specs=in_specs, out_specs=out_specs, check_vma=False
    )
```

time: 77.1 us -> 37.2 us (0.48)
  blocking collectives: 58.9 us -> 0 us
  matrix products: 15.6 us -> 0 us
  starting transfers between devices: 0 us -> 14.3 us
  Pallas kernels: 0 us -> 12.7 us
  waiting for transfers between devices: 0 us -> 9.25 us
  local copies, waits for them, and re-layouts: 1.22 us -> 0 us
    psum x3 -> x0, blocking collectives: 52.6 us -> none  [the longest x1 32 us: per_device(): summed_all = lax.psum(partial_value, 'ctx')]
    dot_general x3 -> x0, matrix products: 15.6 us -> none  [the longest x1 12.8 us: per_device(): jnp.dot(lax.all_gather(grad_rows, 'feat', axis=0, tiled=True), projection...]
    ppermute x0 -> x13, starting transfers between devices: none -> 14.3 us  [swap(): return lax.ppermute(value, tuple(axes) if len(axes) > 1 else axes[0], pairs)]
    pallas_call x0 -> x7, Pallas kernels: none -> 12.7 us  [the longest x2 4.99 us: load(): pl.pallas_call(functools.partial(load_body, number), out_shape=pltpu.VMEM...]
    ppermute x0 -> x13, waiting for transfers between devices: none -> 9.25 us  [swap(): return lax.ppermute(value, tuple(axes) if len(axes) > 1 else axes[0], pairs)]
    all_gather x2 -> x0, blocking collectives: 6.26 us -> none  [the longest x1 4.41 us: per_device(): lax.all_gather(grad_rows, 'feat', axis=0, tiled=True)]
    unnamed x7 -> x0, local copies, waits for them, and re-layouts: 0.96 us -> none
  transfers between devices with their start and end apart: 0 -> 13, of which waited for: 0 -> 5; matrix products, arithmetic and copies ran while one was open for 0% -> 0% of each run, Pallas kernels for 0% -> 13%
where the time goes in v2:
time: 37.2 us; the launch traced here: 37 us
  starting transfers between devices  14.3 us (38%)
  Pallas kernels  12.7 us (34%)
  waiting for transfers between devices  9.25 us (25%)
  between operations  0.75 us (2%)
    ppermute x13, starting transfers between devices, swap(): return lax.ppermute(value, tuple(axes) if len(axes) > 1 else axes[0], pairs)  14.3 us
    ppermute x13, waiting for transfers between devices, swap(): return lax.ppermute(value, tuple(axes) if len(axes) > 1 else axes[0], pairs)  9.25 us
    pallas_call x2, Pallas kernels, load(): pl.pallas_call(functools.partial(load_body, number), out_shape=pltpu.VMEM...  4.99 us
    pallas_call x1, Pallas kernels, project(): pl.pallas_call(functools.partial(project_body, len(sources)), out_shape=j...  4.02 us
    pallas_call x1, Pallas kernels, gradient(): pl.pallas_call(functools.partial(gradient_body, chunks, counts), out_shap...  2.84 us
  transfers between devices with their start and end apart: 13, of which 5 were waited for; matrix products, arithmetic and copies ran while one was open for 0% of the time, Pallas kernels for 13%

profile of v2, /device:TPU:0, one launch (start us, length us, event | category | flops | bytes accessed | tf_op | source)
XLA Modules:
  0.0 37.0 jit_solution(10506339240232779146)
XLA Ops:
  0.7 2.8 %shard_map.64 = (f32[1,4,1024]{2,1,0:T(4,128)S(1)}, f32[1,4,1024]{2,1,0:T(4,128)S(1)}, f32[1,4,1024]{2,1,0:T(4,128)S(1)}, f32[1,4,1024]{2,1,0:T(4,128)S(1)}, s32...) custom-call(bf16[1,128,8192]{2,1,0:T(8,128)(2,1)} %hidden_hbm.1, bf16[16,8192]{1,0:T(8,128)(2,1)} %bitcast.1, ...), custom_call_target="tpu_custom_call" | custom-call | tf_op jit(solution)/shard_map/pallas_call | solution.py:144
  3.5 3.1 %collective-permute-start = (f32[1,4,1024]{2,1,0:T(4,128)S(1)}, f32[1,4,1024]{2,1,0:T(4,128)S(1)}, u32[]{:S(2)}, u32[]{:S(2)}) collective-permute-start(f32[1,4,1024]{2,1,0:T(4,128)S(1)} %get-tuple-element.17), channel_id=1, source_target_pairs={{0,4},{4,0},{8,12},{12,8},{1,5},{5,1},{9,13},{13,9},{2,6},{6,2},{1... | collective-permute-start | bytes 49160 | tf_op jit(solution)/shard_map/ppermute | solution.py:40
  6.6 2.6 %collective-permute-start.1 = (f32[1,4,1024]{2,1,0:T(4,128)S(1)}, f32[1,4,1024]{2,1,0:T(4,128)S(1)}, u32[]{:S(2)}, u32[]{:S(2)}) collective-permute-start(f32[1,4,1024]{2,1,0:T(4,128)S(1)} %get-tuple-element.18), channel_id=1, source_target_pairs={{0,8},{4,12},{8,0},{12,4},{1,9},{5,13},{9,1},{13,5},{2,10},{6,14},... | collective-permute-start | bytes 49160 | tf_op jit(solution)/shard_map/ppermute | solution.py:40
  9.2 2.8 %shard_map.65.refs_4_.refs_5_ = bf16[1536,2048]{1,0:T(8,128)(2,1)S(1)} custom-call(s32[4,128]{1,0:T(4,128)S(1)} %get-tuple-element.15.after_ref.ranks_ref, bf16[4096,4096]{1,0:T(8,128)(2,1)} %projection_hbm.7), custom_call_target="tpu_custom_call" | custom-call | tf_op jit(solution)/shard_map/pallas_call | solution.py:79
  12.0 0.0 collective-permute-done.1.refs_2_
  12.0 2.7 %collective-permute-done.2.refs_3_ = f32[1,4,1024]{2,1,0:T(4,128)S(1)} collective-permute-done((f32[1,4,1024]{2,1,0:T(4,128)S(1)}, f32[1,4,1024]{2,1,0:T(4,128)S(1)}, u32[]{:S(2)}, u32[]{:S(2)}) %collective-permute-start.2) | collective-permute-done | bytes 16416 | tf_op jit(solution)/shard_map/ppermute | solution.py:40
  14.8 0.1 collective-permute-start.5
  14.8 1.6 %collective-permute-start.4 = (bf16[1,4,1024]{2,1,0:T(4,128)(2,1)S(1)}, bf16[1,4,1024]{2,1,0:T(4,128)(2,1)S(1)}, u32[]{:S(2)}, u32[]{:S(2)}) collective-permute-start(bf16[1,4,1024]{2,1,0:T(4,128)(2,1)S(1)} %shard_map.66.after_ref.refs_0_), channel_id=1, source_target_pairs={{0,2},{1,3},{2,0},{3,1},{4,6},{5,7},{6,4},{7,5},{8,10},{9,11},{10,... | collective-permute-start | bytes 24584 | tf_op jit(solution)/shard_map/ppermute | solution.py:40
  16.4 0.3 collective-permute-start.3
  16.7 2.2 %shard_map.67.refs_6_ = bf16[1024,2048]{1,0:T(8,128)(2,1)S(1)} custom-call(bf16[1,4,1024]{2,1,0:T(4,128)(2,1)S(1)} %shard_map.66.after_ref.refs_0_, bf16[4096,4096]{1,0:T(8,128)(2,1)} %projection_hbm.7), custom_call_target="tpu_custom_call" | custom-call | tf_op jit(solution)/shard_map/pallas_call | solution.py:79
  18.9 0.0 collective-permute-done.5.refs_3_
  18.9 0.0 collective-permute-done.4.refs_2_
  18.9 4.0 %shard_map.68.refs_0_ = f32[8,2048]{1,0:T(8,128)S(1)} custom-call(s32[4,128]{1,0:T(4,128)S(1)} %get-tuple-element.15.after_ref.ranks_ref, bf16[4096,4096]{1,0:T(8,128)(2,1)} %projection_hbm.7, bf16[1,4,1024]{2,1,0:T(4,128)(2,1)S(1)} %shard_map.66.after_ref.refs_0_, bf16[1,4,1024]{2,1,0:T(4,128)(2,1)S(1)} %collective-permute-done.3.refs_1_, ...), custom_call_target="tpu_custom_call" | custom-call | tf_op jit(solution)/shard_map/pallas_call | solution.py:212
  23.0 1.2 %collective-permute-start.8 = (f32[8,2048]{1,0:T(8,128)S(1)}, f32[8,2048]{1,0:T(8,128)S(1)}, u32[]{:S(2)}, u32[]{:S(2)}) collective-permute-start(f32[8,2048]{1,0:T(8,128)S(1)} %shard_map.68.refs_0_), channel_id=1, source_target_pairs={{0,12},{4,8},{8,4},{12,0},{1,13},{5,9},{9,5},{13,1},{2,14},{6,10},... | collective-permute-start | bytes 196616 | tf_op jit(solution)/shard_map/ppermute | solution.py:40
  24.1 3.3 %collective-permute-start.6 = (f32[8,2048]{1,0:T(8,128)S(1)}, f32[8,2048]{1,0:T(8,128)S(1)}, u32[]{:S(2)}, u32[]{:S(2)}) collective-permute-start(f32[8,2048]{1,0:T(8,128)S(1)} %shard_map.68.refs_0_), channel_id=1, source_target_pairs={{0,4},{4,0},{8,12},{12,8},{1,5},{5,1},{9,13},{13,9},{2,6},{6,2},{1... | collective-permute-start | bytes 196616 | tf_op jit(solution)/shard_map/ppermute | solution.py:40
  27.4 2.4 %collective-permute-done.8.refs_3_ = f32[8,2048]{1,0:T(8,128)S(1)} collective-permute-done((f32[8,2048]{1,0:T(8,128)S(1)}, f32[8,2048]{1,0:T(8,128)S(1)}, u32[]{:S(2)}, u32[]{:S(2)}) %collective-permute-start.8) | collective-permute-done | bytes 65568 | tf_op jit(solution)/shard_map/ppermute | solution.py:40
  29.8 2.0 %collective-permute-done.7.refs_2_ = f32[8,2048]{1,0:T(8,128)S(1)} collective-permute-done((f32[8,2048]{1,0:T(8,128)S(1)}, f32[8,2048]{1,0:T(8,128)S(1)}, u32[]{:S(2)}, u32[]{:S(2)}) %collective-permute-start.7) | collective-permute-done | bytes 65568 | tf_op jit(solution)/shard_map/ppermute | solution.py:40
  31.8 0.1 shard_map.69
  31.9 1.3 %collective-permute-start.11 = (f32[2,128]{1,0:T(2,128)S(1)}, f32[2,128]{1,0:T(2,128)S(1)}, u32[]{:S(2)}, u32[]{:S(2)}) collective-permute-start(f32[2,128]{1,0:T(2,128)S(1)} %get-tuple-element.23.refs_2_), channel_id=1, source_target_pairs={{0,2},{1,3},{2,0},{3,1},{4,6},{5,7},{6,4},{7,5},{8,10},{9,11},{10,... | collective-permute-start | bytes 3080 | tf_op jit(solution)/shard_map/ppermute | solution.py:40
  33.2 0.5 %collective-permute-start.12 = (f32[2,128]{1,0:T(2,128)S(1)}, f32[2,128]{1,0:T(2,128)S(1)}, u32[]{:S(2)}, u32[]{:S(2)}) collective-permute-start(f32[2,128]{1,0:T(2,128)S(1)} %get-tuple-element.24), channel_id=1, source_target_pairs={{0,3},{1,2},{2,1},{3,0},{4,7},{5,6},{6,5},{7,4},{8,11},{9,10},{10,... | collective-permute-start | bytes 3080 | tf_op jit(solution)/shard_map/ppermute | solution.py:40
  33.8 0.4 collective-permute-start.10
  34.1 1.4 %collective-permute-done.11.refs_4_ = f32[2,128]{1,0:T(2,128)S(1)} collective-permute-done((f32[2,128]{1,0:T(2,128)S(1)}, f32[2,128]{1,0:T(2,128)S(1)}, u32[]{:S(2)}, u32[]{:S(2)}) %collective-permute-start.11) | collective-permute-done | bytes 1056 | tf_op jit(solution)/shard_map/ppermute | solution.py:40
  35.5 0.7 %collective-permute-done.12.refs_5_ = f32[2,128]{1,0:T(2,128)S(1)} collective-permute-done((f32[2,128]{1,0:T(2,128)S(1)}, f32[2,128]{1,0:T(2,128)S(1)}, u32[]{:S(2)}, u32[]{:S(2)}) %collective-permute-start.12) | collective-permute-done | bytes 1056 | tf_op jit(solution)/shard_map/ppermute | solution.py:40
  36.2 0.7 %shard_map.70 = f32[2,4096]{1,0:T(2,128)} custom-call(f32[2,2048]{1,0:T(2,128)S(1)} %get-tuple-element.21.refs_0_, f32[2,2048]{1,0:T(2,128)S(1)} %collective-permute-done.9.refs_1_, f32[2,128]{1,0:T(2,128)S(1)} %get-tuple-element.23.refs_2_, f32[2,128]{1,0:T(2,128)S(1)} %collective-permute-done.10.refs_3_, f32[2,128]{1,0:T(2,128)S(1)} %collective-permute-done.11.refs_4_, ...), custom_call_target="tpu_custom_call" | custom-call | tf_op jit(solution)/shard_map/pallas_call | solution.py:264
  (9 shorter events, 0.0 us)
Async XLA Ops:
  3.5 8.5 %collective-permute-start = (f32[1,4,1024]{2,1,0:T(4,128)S(1)}, f32[1,4,1024]{2,1,0:T(4,128)S(1)}, u32[]{:S(2)}, u32[]{:S(2)}) collective-permute-start(f32[1,4,1024]{2,1,0:T(4,128)S(1)} %get-tuple-element.17), channel_id=1, source_target_pairs={{0,4},{4,0},{8,12},{12,8},{1,5},{5,1},{9,13},{13,9},{2,6},{6,2},{1... | collective-permute-start | bytes 49160 | tf_op jit(solution)/shard_map/ppermute | solution.py:40
  6.6 5.4 %collective-permute-start.1 = (f32[1,4,1024]{2,1,0:T(4,128)S(1)}, f32[1,4,1024]{2,1,0:T(4,128)S(1)}, u32[]{:S(2)}, u32[]{:S(2)}) collective-permute-start(f32[1,4,1024]{2,1,0:T(4,128)S(1)} %get-tuple-element.18), channel_id=1, source_target_pairs={{0,8},{4,12},{8,0},{12,4},{1,9},{5,13},{9,1},{13,5},{2,10},{6,14},... | collective-permute-start | bytes 49160 | tf_op jit(solution)/shard_map/ppermute | solution.py:40
  9.2 5.5 %collective-permute-start.2 = (f32[1,4,1024]{2,1,0:T(4,128)S(1)}, f32[1,4,1024]{2,1,0:T(4,128)S(1)}, u32[]{:S(2)}, u32[]{:S(2)}) collective-permute-start(f32[1,4,1024]{2,1,0:T(4,128)S(1)} %get-tuple-element.19), channel_id=1, source_target_pairs={{0,12},{4,8},{8,4},{12,0},{1,13},{5,9},{9,5},{13,1},{2,14},{6,10},... | collective-permute-start | bytes 49160 | tf_op jit(solution)/shard_map/ppermute | solution.py:40
  14.8 4.1 %collective-permute-start.5 = (bf16[1,4,1024]{2,1,0:T(4,128)(2,1)S(1)}, bf16[1,4,1024]{2,1,0:T(4,128)(2,1)S(1)}, u32[]{:S(2)}, u32[]{:S(2)}) collective-permute-start(bf16[1,4,1024]{2,1,0:T(4,128)(2,1)S(1)} %shard_map.66.after_ref.refs_0_), channel_id=1, source_target_pairs={{0,3},{1,2},{2,1},{3,0},{4,7},{5,6},{6,5},{7,4},{8,11},{9,10},{10,... | collective-permute-start | bytes 24584 | tf_op jit(solution)/shard_map/ppermute | solution.py:40
  14.8 4.1 %collective-permute-start.4 = (bf16[1,4,1024]{2,1,0:T(4,128)(2,1)S(1)}, bf16[1,4,1024]{2,1,0:T(4,128)(2,1)S(1)}, u32[]{:S(2)}, u32[]{:S(2)}) collective-permute-start(bf16[1,4,1024]{2,1,0:T(4,128)(2,1)S(1)} %shard_map.66.after_ref.refs_0_), channel_id=1, source_target_pairs={{0,2},{1,3},{2,0},{3,1},{4,6},{5,7},{6,4},{7,5},{8,10},{9,11},{10,... | collective-permute-start | bytes 24584 | tf_op jit(solution)/shard_map/ppermute | solution.py:40
  16.4 2.5 %collective-permute-start.3 = (bf16[1,4,1024]{2,1,0:T(4,128)(2,1)S(1)}, bf16[1,4,1024]{2,1,0:T(4,128)(2,1)S(1)}, u32[]{:S(2)}, u32[]{:S(2)}) collective-permute-start(bf16[1,4,1024]{2,1,0:T(4,128)(2,1)S(1)} %shard_map.66.after_ref.refs_0_), channel_id=1, source_target_pairs={{0,1},{1,0},{2,3},{3,2},{4,5},{5,4},{6,7},{7,6},{8,9},{9,8},{10,11... | collective-permute-start | bytes 24584 | tf_op jit(solution)/shard_map/ppermute | solution.py:40
  23.0 6.9 %collective-permute-start.8 = (f32[8,2048]{1,0:T(8,128)S(1)}, f32[8,2048]{1,0:T(8,128)S(1)}, u32[]{:S(2)}, u32[]{:S(2)}) collective-permute-start(f32[8,2048]{1,0:T(8,128)S(1)} %shard_map.68.refs_0_), channel_id=1, source_target_pairs={{0,12},{4,8},{8,4},{12,0},{1,13},{5,9},{9,5},{13,1},{2,14},{6,10},... | collective-permute-start | bytes 196616 | tf_op jit(solution)/shard_map/ppermute | solution.py:40
  24.1 7.6 %collective-permute-start.7 = (f32[8,2048]{1,0:T(8,128)S(1)}, f32[8,2048]{1,0:T(8,128)S(1)}, u32[]{:S(2)}, u32[]{:S(2)}) collective-permute-start(f32[8,2048]{1,0:T(8,128)S(1)} %shard_map.68.refs_0_), channel_id=1, source_target_pairs={{0,8},{4,12},{8,0},{12,4},{1,9},{5,13},{9,1},{13,5},{2,10},{6,14},... | collective-permute-start | bytes 196616 | tf_op jit(solution)/shard_map/ppermute | solution.py:40
  24.1 7.6 %collective-permute-start.6 = (f32[8,2048]{1,0:T(8,128)S(1)}, f32[8,2048]{1,0:T(8,128)S(1)}, u32[]{:S(2)}, u32[]{:S(2)}) collective-permute-start(f32[8,2048]{1,0:T(8,128)S(1)} %shard_map.68.refs_0_), channel_id=1, source_target_pairs={{0,4},{4,0},{8,12},{12,8},{1,5},{5,1},{9,13},{13,9},{2,6},{6,2},{1... | collective-permute-start | bytes 196616 | tf_op jit(solution)/shard_map/ppermute | solution.py:40
  31.9 4.4 %collective-permute-start.9 = (f32[2,2048]{1,0:T(2,128)S(1)}, f32[2,2048]{1,0:T(2,128)S(1)}, u32[]{:S(2)}, u32[]{:S(2)}) collective-permute-start(f32[2,2048]{1,0:T(2,128)S(1)} %get-tuple-element.22), channel_id=1, source_target_pairs={{0,1},{1,0},{2,3},{3,2},{4,5},{5,4},{6,7},{7,6},{8,9},{9,8},{10,11... | collective-permute-start | bytes 49160 | tf_op jit(solution)/shard_map/ppermute | solution.py:40
  31.9 3.6 %collective-permute-start.11 = (f32[2,128]{1,0:T(2,128)S(1)}, f32[2,128]{1,0:T(2,128)S(1)}, u32[]{:S(2)}, u32[]{:S(2)}) collective-permute-start(f32[2,128]{1,0:T(2,128)S(1)} %get-tuple-element.23.refs_2_), channel_id=1, source_target_pairs={{0,2},{1,3},{2,0},{3,1},{4,6},{5,7},{6,4},{7,5},{8,10},{9,11},{10,... | collective-permute-start | bytes 3080 | tf_op jit(solution)/shard_map/ppermute | solution.py:40
  33.2 3.0 %collective-permute-start.12 = (f32[2,128]{1,0:T(2,128)S(1)}, f32[2,128]{1,0:T(2,128)S(1)}, u32[]{:S(2)}, u32[]{:S(2)}) collective-permute-start(f32[2,128]{1,0:T(2,128)S(1)} %get-tuple-element.24), channel_id=1, source_target_pairs={{0,3},{1,2},{2,1},{3,0},{4,7},{5,6},{6,5},{7,4},{8,11},{9,10},{10,... | collective-permute-start | bytes 3080 | tf_op jit(solution)/shard_map/ppermute | solution.py:40
  33.8 2.5 %collective-permute-start.10 = (f32[2,128]{1,0:T(2,128)S(1)}, f32[2,128]{1,0:T(2,128)S(1)}, u32[]{:S(2)}, u32[]{:S(2)}) collective-permute-start(f32[2,128]{1,0:T(2,128)S(1)} %get-tuple-element.24), channel_id=1, source_target_pairs={{0,1},{1,0},{2,3},{3,2},{4,5},{5,4},{6,7},{7,6},{8,9},{9,8},{10,11... | collective-permute-start | bytes 3080 | tf_op jit(solution)/shard_map/ppermute | solution.py:40

commit v3 on v2

--- a/solution.py
+++ b/solution.py
@@ -28,6 +28,11 @@
     if is_power(count):
         return index ^ target
     return lax.rem(target - index + count, count)
+
+
+def exchange_steps(feat_count, ex_count):
+    steps = itertools.product(range(feat_count), range(ex_count))
+    return sorted(steps, key=lambda s: (any(s), not all(s), s))
 
 
 def swap(value, axes, steps):
@@ -126,7 +131,7 @@
         outs[step][...] = blocks[place_at(place, ctx_count, step)]
     feat, ex = lax.axis_index("feat"), lax.axis_index("ex")
     per_ex = own * feat_count
-    for k, steps in enumerate(itertools.product(range(feat_count), range(ex_count))):
+    for k, steps in enumerate(exchange_steps(feat_count, ex_count)):
         from_feat, from_ex = place_at(feat, feat_count, steps[0], -1), place_at(ex, ex_count, steps[1], -1)
         for e in range(own):
             wanted = order[(from_feat * ex_count + from_ex) * own + e]
@@ -140,7 +145,7 @@
     own, tokens, width = hidden.shape
     rank, model = factor.shape[0], cotangent.shape[2]
     shape = (own, rank // ctx_count, model)
-    chunks = 4
+    chunks = 2
     return pl.pallas_call(
         functools.partial(gradient_body, chunks, counts),
         out_shape=[jax.ShapeDtypeStruct(shape, jnp.float32)] * ctx_count
@@ -184,7 +189,7 @@
     sources, shares, (out, last_share, rows_ref, sem) = refs[:source_count], refs[source_count:-4], refs[-4:]
     copy = share_copy(projection_hbm, last_share, sem, len(shares))
     copy.start()
-    padded, width = out.shape
+    padded, count = rows_ref.shape[0], out.shape[0]
     own, share, model = sources[0].shape
     row = lax.broadcasted_iota(jnp.int32, (padded, model), 0)
     ranks = ranks_ref[...][:, :1]
@@ -200,18 +205,17 @@
         if number == len(shares):
             copy.wait()
         part = jnp.dot(rows_ref[:, first : first + depth], weights[...], preferred_element_type=jnp.float32)
-        if number == 0:
-            out[...] = part
-        else:
-            out[...] += part
+        total = part if number == 0 else total + part
+    out[...] = total[:count]
 
 
 def project(sources, ranks, projection, shares, ex_count):
     depth, width = projection.shape
-    padded = max(8, ranks.shape[0])
+    count = ranks.shape[0]
+    padded = max(8, count)
     return pl.pallas_call(
         functools.partial(project_body, len(sources)),
-        out_shape=jax.ShapeDtypeStruct((padded, width // ex_count), jnp.float32),
+        out_shape=jax.ShapeDtypeStruct((count, width // ex_count), jnp.float32),
         in_specs=[VMEM, HBM] + [VMEM] * (len(sources) + len(shares)),
         out_specs=VMEM,
         scratch_shapes=[
@@ -223,28 +227,35 @@
     )(ranks, hbm(projection), *sources, *[pltpu.with_memory_space_constraint(v, pltpu.VMEM) for v in shares])
 
 
-def total_body(per_ex, ex_count, *refs):
-    parts, outs = refs[: -2 * ex_count], refs[-2 * ex_count :]
+def total_body(ex_count, *refs):
+    parts, (own_rows, *others), squares_outs = refs[: -2 * ex_count], refs[-2 * ex_count : -ex_count], refs[-ex_count:]
     total = parts[0][...]
     for part in parts[1:]:
         total = total + part[...]
     squares = jnp.sum(total * total, axis=1, keepdims=True)
+    per_ex, width = own_rows.shape
+    own_rows[...] = total[:per_ex]
     for step in range(ex_count):
         rows = slice(step * per_ex, (step + 1) * per_ex)
-        outs[2 * step][...] = total[rows]
-        outs[2 * step + 1][...] = jnp.broadcast_to(squares[rows], (per_ex, 128))
-
-
-def totals(parts, count, ex_count):
-    per_ex, width = count // ex_count, parts[0].shape[1]
-    shapes = [jax.ShapeDtypeStruct((per_ex, width), jnp.float32), jax.ShapeDtypeStruct((per_ex, 128), jnp.float32)]
-    return pl.pallas_call(
-        functools.partial(total_body, per_ex, ex_count),
-        out_shape=shapes * ex_count,
+        spread = jnp.broadcast_to(squares[rows], (per_ex, 128))
+        squares_outs[step][...] = spread
+        if step:
+            others[step - 1][:, :width] = total[rows]
+            others[step - 1][:, width:] = spread
+
+
+def totals(parts, ex_count):
+    count, width = parts[0].shape
+    per_ex = count // ex_count
+    shape = lambda columns: jax.ShapeDtypeStruct((per_ex, columns), jnp.float32)
+    outs = pl.pallas_call(
+        functools.partial(total_body, ex_count),
+        out_shape=[shape(width)] + [shape(width + 128)] * (ex_count - 1) + [shape(128)] * ex_count,
         in_specs=[VMEM] * len(parts),
         out_specs=[VMEM] * (2 * ex_count),
         compiler_params=params(8),
     )(*parts)
+    return outs[:ex_count], outs[ex_count:]
 
 
 def scale_body(ex_count, columns, *refs):
@@ -253,10 +264,12 @@
     total = squares[0][...]
     for square in squares[1:]:
         total = total + square[...]
+    for row in rows[1:]:
+        total = total + row[:, width:]
     norm = jnp.sqrt(total[:, :1] / columns + 1e-06)
     for step in range(ex_count):
         place = place_at(lax.axis_index("ex"), ex_count, step, -1)
-        out[:, pl.ds(pl.multiple_of(place * width, 128), width)] = rows[step][...] / norm
+        out[:, pl.ds(pl.multiple_of(place * width, 128), width)] = rows[step][:, :width] / norm
 
 
 def scale(rows, squares, columns):
@@ -272,24 +285,23 @@
 
 def per_device(hidden, cotangent, adapter_down_factor, projection, lengths, slot_example_order):
     counts = ctx_count, feat_count, ex_count = tuple(map(lax.axis_size, ("ctx", "feat", "ex")))
-    count = hidden.shape[0] * feat_count * ex_count
     ctx_steps = range(1, ctx_count)
-    chip_steps = list(itertools.product(range(feat_count), range(ex_count)))[1:]
+    chip_steps = exchange_steps(feat_count, ex_count)[1:]
 
     *blocks, ranks, share = gradient(
         hidden, adapter_down_factor.T, cotangent, projection, lengths, slot_example_order, counts
     )
     shares = [share, load(projection, 1, ex_count, ranks)]
     grad_rows = sum_rows(
-        [blocks[0]] + [swap(blocks[s], ("ctx",), (s,)) for s in ctx_steps], jnp.bfloat16, shares[1]
+        [blocks[0]] + [swap(blocks[s], ("ctx",), (s,)) for s in reversed(ctx_steps)], jnp.bfloat16, shares[1]
     )
     shares.append(load(projection, 2, ex_count, grad_rows))
-    sources = [grad_rows] + [swap(grad_rows, ("feat", "ex"), steps) for steps in chip_steps]
+    sources = [grad_rows] + [swap(grad_rows, ("feat", "ex"), s) for s in chip_steps]
     product = project(sources, ranks, projection, shares, ex_count)
-    outs = totals([product] + [swap(product, ("ctx",), (s,)) for s in ctx_steps], count, ex_count)
-    rows = [outs[0]] + [swap(outs[2 * s], ("ex",), (s,)) for s in range(1, ex_count)]
-    squares = [outs[1]] + [swap(outs[2 * s[1] + 1], ("feat", "ex"), s) for s in chip_steps]
-    return scale(rows, squares, projection.shape[1] * feat_count)
+    rows, squares = totals([product] + [swap(product, ("ctx",), (s,)) for s in ctx_steps], ex_count)
+    taken = [rows[0]] + [swap(rows[s], ("ex",), (s,)) for s in range(1, ex_count)]
+    sums = [squares[0]] + [swap(squares[e], ("feat", "ex"), (f, e)) for f, e in chip_steps if f]
+    return scale(taken, sums, projection.shape[1] * feat_count)
 
 
 def solution(mesh):

time: 37.2 us -> 35.2 us (0.946)
  waiting for transfers between devices: 9.25 us -> 7.26 us
    ppermute x13 -> x12, waiting for transfers between devices: 9.25 us -> 7.26 us  [swap(): return lax.ppermute(value, tuple(axes) if len(axes) > 1 else axes[0], pairs)]
    ppermute x13 -> x12, starting transfers between devices: 14.3 us -> 14.6 us  [swap(): return lax.ppermute(value, tuple(axes) if len(axes) > 1 else axes[0], pairs)]
  transfers between devices with their start and end apart: 13 -> 12, of which waited for: 5 -> 6; matrix products, arithmetic and copies ran while one was open for 0% -> 0% of each run, Pallas kernels for 13% -> 14%
where the time goes in v3:
time: 35.2 us; the launch traced here: 35 us
  starting transfers between devices  14.6 us (41%)
  Pallas kernels  12.4 us (35%)
  waiting for transfers between devices  7.26 us (21%)
  between operations  0.72 us (2%)
    ppermute x12, starting transfers between devices, swap(): return lax.ppermute(value, tuple(axes) if len(axes) > 1 else axes[0], pairs)  14.6 us
    ppermute x12, waiting for transfers between devices, swap(): return lax.ppermute(value, tuple(axes) if len(axes) > 1 else axes[0], pairs)  7.26 us
    pallas_call x2, Pallas kernels, load(): pl.pallas_call(functools.partial(load_body, number), out_shape=pltpu.VMEM...  4.99 us
    pallas_call x1, Pallas kernels, project(): pl.pallas_call(functools.partial(project_body, len(sources)), out_shape=j...  4.01 us
    pallas_call x1, Pallas kernels, gradient(): pl.pallas_call(functools.partial(gradient_body, chunks, counts), out_shap...  2.58 us
    pallas_call x1, Pallas kernels, scale(): pl.pallas_call(functools.partial(scale_body, len(rows), columns), out_sha...  0.71 us
  transfers between devices with their start and end apart: 12, of which 6 were waited for; matrix products, arithmetic and copies ran while one was open for 0% of the time, Pallas kernels for 14%

profile of v3, /device:TPU:0, one launch (start us, length us, event | category | flops | bytes accessed | tf_op | source)
XLA Modules:
  0.0 35.0 jit_solution(13404008142253705465)
XLA Ops:
  0.7 2.6 %shard_map.64 = (f32[1,4,1024]{2,1,0:T(4,128)S(1)}, f32[1,4,1024]{2,1,0:T(4,128)S(1)}, f32[1,4,1024]{2,1,0:T(4,128)S(1)}, f32[1,4,1024]{2,1,0:T(4,128)S(1)}, s32...) custom-call(bf16[1,128,8192]{2,1,0:T(8,128)(2,1)} %hidden_hbm.1, bf16[16,8192]{1,0:T(8,128)(2,1)} %bitcast.1, ...), custom_call_target="tpu_custom_call" | custom-call | tf_op jit(solution)/shard_map/pallas_call | solution.py:149
  3.2 5.1 %collective-permute-start = (f32[1,4,1024]{2,1,0:T(4,128)S(1)}, f32[1,4,1024]{2,1,0:T(4,128)S(1)}, u32[]{:S(2)}, u32[]{:S(2)}) collective-permute-start(f32[1,4,1024]{2,1,0:T(4,128)S(1)} %get-tuple-element.17), channel_id=1, source_target_pairs={{0,12},{4,8},{8,4},{12,0},{1,13},{5,9},{9,5},{13,1},{2,14},{6,10},... | collective-permute-start | bytes 49160 | tf_op jit(solution)/shard_map/ppermute | solution.py:45
  8.4 0.0 collective-permute-start.1
  8.4 0.6 %collective-permute-start.2 = (f32[1,4,1024]{2,1,0:T(4,128)S(1)}, f32[1,4,1024]{2,1,0:T(4,128)S(1)}, u32[]{:S(2)}, u32[]{:S(2)}) collective-permute-start(f32[1,4,1024]{2,1,0:T(4,128)S(1)} %get-tuple-element.19), channel_id=1, source_target_pairs={{0,4},{4,0},{8,12},{12,8},{1,5},{5,1},{9,13},{13,9},{2,6},{6,2},{1... | collective-permute-start | bytes 49160 | tf_op jit(solution)/shard_map/ppermute | solution.py:45
  9.0 2.8 %shard_map.65.refs_4_.refs_5_ = bf16[1536,2048]{1,0:T(8,128)(2,1)S(1)} custom-call(s32[4,128]{1,0:T(4,128)S(1)} %get-tuple-element.15.after_ref.ranks_ref, bf16[4096,4096]{1,0:T(8,128)(2,1)} %projection_hbm.7), custom_call_target="tpu_custom_call" | custom-call | tf_op jit(solution)/shard_map/pallas_call | solution.py:84
  11.8 0.0 collective-permute-done.refs_1_
  11.8 1.2 %collective-permute-done.1.refs_2_ = f32[1,4,1024]{2,1,0:T(4,128)S(1)} collective-permute-done((f32[1,4,1024]{2,1,0:T(4,128)S(1)}, f32[1,4,1024]{2,1,0:T(4,128)S(1)}, u32[]{:S(2)}, u32[]{:S(2)}) %collective-permute-start.1) | collective-permute-done | bytes 16416 | tf_op jit(solution)/shard_map/ppermute | solution.py:45
  13.0 0.0 collective-permute-done.2.refs_3_
  13.0 1.6 %collective-permute-start.5 = (bf16[1,4,1024]{2,1,0:T(4,128)(2,1)S(1)}, bf16[1,4,1024]{2,1,0:T(4,128)(2,1)S(1)}, u32[]{:S(2)}, u32[]{:S(2)}) collective-permute-start(bf16[1,4,1024]{2,1,0:T(4,128)(2,1)S(1)} %shard_map.66.after_ref.refs_0_), channel_id=1, source_target_pairs={{0,2},{1,3},{2,0},{3,1},{4,6},{5,7},{6,4},{7,5},{8,10},{9,11},{10,... | collective-permute-start | bytes 24584 | tf_op jit(solution)/shard_map/ppermute | solution.py:45
  14.6 0.0 collective-permute-start.4
  14.6 0.6 %collective-permute-start.3 = (bf16[1,4,1024]{2,1,0:T(4,128)(2,1)S(1)}, bf16[1,4,1024]{2,1,0:T(4,128)(2,1)S(1)}, u32[]{:S(2)}, u32[]{:S(2)}) collective-permute-start(bf16[1,4,1024]{2,1,0:T(4,128)(2,1)S(1)} %shard_map.66.after_ref.refs_0_), channel_id=1, source_target_pairs={{0,3},{1,2},{2,1},{3,0},{4,7},{5,6},{6,5},{7,4},{8,11},{9,10},{10,... | collective-permute-start | bytes 24584 | tf_op jit(solution)/shard_map/ppermute | solution.py:45
  15.2 2.2 %shard_map.67.refs_6_ = bf16[1024,2048]{1,0:T(8,128)(2,1)S(1)} custom-call(bf16[1,4,1024]{2,1,0:T(4,128)(2,1)S(1)} %shard_map.66.after_ref.refs_0_, bf16[4096,4096]{1,0:T(8,128)(2,1)} %projection_hbm.7), custom_call_target="tpu_custom_call" | custom-call | tf_op jit(solution)/shard_map/pallas_call | solution.py:84
  17.5 0.2 collective-permute-done.3.refs_1_
  17.7 4.0 %shard_map.68.refs_0_ = f32[4,2048]{1,0:T(4,128)S(1)} custom-call(s32[4,128]{1,0:T(4,128)S(1)} %get-tuple-element.15.after_ref.ranks_ref, bf16[4096,4096]{1,0:T(8,128)(2,1)} %projection_hbm.7, bf16[1,4,1024]{2,1,0:T(4,128)(2,1)S(1)} %shard_map.66.after_ref.refs_0_, bf16[1,4,1024]{2,1,0:T(4,128)(2,1)S(1)} %collective-permute-done.3.refs_1_, ...), custom_call_target="tpu_custom_call" | custom-call | tf_op jit(solution)/shard_map/pallas_call | solution.py:216
  21.7 2.6 %collective-permute-start.8 = (f32[4,2048]{1,0:T(4,128)S(1)}, f32[4,2048]{1,0:T(4,128)S(1)}, u32[]{:S(2)}, u32[]{:S(2)}) collective-permute-start(f32[4,2048]{1,0:T(4,128)S(1)} %shard_map.68.refs_0_), channel_id=1, source_target_pairs={{0,12},{4,8},{8,4},{12,0},{1,13},{5,9},{9,5},{13,1},{2,14},{6,10},... | collective-permute-start | bytes 98312 | tf_op jit(solution)/shard_map/ppermute | solution.py:45
  24.3 1.8 %collective-permute-start.6 = (f32[4,2048]{1,0:T(4,128)S(1)}, f32[4,2048]{1,0:T(4,128)S(1)}, u32[]{:S(2)}, u32[]{:S(2)}) collective-permute-start(f32[4,2048]{1,0:T(4,128)S(1)} %shard_map.68.refs_0_), channel_id=1, source_target_pairs={{0,4},{4,0},{8,12},{12,8},{1,5},{5,1},{9,13},{13,9},{2,6},{6,2},{1... | collective-permute-start | bytes 98312 | tf_op jit(solution)/shard_map/ppermute | solution.py:45
  26.2 1.4 %collective-permute-done.8.refs_3_ = f32[4,2048]{1,0:T(4,128)S(1)} collective-permute-done((f32[4,2048]{1,0:T(4,128)S(1)}, f32[4,2048]{1,0:T(4,128)S(1)}, u32[]{:S(2)}, u32[]{:S(2)}) %collective-permute-start.8) | collective-permute-done | bytes 32800 | tf_op jit(solution)/shard_map/ppermute | solution.py:45
  27.5 1.7 %collective-permute-done.7.refs_2_ = f32[4,2048]{1,0:T(4,128)S(1)} collective-permute-done((f32[4,2048]{1,0:T(4,128)S(1)}, f32[4,2048]{1,0:T(4,128)S(1)}, u32[]{:S(2)}, u32[]{:S(2)}) %collective-permute-start.7) | collective-permute-done | bytes 32800 | tf_op jit(solution)/shard_map/ppermute | solution.py:45
  29.2 0.1 shard_map.69
  29.3 1.4 %collective-permute-start.10 = (f32[2,128]{1,0:T(2,128)S(1)}, f32[2,128]{1,0:T(2,128)S(1)}, u32[]{:S(2)}, u32[]{:S(2)}) collective-permute-start(f32[2,128]{1,0:T(2,128)S(1)} %get-tuple-element.24), channel_id=1, source_target_pairs={{0,3},{1,2},{2,1},{3,0},{4,7},{5,6},{6,5},{7,4},{8,11},{9,10},{10,... | collective-permute-start | bytes 3080 | tf_op jit(solution)/shard_map/ppermute | solution.py:45
  30.7 0.7 %collective-permute-start.11 = (f32[2,128]{1,0:T(2,128)S(1)}, f32[2,128]{1,0:T(2,128)S(1)}, u32[]{:S(2)}, u32[]{:S(2)}) collective-permute-start(f32[2,128]{1,0:T(2,128)S(1)} %get-tuple-element.23.refs_2_), channel_id=1, source_target_pairs={{0,2},{1,3},{2,0},{3,1},{4,6},{5,7},{6,4},{7,5},{8,10},{9,11},{10,... | collective-permute-start | bytes 3080 | tf_op jit(solution)/shard_map/ppermute | solution.py:45
  31.4 0.9 %collective-permute-done.10.refs_3_ = f32[2,128]{1,0:T(2,128)S(1)} collective-permute-done((f32[2,128]{1,0:T(2,128)S(1)}, f32[2,128]{1,0:T(2,128)S(1)}, u32[]{:S(2)}, u32[]{:S(2)}) %collective-permute-start.10) | collective-permute-done | bytes 1056 | tf_op jit(solution)/shard_map/ppermute | solution.py:45
  32.3 1.9 %collective-permute-done.11.refs_4_ = f32[2,128]{1,0:T(2,128)S(1)} collective-permute-done((f32[2,128]{1,0:T(2,128)S(1)}, f32[2,128]{1,0:T(2,128)S(1)}, u32[]{:S(2)}, u32[]{:S(2)}) %collective-permute-start.11) | collective-permute-done | bytes 1056 | tf_op jit(solution)/shard_map/ppermute | solution.py:45
  34.3 0.7 %shard_map.70 = f32[2,4096]{1,0:T(2,128)} custom-call(f32[2,2048]{1,0:T(2,128)S(1)} %get-tuple-element.21.refs_0_, f32[2,2176]{1,0:T(2,128)S(1)} %collective-permute-done.9.refs_1_, f32[2,128]{1,0:T(2,128)S(1)} %get-tuple-element.23.refs_2_, f32[2,128]{1,0:T(2,128)S(1)} %collective-permute-done.10.refs_3_, f32[2,128]{1,0:T(2,128)S(1)} %collective-permute-done.11.refs_4_), custom_call_target="tpu_custom_call" | custom-call | tf_op jit(solution)/shard_map/pallas_call | solution.py:277
  (7 shorter events, 0.0 us)
Async XLA Ops:
  3.2 8.6 %collective-permute-start = (f32[1,4,1024]{2,1,0:T(4,128)S(1)}, f32[1,4,1024]{2,1,0:T(4,128)S(1)}, u32[]{:S(2)}, u32[]{:S(2)}) collective-permute-start(f32[1,4,1024]{2,1,0:T(4,128)S(1)} %get-tuple-element.17), channel_id=1, source_target_pairs={{0,12},{4,8},{8,4},{12,0},{1,13},{5,9},{9,5},{13,1},{2,14},{6,10},... | collective-permute-start | bytes 49160 | tf_op jit(solution)/shard_map/ppermute | solution.py:45
  8.4 4.6 %collective-permute-start.1 = (f32[1,4,1024]{2,1,0:T(4,128)S(1)}, f32[1,4,1024]{2,1,0:T(4,128)S(1)}, u32[]{:S(2)}, u32[]{:S(2)}) collective-permute-start(f32[1,4,1024]{2,1,0:T(4,128)S(1)} %get-tuple-element.18), channel_id=1, source_target_pairs={{0,8},{4,12},{8,0},{12,4},{1,9},{5,13},{9,1},{13,5},{2,10},{6,14},... | collective-permute-start | bytes 49160 | tf_op jit(solution)/shard_map/ppermute | solution.py:45
  8.4 4.6 %collective-permute-start.2 = (f32[1,4,1024]{2,1,0:T(4,128)S(1)}, f32[1,4,1024]{2,1,0:T(4,128)S(1)}, u32[]{:S(2)}, u32[]{:S(2)}) collective-permute-start(f32[1,4,1024]{2,1,0:T(4,128)S(1)} %get-tuple-element.19), channel_id=1, source_target_pairs={{0,4},{4,0},{8,12},{12,8},{1,5},{5,1},{9,13},{13,9},{2,6},{6,2},{1... | collective-permute-start | bytes 49160 | tf_op jit(solution)/shard_map/ppermute | solution.py:45
  13.0 4.4 %collective-permute-start.5 = (bf16[1,4,1024]{2,1,0:T(4,128)(2,1)S(1)}, bf16[1,4,1024]{2,1,0:T(4,128)(2,1)S(1)}, u32[]{:S(2)}, u32[]{:S(2)}) collective-permute-start(bf16[1,4,1024]{2,1,0:T(4,128)(2,1)S(1)} %shard_map.66.after_ref.refs_0_), channel_id=1, source_target_pairs={{0,2},{1,3},{2,0},{3,1},{4,6},{5,7},{6,4},{7,5},{8,10},{9,11},{10,... | collective-permute-start | bytes 24584 | tf_op jit(solution)/shard_map/ppermute | solution.py:45
  14.6 2.9 %collective-permute-start.4 = (bf16[1,4,1024]{2,1,0:T(4,128)(2,1)S(1)}, bf16[1,4,1024]{2,1,0:T(4,128)(2,1)S(1)}, u32[]{:S(2)}, u32[]{:S(2)}) collective-permute-start(bf16[1,4,1024]{2,1,0:T(4,128)(2,1)S(1)} %shard_map.66.after_ref.refs_0_), channel_id=1, source_target_pairs={{0,1},{1,0},{2,3},{3,2},{4,5},{5,4},{6,7},{7,6},{8,9},{9,8},{10,11... | collective-permute-start | bytes 24584 | tf_op jit(solution)/shard_map/ppermute | solution.py:45
  14.6 3.1 %collective-permute-start.3 = (bf16[1,4,1024]{2,1,0:T(4,128)(2,1)S(1)}, bf16[1,4,1024]{2,1,0:T(4,128)(2,1)S(1)}, u32[]{:S(2)}, u32[]{:S(2)}) collective-permute-start(bf16[1,4,1024]{2,1,0:T(4,128)(2,1)S(1)} %shard_map.66.after_ref.refs_0_), channel_id=1, source_target_pairs={{0,3},{1,2},{2,1},{3,0},{4,7},{5,6},{6,5},{7,4},{8,11},{9,10},{10,... | collective-permute-start | bytes 24584 | tf_op jit(solution)/shard_map/ppermute | solution.py:45
  21.7 5.8 %collective-permute-start.8 = (f32[4,2048]{1,0:T(4,128)S(1)}, f32[4,2048]{1,0:T(4,128)S(1)}, u32[]{:S(2)}, u32[]{:S(2)}) collective-permute-start(f32[4,2048]{1,0:T(4,128)S(1)} %shard_map.68.refs_0_), channel_id=1, source_target_pairs={{0,12},{4,8},{8,4},{12,0},{1,13},{5,9},{9,5},{13,1},{2,14},{6,10},... | collective-permute-start | bytes 98312 | tf_op jit(solution)/shard_map/ppermute | solution.py:45
  24.3 4.8 %collective-permute-start.7 = (f32[4,2048]{1,0:T(4,128)S(1)}, f32[4,2048]{1,0:T(4,128)S(1)}, u32[]{:S(2)}, u32[]{:S(2)}) collective-permute-start(f32[4,2048]{1,0:T(4,128)S(1)} %shard_map.68.refs_0_), channel_id=1, source_target_pairs={{0,8},{4,12},{8,0},{12,4},{1,9},{5,13},{9,1},{13,5},{2,10},{6,14},... | collective-permute-start | bytes 98312 | tf_op jit(solution)/shard_map/ppermute | solution.py:45
  24.3 4.8 %collective-permute-start.6 = (f32[4,2048]{1,0:T(4,128)S(1)}, f32[4,2048]{1,0:T(4,128)S(1)}, u32[]{:S(2)}, u32[]{:S(2)}) collective-permute-start(f32[4,2048]{1,0:T(4,128)S(1)} %shard_map.68.refs_0_), channel_id=1, source_target_pairs={{0,4},{4,0},{8,12},{12,8},{1,5},{5,1},{9,13},{13,9},{2,6},{6,2},{1... | collective-permute-start | bytes 98312 | tf_op jit(solution)/shard_map/ppermute | solution.py:45
  29.3 5.0 %collective-permute-start.9 = (f32[2,2176]{1,0:T(2,128)S(1)}, f32[2,2176]{1,0:T(2,128)S(1)}, u32[]{:S(2)}, u32[]{:S(2)}) collective-permute-start(f32[2,2176]{1,0:T(2,128)S(1)} %get-tuple-element.22), channel_id=1, source_target_pairs={{0,1},{1,0},{2,3},{3,2},{4,5},{5,4},{6,7},{7,6},{8,9},{9,8},{10,11... | collective-permute-start | bytes 52232 | tf_op jit(solution)/shard_map/ppermute | solution.py:45
  29.3 3.1 %collective-permute-start.10 = (f32[2,128]{1,0:T(2,128)S(1)}, f32[2,128]{1,0:T(2,128)S(1)}, u32[]{:S(2)}, u32[]{:S(2)}) collective-permute-start(f32[2,128]{1,0:T(2,128)S(1)} %get-tuple-element.24), channel_id=1, source_target_pairs={{0,3},{1,2},{2,1},{3,0},{4,7},{5,6},{6,5},{7,4},{8,11},{9,10},{10,... | collective-permute-start | bytes 3080 | tf_op jit(solution)/shard_map/ppermute | solution.py:45
  30.7 3.6 %collective-permute-start.11 = (f32[2,128]{1,0:T(2,128)S(1)}, f32[2,128]{1,0:T(2,128)S(1)}, u32[]{:S(2)}, u32[]{:S(2)}) collective-permute-start(f32[2,128]{1,0:T(2,128)S(1)} %get-tuple-element.23.refs_2_), channel_id=1, source_target_pairs={{0,2},{1,3},{2,0},{3,1},{4,6},{5,7},{6,4},{7,5},{8,10},{9,11},{10,... | collective-permute-start | bytes 3080 | tf_op jit(solution)/shard_map/ppermute | solution.py:45

commit v4 on v3

--- a/solution.py
+++ b/solution.py
@@ -228,7 +228,8 @@
 
 
 def total_body(ex_count, *refs):
-    parts, (own_rows, *others), squares_outs = refs[: -2 * ex_count], refs[-2 * ex_count : -ex_count], refs[-ex_count:]
+    parts = refs[: -2 * ex_count - 1]
+    near, *others, own_rows, own_squares = refs[-2 * ex_count - 1 :]
     total = parts[0][...]
     for part in parts[1:]:
         total = total + part[...]
@@ -238,28 +239,31 @@
     for step in range(ex_count):
         rows = slice(step * per_ex, (step + 1) * per_ex)
         spread = jnp.broadcast_to(squares[rows], (per_ex, 128))
-        squares_outs[step][...] = spread
-        if step:
-            others[step - 1][:, :width] = total[rows]
-            others[step - 1][:, width:] = spread
+        if step == 0:
+            near[...] = spread
+            own_squares[...] = spread
+        else:
+            others[2 * step - 2][:, :width] = total[rows]
+            others[2 * step - 2][:, width:] = spread
+            others[2 * step - 1][...] = spread
 
 
 def totals(parts, ex_count):
     count, width = parts[0].shape
     per_ex = count // ex_count
     shape = lambda columns: jax.ShapeDtypeStruct((per_ex, columns), jnp.float32)
-    outs = pl.pallas_call(
+    near, *others, own_rows, own_squares = pl.pallas_call(
         functools.partial(total_body, ex_count),
-        out_shape=[shape(width)] + [shape(width + 128)] * (ex_count - 1) + [shape(128)] * ex_count,
+        out_shape=[shape(128)] + [shape(width + 128), shape(128)] * (ex_count - 1) + [shape(width), shape(128)],
         in_specs=[VMEM] * len(parts),
-        out_specs=[VMEM] * (2 * ex_count),
+        out_specs=[VMEM] * (2 * ex_count + 1),
         compiler_params=params(8),
     )(*parts)
-    return outs[:ex_count], outs[ex_count:]
-
-
-def scale_body(ex_count, columns, *refs):
-    rows, squares, out = refs[:ex_count], refs[ex_count:-1], refs[-1]
+    return [own_rows, *others[::2]], [near, *others[1::2]], own_squares
+
+
+def scale_body(near_count, ex_count, columns, *refs):
+    rows, squares, out = refs[near_count : near_count + ex_count], refs[:near_count] + refs[near_count + ex_count : -1], refs[-1]
     width = rows[0].shape[1]
     total = squares[0][...]
     for square in squares[1:]:
@@ -272,20 +276,21 @@
         out[:, pl.ds(pl.multiple_of(place * width, 128), width)] = rows[step][:, :width] / norm
 
 
-def scale(rows, squares, columns):
+def scale(near, rows, squares, columns):
     per_ex, width = rows[0].shape
-    return pl.pallas_call(
-        functools.partial(scale_body, len(rows), columns),
+    operands = (*near, *rows, *squares)
+    return pl.pallas_call(
+        functools.partial(scale_body, len(near), len(rows), columns),
         out_shape=jax.ShapeDtypeStruct((per_ex, width * len(rows)), jnp.float32),
-        in_specs=[VMEM] * (len(rows) + len(squares)),
+        in_specs=[VMEM] * len(operands),
         out_specs=VMEM,
         compiler_params=params(8),
-    )(*rows, *squares)
+    )(*operands)
 
 
 def per_device(hidden, cotangent, adapter_down_factor, projection, lengths, slot_example_order):
     counts = ctx_count, feat_count, ex_count = tuple(map(lax.axis_size, ("ctx", "feat", "ex")))
-    ctx_steps = range(1, ctx_count)
+    ctx_steps = sorted(range(1, ctx_count), key=lambda s: (s == 1, s))
     chip_steps = exchange_steps(feat_count, ex_count)[1:]
 
     *blocks, ranks, share = gradient(
@@ -293,15 +298,17 @@
     )
     shares = [share, load(projection, 1, ex_count, ranks)]
     grad_rows = sum_rows(
-        [blocks[0]] + [swap(blocks[s], ("ctx",), (s,)) for s in reversed(ctx_steps)], jnp.bfloat16, shares[1]
+        [blocks[0]] + [swap(blocks[s], ("ctx",), (s,)) for s in ctx_steps], jnp.bfloat16, shares[1]
     )
     shares.append(load(projection, 2, ex_count, grad_rows))
     sources = [grad_rows] + [swap(grad_rows, ("feat", "ex"), s) for s in chip_steps]
     product = project(sources, ranks, projection, shares, ex_count)
-    rows, squares = totals([product] + [swap(product, ("ctx",), (s,)) for s in ctx_steps], ex_count)
+    rows, squares, own_squares = totals([product] + [swap(product, ("ctx",), (s,)) for s in reversed(ctx_steps)], ex_count)
     taken = [rows[0]] + [swap(rows[s], ("ex",), (s,)) for s in range(1, ex_count)]
-    sums = [squares[0]] + [swap(squares[e], ("feat", "ex"), (f, e)) for f, e in chip_steps if f]
-    return scale(taken, sums, projection.shape[1] * feat_count)
+    near, far = (
+        [swap(squares[e], ("feat", "ex"), (f, e)) for f, e in chip_steps if f and bool(e) == both] for both in (False, True)
+    )
+    return scale(near, taken, [*far, own_squares], projection.shape[1] * feat_count)
 
 
 def solution(mesh):

time: 35.2 us -> 34.5 us (0.980)
  starting transfers between devices: 14.6 us -> 13.3 us
  waiting for transfers between devices: 7.26 us -> 7.78 us
    ppermute x12, starting transfers between devices: 14.6 us -> 13.3 us  [swap(): return lax.ppermute(value, tuple(axes) if len(axes) > 1 else axes[0], pairs)]
    ppermute x12, waiting for transfers between devices: 7.26 us -> 7.78 us  [swap(): return lax.ppermute(value, tuple(axes) if len(axes) > 1 else axes[0], pairs)]
  transfers between devices with their start and end apart: 12 -> 12, of which waited for: 6 -> 6; matrix products, arithmetic and copies ran while one was open for 0% -> 0% of each run, Pallas kernels for 14% -> 15%
where the time goes in v4:
time: 34.5 us; the launch traced here: 34.2 us
  starting transfers between devices  13.3 us (39%)
  Pallas kernels  12.4 us (36%)
  waiting for transfers between devices  7.78 us (23%)
  between operations  0.73 us (2%)
    ppermute x12, starting transfers between devices, swap(): return lax.ppermute(value, tuple(axes) if len(axes) > 1 else axes[0], pairs)  13.3 us
    ppermute x12, waiting for transfers between devices, swap(): return lax.ppermute(value, tuple(axes) if len(axes) > 1 else axes[0], pairs)  7.78 us
    pallas_call x2, Pallas kernels, load(): pl.pallas_call(functools.partial(load_body, number), out_shape=pltpu.VMEM...  4.99 us
    pallas_call x1, Pallas kernels, project(): pl.pallas_call(functools.partial(project_body, len(sources)), out_shape=j...  4.01 us
    pallas_call x1, Pallas kernels, gradient(): pl.pallas_call(functools.partial(gradient_body, chunks, counts), out_shap...  2.58 us
    pallas_call x1, Pallas kernels, scale(): pl.pallas_call(functools.partial(scale_body, len(near), len(rows), column...  0.71 us
  transfers between devices with their start and end apart: 12, of which 6 were waited for; matrix products, arithmetic and copies ran while one was open for 0% of the time, Pallas kernels for 15%

profile of v4, /device:TPU:0, one launch (start us, length us, event | category | flops | bytes accessed | tf_op | source)
XLA Modules:
  0.0 34.2 jit_solution(487535919071661018)
XLA Ops:
  0.7 2.6 %shard_map.64 = (f32[1,4,1024]{2,1,0:T(4,128)S(1)}, f32[1,4,1024]{2,1,0:T(4,128)S(1)}, f32[1,4,1024]{2,1,0:T(4,128)S(1)}, f32[1,4,1024]{2,1,0:T(4,128)S(1)}, s32...) custom-call(bf16[1,128,8192]{2,1,0:T(8,128)(2,1)} %hidden_hbm.1, bf16[16,8192]{1,0:T(8,128)(2,1)} %bitcast.1, ...), custom_call_target="tpu_custom_call" | custom-call | tf_op jit(solution)/shard_map/pallas_call | solution.py:149
  3.2 4.1 %collective-permute-start = (f32[1,4,1024]{2,1,0:T(4,128)S(1)}, f32[1,4,1024]{2,1,0:T(4,128)S(1)}, u32[]{:S(2)}, u32[]{:S(2)}) collective-permute-start(f32[1,4,1024]{2,1,0:T(4,128)S(1)} %get-tuple-element.18), channel_id=1, source_target_pairs={{0,8},{4,12},{8,0},{12,4},{1,9},{5,13},{9,1},{13,5},{2,10},{6,14},... | collective-permute-start | bytes 49160 | tf_op jit(solution)/shard_map/ppermute | solution.py:45
  7.4 1.3 %collective-permute-start.1 = (f32[1,4,1024]{2,1,0:T(4,128)S(1)}, f32[1,4,1024]{2,1,0:T(4,128)S(1)}, u32[]{:S(2)}, u32[]{:S(2)}) collective-permute-start(f32[1,4,1024]{2,1,0:T(4,128)S(1)} %get-tuple-element.19), channel_id=1, source_target_pairs={{0,12},{4,8},{8,4},{12,0},{1,13},{5,9},{9,5},{13,1},{2,14},{6,10},... | collective-permute-start | bytes 49160 | tf_op jit(solution)/shard_map/ppermute | solution.py:45
  8.7 0.2 collective-permute-start.2
  8.9 2.8 %shard_map.65.refs_4_.refs_5_ = bf16[1536,2048]{1,0:T(8,128)(2,1)S(1)} custom-call(s32[4,128]{1,0:T(4,128)S(1)} %get-tuple-element.16.after_ref.ranks_ref, bf16[4096,4096]{1,0:T(8,128)(2,1)} %projection_hbm.7), custom_call_target="tpu_custom_call" | custom-call | tf_op jit(solution)/shard_map/pallas_call | solution.py:84
  11.8 0.0 collective-permute-done.refs_1_
  11.8 1.1 %collective-permute-done.1.refs_2_ = f32[1,4,1024]{2,1,0:T(4,128)S(1)} collective-permute-done((f32[1,4,1024]{2,1,0:T(4,128)S(1)}, f32[1,4,1024]{2,1,0:T(4,128)S(1)}, u32[]{:S(2)}, u32[]{:S(2)}) %collective-permute-start.1) | collective-permute-done | bytes 16416 | tf_op jit(solution)/shard_map/ppermute | solution.py:45
  12.9 0.0 collective-permute-done.2.refs_3_
  12.9 1.6 %collective-permute-start.5 = (bf16[1,4,1024]{2,1,0:T(4,128)(2,1)S(1)}, bf16[1,4,1024]{2,1,0:T(4,128)(2,1)S(1)}, u32[]{:S(2)}, u32[]{:S(2)}) collective-permute-start(bf16[1,4,1024]{2,1,0:T(4,128)(2,1)S(1)} %shard_map.66.after_ref.refs_0_), channel_id=1, source_target_pairs={{0,2},{1,3},{2,0},{3,1},{4,6},{5,7},{6,4},{7,5},{8,10},{9,11},{10,... | collective-permute-start | bytes 24584 | tf_op jit(solution)/shard_map/ppermute | solution.py:45
  14.5 0.6 %collective-permute-start.3 = (bf16[1,4,1024]{2,1,0:T(4,128)(2,1)S(1)}, bf16[1,4,1024]{2,1,0:T(4,128)(2,1)S(1)}, u32[]{:S(2)}, u32[]{:S(2)}) collective-permute-start(bf16[1,4,1024]{2,1,0:T(4,128)(2,1)S(1)} %shard_map.66.after_ref.refs_0_), channel_id=1, source_target_pairs={{0,3},{1,2},{2,1},{3,0},{4,7},{5,6},{6,5},{7,4},{8,11},{9,10},{10,... | collective-permute-start | bytes 24584 | tf_op jit(solution)/shard_map/ppermute | solution.py:45
  15.1 2.2 %shard_map.67.refs_6_ = bf16[1024,2048]{1,0:T(8,128)(2,1)S(1)} custom-call(bf16[1,4,1024]{2,1,0:T(4,128)(2,1)S(1)} %shard_map.66.after_ref.refs_0_, bf16[4096,4096]{1,0:T(8,128)(2,1)} %projection_hbm.7), custom_call_target="tpu_custom_call" | custom-call | tf_op jit(solution)/shard_map/pallas_call | solution.py:84
  17.4 0.2 collective-permute-done.3.refs_1_
  17.6 4.0 %shard_map.68.refs_0_ = f32[4,2048]{1,0:T(4,128)S(1)} custom-call(s32[4,128]{1,0:T(4,128)S(1)} %get-tuple-element.16.after_ref.ranks_ref, bf16[4096,4096]{1,0:T(8,128)(2,1)} %projection_hbm.7, bf16[1,4,1024]{2,1,0:T(4,128)(2,1)S(1)} %shard_map.66.after_ref.refs_0_, bf16[1,4,1024]{2,1,0:T(4,128)(2,1)S(1)} %collective-permute-done.3.refs_1_, ...), custom_call_target="tpu_custom_call" | custom-call | tf_op jit(solution)/shard_map/pallas_call | solution.py:216
  21.6 1.7 %collective-permute-start.8 = (f32[4,2048]{1,0:T(4,128)S(1)}, f32[4,2048]{1,0:T(4,128)S(1)}, u32[]{:S(2)}, u32[]{:S(2)}) collective-permute-start(f32[4,2048]{1,0:T(4,128)S(1)} %shard_map.68.refs_0_), channel_id=1, source_target_pairs={{0,8},{4,12},{8,0},{12,4},{1,9},{5,13},{9,1},{13,5},{2,10},{6,14},... | collective-permute-start | bytes 98312 | tf_op jit(solution)/shard_map/ppermute | solution.py:45
  23.3 1.3 %collective-permute-start.7 = (f32[4,2048]{1,0:T(4,128)S(1)}, f32[4,2048]{1,0:T(4,128)S(1)}, u32[]{:S(2)}, u32[]{:S(2)}) collective-permute-start(f32[4,2048]{1,0:T(4,128)S(1)} %shard_map.68.refs_0_), channel_id=1, source_target_pairs={{0,12},{4,8},{8,4},{12,0},{1,13},{5,9},{9,5},{13,1},{2,14},{6,10},... | collective-permute-start | bytes 98312 | tf_op jit(solution)/shard_map/ppermute | solution.py:45
  24.7 0.5 %collective-permute-start.6 = (f32[4,2048]{1,0:T(4,128)S(1)}, f32[4,2048]{1,0:T(4,128)S(1)}, u32[]{:S(2)}, u32[]{:S(2)}) collective-permute-start(f32[4,2048]{1,0:T(4,128)S(1)} %shard_map.68.refs_0_), channel_id=1, source_target_pairs={{0,4},{4,0},{8,12},{12,8},{1,5},{5,1},{9,13},{13,9},{2,6},{6,2},{1... | collective-permute-start | bytes 98312 | tf_op jit(solution)/shard_map/ppermute | solution.py:45
  25.1 2.1 %collective-permute-done.8.refs_3_ = f32[4,2048]{1,0:T(4,128)S(1)} collective-permute-done((f32[4,2048]{1,0:T(4,128)S(1)}, f32[4,2048]{1,0:T(4,128)S(1)}, u32[]{:S(2)}, u32[]{:S(2)}) %collective-permute-start.8) | collective-permute-done | bytes 32800 | tf_op jit(solution)/shard_map/ppermute | solution.py:45
  27.3 1.8 %collective-permute-done.7.refs_2_ = f32[4,2048]{1,0:T(4,128)S(1)} collective-permute-done((f32[4,2048]{1,0:T(4,128)S(1)}, f32[4,2048]{1,0:T(4,128)S(1)}, u32[]{:S(2)}, u32[]{:S(2)}) %collective-permute-start.7) | collective-permute-done | bytes 32800 | tf_op jit(solution)/shard_map/ppermute | solution.py:45
  29.1 0.1 shard_map.69
  29.2 1.4 %collective-permute-start.9 = (f32[2,128]{1,0:T(2,128)S(1)}, f32[2,128]{1,0:T(2,128)S(1)}, u32[]{:S(2)}, u32[]{:S(2)}) collective-permute-start(f32[2,128]{1,0:T(2,128)S(1)} %get-tuple-element.22), channel_id=1, source_target_pairs={{0,2},{1,3},{2,0},{3,1},{4,6},{5,7},{6,4},{7,5},{8,10},{9,11},{10,... | collective-permute-start | bytes 3080 | tf_op jit(solution)/shard_map/ppermute | solution.py:45
  30.5 0.5 %collective-permute-start.11 = (f32[2,128]{1,0:T(2,128)S(1)}, f32[2,128]{1,0:T(2,128)S(1)}, u32[]{:S(2)}, u32[]{:S(2)}) collective-permute-start(f32[2,128]{1,0:T(2,128)S(1)} %get-tuple-element.25), channel_id=1, source_target_pairs={{0,3},{1,2},{2,1},{3,0},{4,7},{5,6},{6,5},{7,4},{8,11},{9,10},{10,... | collective-permute-start | bytes 3080 | tf_op jit(solution)/shard_map/ppermute | solution.py:45
  31.0 1.8 %collective-permute-done.9.refs_0_ = f32[2,128]{1,0:T(2,128)S(1)} collective-permute-done((f32[2,128]{1,0:T(2,128)S(1)}, f32[2,128]{1,0:T(2,128)S(1)}, u32[]{:S(2)}, u32[]{:S(2)}) %collective-permute-start.9) | collective-permute-done | bytes 1056 | tf_op jit(solution)/shard_map/ppermute | solution.py:45
  32.8 0.7 %collective-permute-done.11.refs_3_ = f32[2,128]{1,0:T(2,128)S(1)} collective-permute-done((f32[2,128]{1,0:T(2,128)S(1)}, f32[2,128]{1,0:T(2,128)S(1)}, u32[]{:S(2)}, u32[]{:S(2)}) %collective-permute-start.11) | collective-permute-done | bytes 1056 | tf_op jit(solution)/shard_map/ppermute | solution.py:45
  33.5 0.7 %shard_map.70 = f32[2,4096]{1,0:T(2,128)} custom-call(f32[2,128]{1,0:T(2,128)S(1)} %collective-permute-done.9.refs_0_, f32[2,2048]{1,0:T(2,128)S(1)} %get-tuple-element.23.refs_1_, f32[2,2176]{1,0:T(2,128)S(1)} %collective-permute-done.10.refs_2_, f32[2,128]{1,0:T(2,128)S(1)} %collective-permute-done.11.refs_3_, f32[2,128]{1,0:T(2,128)S(1)} %get-tuple-element.26.refs_4_), custom_call_target="tpu_custom_call" | custom-call | tf_op jit(solution)/shard_map/pallas_call | solution.py:282
  (7 shorter events, 0.0 us)
Async XLA Ops:
  3.2 8.5 %collective-permute-start = (f32[1,4,1024]{2,1,0:T(4,128)S(1)}, f32[1,4,1024]{2,1,0:T(4,128)S(1)}, u32[]{:S(2)}, u32[]{:S(2)}) collective-permute-start(f32[1,4,1024]{2,1,0:T(4,128)S(1)} %get-tuple-element.18), channel_id=1, source_target_pairs={{0,8},{4,12},{8,0},{12,4},{1,9},{5,13},{9,1},{13,5},{2,10},{6,14},... | collective-permute-start | bytes 49160 | tf_op jit(solution)/shard_map/ppermute | solution.py:45
  7.4 5.5 %collective-permute-start.1 = (f32[1,4,1024]{2,1,0:T(4,128)S(1)}, f32[1,4,1024]{2,1,0:T(4,128)S(1)}, u32[]{:S(2)}, u32[]{:S(2)}) collective-permute-start(f32[1,4,1024]{2,1,0:T(4,128)S(1)} %get-tuple-element.19), channel_id=1, source_target_pairs={{0,12},{4,8},{8,4},{12,0},{1,13},{5,9},{9,5},{13,1},{2,14},{6,10},... | collective-permute-start | bytes 49160 | tf_op jit(solution)/shard_map/ppermute | solution.py:45
  8.7 4.2 %collective-permute-start.2 = (f32[1,4,1024]{2,1,0:T(4,128)S(1)}, f32[1,4,1024]{2,1,0:T(4,128)S(1)}, u32[]{:S(2)}, u32[]{:S(2)}) collective-permute-start(f32[1,4,1024]{2,1,0:T(4,128)S(1)} %get-tuple-element.20), channel_id=1, source_target_pairs={{0,4},{4,0},{8,12},{12,8},{1,5},{5,1},{9,13},{13,9},{2,6},{6,2},{1... | collective-permute-start | bytes 49160 | tf_op jit(solution)/shard_map/ppermute | solution.py:45
  12.9 4.4 %collective-permute-start.5 = (bf16[1,4,1024]{2,1,0:T(4,128)(2,1)S(1)}, bf16[1,4,1024]{2,1,0:T(4,128)(2,1)S(1)}, u32[]{:S(2)}, u32[]{:S(2)}) collective-permute-start(bf16[1,4,1024]{2,1,0:T(4,128)(2,1)S(1)} %shard_map.66.after_ref.refs_0_), channel_id=1, source_target_pairs={{0,2},{1,3},{2,0},{3,1},{4,6},{5,7},{6,4},{7,5},{8,10},{9,11},{10,... | collective-permute-start | bytes 24584 | tf_op jit(solution)/shard_map/ppermute | solution.py:45
  14.5 2.9 %collective-permute-start.4 = (bf16[1,4,1024]{2,1,0:T(4,128)(2,1)S(1)}, bf16[1,4,1024]{2,1,0:T(4,128)(2,1)S(1)}, u32[]{:S(2)}, u32[]{:S(2)}) collective-permute-start(bf16[1,4,1024]{2,1,0:T(4,128)(2,1)S(1)} %shard_map.66.after_ref.refs_0_), channel_id=1, source_target_pairs={{0,1},{1,0},{2,3},{3,2},{4,5},{5,4},{6,7},{7,6},{8,9},{9,8},{10,11... | collective-permute-start | bytes 24584 | tf_op jit(solution)/shard_map/ppermute | solution.py:45
  14.5 3.1 %collective-permute-start.3 = (bf16[1,4,1024]{2,1,0:T(4,128)(2,1)S(1)}, bf16[1,4,1024]{2,1,0:T(4,128)(2,1)S(1)}, u32[]{:S(2)}, u32[]{:S(2)}) collective-permute-start(bf16[1,4,1024]{2,1,0:T(4,128)(2,1)S(1)} %shard_map.66.after_ref.refs_0_), channel_id=1, source_target_pairs={{0,3},{1,2},{2,1},{3,0},{4,7},{5,6},{6,5},{7,4},{8,11},{9,10},{10,... | collective-permute-start | bytes 24584 | tf_op jit(solution)/shard_map/ppermute | solution.py:45
  21.6 5.7 %collective-permute-start.8 = (f32[4,2048]{1,0:T(4,128)S(1)}, f32[4,2048]{1,0:T(4,128)S(1)}, u32[]{:S(2)}, u32[]{:S(2)}) collective-permute-start(f32[4,2048]{1,0:T(4,128)S(1)} %shard_map.68.refs_0_), channel_id=1, source_target_pairs={{0,8},{4,12},{8,0},{12,4},{1,9},{5,13},{9,1},{13,5},{2,10},{6,14},... | collective-permute-start | bytes 98312 | tf_op jit(solution)/shard_map/ppermute | solution.py:45
  23.3 5.7 %collective-permute-start.7 = (f32[4,2048]{1,0:T(4,128)S(1)}, f32[4,2048]{1,0:T(4,128)S(1)}, u32[]{:S(2)}, u32[]{:S(2)}) collective-permute-start(f32[4,2048]{1,0:T(4,128)S(1)} %shard_map.68.refs_0_), channel_id=1, source_target_pairs={{0,12},{4,8},{8,4},{12,0},{1,13},{5,9},{9,5},{13,1},{2,14},{6,10},... | collective-permute-start | bytes 98312 | tf_op jit(solution)/shard_map/ppermute | solution.py:45
  24.7 4.4 %collective-permute-start.6 = (f32[4,2048]{1,0:T(4,128)S(1)}, f32[4,2048]{1,0:T(4,128)S(1)}, u32[]{:S(2)}, u32[]{:S(2)}) collective-permute-start(f32[4,2048]{1,0:T(4,128)S(1)} %shard_map.68.refs_0_), channel_id=1, source_target_pairs={{0,4},{4,0},{8,12},{12,8},{1,5},{5,1},{9,13},{13,9},{2,6},{6,2},{1... | collective-permute-start | bytes 98312 | tf_op jit(solution)/shard_map/ppermute | solution.py:45
  29.2 4.4 %collective-permute-start.10 = (f32[2,2176]{1,0:T(2,128)S(1)}, f32[2,2176]{1,0:T(2,128)S(1)}, u32[]{:S(2)}, u32[]{:S(2)}) collective-permute-start(f32[2,2176]{1,0:T(2,128)S(1)} %get-tuple-element.24), channel_id=1, source_target_pairs={{0,1},{1,0},{2,3},{3,2},{4,5},{5,4},{6,7},{7,6},{8,9},{9,8},{10,11... | collective-permute-start | bytes 52232 | tf_op jit(solution)/shard_map/ppermute | solution.py:45
  29.2 3.6 %collective-permute-start.9 = (f32[2,128]{1,0:T(2,128)S(1)}, f32[2,128]{1,0:T(2,128)S(1)}, u32[]{:S(2)}, u32[]{:S(2)}) collective-permute-start(f32[2,128]{1,0:T(2,128)S(1)} %get-tuple-element.22), channel_id=1, source_target_pairs={{0,2},{1,3},{2,0},{3,1},{4,6},{5,7},{6,4},{7,5},{8,10},{9,11},{10,... | collective-permute-start | bytes 3080 | tf_op jit(solution)/shard_map/ppermute | solution.py:45
  30.5 3.0 %collective-permute-start.11 = (f32[2,128]{1,0:T(2,128)S(1)}, f32[2,128]{1,0:T(2,128)S(1)}, u32[]{:S(2)}, u32[]{:S(2)}) collective-permute-start(f32[2,128]{1,0:T(2,128)S(1)} %get-tuple-element.25), channel_id=1, source_target_pairs={{0,3},{1,2},{2,1},{3,0},{4,7},{5,6},{6,5},{7,4},{8,11},{9,10},{10,... | collective-permute-start | bytes 3080 | tf_op jit(solution)/shard_map/ppermute | solution.py:45

commit v5 on v4

--- a/solution.py
+++ b/solution.py
@@ -9,7 +9,7 @@
 from jax.sharding import PartitionSpec as P
 
 MIB = 1 << 20
-SHARES = (1, 3, 2, 2)
+SHARES = (1, 3, 3, 1)
 VMEM = pl.BlockSpec(memory_space=pltpu.VMEM)
 HBM = pl.BlockSpec(memory_space=pltpu.HBM)
 

time: 34.5 us -> 34.2 us (level)
    pallas_call x1, Pallas kernels: 4.01 us -> 3.2 us  [project(): pl.pallas_call(functools.partial(project_body, len(sources)), out_shape=j...]
    pallas_call x2, Pallas kernels: 4.99 us -> 5.58 us  [load(): pl.pallas_call(functools.partial(load_body, number), out_shape=pltpu.VMEM...]
  transfers between devices with their start and end apart: 12 -> 12, of which waited for: 6 -> 5; matrix products, arithmetic and copies ran while one was open for 0% -> 0% of each run, Pallas kernels for 15% -> 16%
where the time goes in v5:
time: 34.2 us; the launch traced here: 34 us
  starting transfers between devices  13.3 us (39%)
  Pallas kernels  12.2 us (36%)
  waiting for transfers between devices  7.77 us (23%)
  between operations  0.73 us (2%)
    ppermute x12, starting transfers between devices, swap(): return lax.ppermute(value, tuple(axes) if len(axes) > 1 else axes[0], pairs)  13.3 us
    ppermute x12, waiting for transfers between devices, swap(): return lax.ppermute(value, tuple(axes) if len(axes) > 1 else axes[0], pairs)  7.77 us
    pallas_call x2, Pallas kernels, load(): pl.pallas_call(functools.partial(load_body, number), out_shape=pltpu.VMEM...  5.58 us
    pallas_call x1, Pallas kernels, project(): pl.pallas_call(functools.partial(project_body, len(sources)), out_shape=j...  3.2 us
    pallas_call x1, Pallas kernels, gradient(): pl.pallas_call(functools.partial(gradient_body, chunks, counts), out_shap...  2.58 us
    pallas_call x1, Pallas kernels, scale(): pl.pallas_call(functools.partial(scale_body, len(near), len(rows), column...  0.71 us
  transfers between devices with their start and end apart: 12, of which 5 were waited for; matrix products, arithmetic and copies ran while one was open for 0% of the time, Pallas kernels for 16%

profile of v5, /device:TPU:0, one launch (start us, length us, event | category | flops | bytes accessed | tf_op | source)
XLA Modules:
  0.0 34.0 jit_solution(7861762265909581961)
XLA Ops:
  0.7 2.6 %shard_map.64 = (f32[1,4,1024]{2,1,0:T(4,128)S(1)}, f32[1,4,1024]{2,1,0:T(4,128)S(1)}, f32[1,4,1024]{2,1,0:T(4,128)S(1)}, f32[1,4,1024]{2,1,0:T(4,128)S(1)}, s32...) custom-call(bf16[1,128,8192]{2,1,0:T(8,128)(2,1)} %hidden_hbm.1, bf16[16,8192]{1,0:T(8,128)(2,1)} %bitcast.1, ...), custom_call_target="tpu_custom_call" | custom-call | tf_op jit(solution)/shard_map/pallas_call | solution.py:149
  3.2 4.1 %collective-permute-start = (f32[1,4,1024]{2,1,0:T(4,128)S(1)}, f32[1,4,1024]{2,1,0:T(4,128)S(1)}, u32[]{:S(2)}, u32[]{:S(2)}) collective-permute-start(f32[1,4,1024]{2,1,0:T(4,128)S(1)} %get-tuple-element.18), channel_id=1, source_target_pairs={{0,8},{4,12},{8,0},{12,4},{1,9},{5,13},{9,1},{13,5},{2,10},{6,14},... | collective-permute-start | bytes 49160 | tf_op jit(solution)/shard_map/ppermute | solution.py:45
  7.4 1.3 %collective-permute-start.1 = (f32[1,4,1024]{2,1,0:T(4,128)S(1)}, f32[1,4,1024]{2,1,0:T(4,128)S(1)}, u32[]{:S(2)}, u32[]{:S(2)}) collective-permute-start(f32[1,4,1024]{2,1,0:T(4,128)S(1)} %get-tuple-element.19), channel_id=1, source_target_pairs={{0,12},{4,8},{8,4},{12,0},{1,13},{5,9},{9,5},{13,1},{2,14},{6,10},... | collective-permute-start | bytes 49160 | tf_op jit(solution)/shard_map/ppermute | solution.py:45
  8.7 0.2 collective-permute-start.2
  8.9 2.8 %shard_map.65.refs_4_.refs_5_ = bf16[1536,2048]{1,0:T(8,128)(2,1)S(1)} custom-call(s32[4,128]{1,0:T(4,128)S(1)} %get-tuple-element.16.after_ref.ranks_ref, bf16[4096,4096]{1,0:T(8,128)(2,1)} %projection_hbm.7), custom_call_target="tpu_custom_call" | custom-call | tf_op jit(solution)/shard_map/pallas_call | solution.py:84
  11.8 0.0 collective-permute-done.refs_1_
  11.8 1.1 %collective-permute-done.1.refs_2_ = f32[1,4,1024]{2,1,0:T(4,128)S(1)} collective-permute-done((f32[1,4,1024]{2,1,0:T(4,128)S(1)}, f32[1,4,1024]{2,1,0:T(4,128)S(1)}, u32[]{:S(2)}, u32[]{:S(2)}) %collective-permute-start.1) | collective-permute-done | bytes 16416 | tf_op jit(solution)/shard_map/ppermute | solution.py:45
  12.9 0.0 collective-permute-done.2.refs_3_
  12.9 1.6 %collective-permute-start.5 = (bf16[1,4,1024]{2,1,0:T(4,128)(2,1)S(1)}, bf16[1,4,1024]{2,1,0:T(4,128)(2,1)S(1)}, u32[]{:S(2)}, u32[]{:S(2)}) collective-permute-start(bf16[1,4,1024]{2,1,0:T(4,128)(2,1)S(1)} %shard_map.66.after_ref.refs_0_), channel_id=1, source_target_pairs={{0,2},{1,3},{2,0},{3,1},{4,6},{5,7},{6,4},{7,5},{8,10},{9,11},{10,... | collective-permute-start | bytes 24584 | tf_op jit(solution)/shard_map/ppermute | solution.py:45
  14.5 0.0 collective-permute-start.4
  14.5 0.6 %collective-permute-start.3 = (bf16[1,4,1024]{2,1,0:T(4,128)(2,1)S(1)}, bf16[1,4,1024]{2,1,0:T(4,128)(2,1)S(1)}, u32[]{:S(2)}, u32[]{:S(2)}) collective-permute-start(bf16[1,4,1024]{2,1,0:T(4,128)(2,1)S(1)} %shard_map.66.after_ref.refs_0_), channel_id=1, source_target_pairs={{0,3},{1,2},{2,1},{3,0},{4,7},{5,6},{6,5},{7,4},{8,11},{9,10},{10,... | collective-permute-start | bytes 24584 | tf_op jit(solution)/shard_map/ppermute | solution.py:45
  15.1 2.8 %shard_map.67.refs_6_ = bf16[1536,2048]{1,0:T(8,128)(2,1)S(1)} custom-call(bf16[1,4,1024]{2,1,0:T(4,128)(2,1)S(1)} %shard_map.66.after_ref.refs_0_, bf16[4096,4096]{1,0:T(8,128)(2,1)} %projection_hbm.7), custom_call_target="tpu_custom_call" | custom-call | tf_op jit(solution)/shard_map/pallas_call | solution.py:84
  18.0 3.2 %shard_map.68.refs_0_ = f32[4,2048]{1,0:T(4,128)S(1)} custom-call(s32[4,128]{1,0:T(4,128)S(1)} %get-tuple-element.16.after_ref.ranks_ref, bf16[4096,4096]{1,0:T(8,128)(2,1)} %projection_hbm.7, bf16[1,4,1024]{2,1,0:T(4,128)(2,1)S(1)} %shard_map.66.after_ref.refs_0_, bf16[1,4,1024]{2,1,0:T(4,128)(2,1)S(1)} %collective-permute-done.3.refs_1_, ...), custom_call_target="tpu_custom_call" | custom-call | tf_op jit(solution)/shard_map/pallas_call | solution.py:216
  21.2 1.7 %collective-permute-start.8 = (f32[4,2048]{1,0:T(4,128)S(1)}, f32[4,2048]{1,0:T(4,128)S(1)}, u32[]{:S(2)}, u32[]{:S(2)}) collective-permute-start(f32[4,2048]{1,0:T(4,128)S(1)} %shard_map.68.refs_0_), channel_id=1, source_target_pairs={{0,8},{4,12},{8,0},{12,4},{1,9},{5,13},{9,1},{13,5},{2,10},{6,14},... | collective-permute-start | bytes 98312 | tf_op jit(solution)/shard_map/ppermute | solution.py:45
  22.9 1.3 %collective-permute-start.7 = (f32[4,2048]{1,0:T(4,128)S(1)}, f32[4,2048]{1,0:T(4,128)S(1)}, u32[]{:S(2)}, u32[]{:S(2)}) collective-permute-start(f32[4,2048]{1,0:T(4,128)S(1)} %shard_map.68.refs_0_), channel_id=1, source_target_pairs={{0,12},{4,8},{8,4},{12,0},{1,13},{5,9},{9,5},{13,1},{2,14},{6,10},... | collective-permute-start | bytes 98312 | tf_op jit(solution)/shard_map/ppermute | solution.py:45
  24.3 0.5 %collective-permute-start.6 = (f32[4,2048]{1,0:T(4,128)S(1)}, f32[4,2048]{1,0:T(4,128)S(1)}, u32[]{:S(2)}, u32[]{:S(2)}) collective-permute-start(f32[4,2048]{1,0:T(4,128)S(1)} %shard_map.68.refs_0_), channel_id=1, source_target_pairs={{0,4},{4,0},{8,12},{12,8},{1,5},{5,1},{9,13},{13,9},{2,6},{6,2},{1... | collective-permute-start | bytes 98312 | tf_op jit(solution)/shard_map/ppermute | solution.py:45
  24.7 2.1 %collective-permute-done.8.refs_3_ = f32[4,2048]{1,0:T(4,128)S(1)} collective-permute-done((f32[4,2048]{1,0:T(4,128)S(1)}, f32[4,2048]{1,0:T(4,128)S(1)}, u32[]{:S(2)}, u32[]{:S(2)}) %collective-permute-start.8) | collective-permute-done | bytes 32800 | tf_op jit(solution)/shard_map/ppermute | solution.py:45
  26.8 1.8 %collective-permute-done.7.refs_2_ = f32[4,2048]{1,0:T(4,128)S(1)} collective-permute-done((f32[4,2048]{1,0:T(4,128)S(1)}, f32[4,2048]{1,0:T(4,128)S(1)}, u32[]{:S(2)}, u32[]{:S(2)}) %collective-permute-start.7) | collective-permute-done | bytes 32800 | tf_op jit(solution)/shard_map/ppermute | solution.py:45
  28.6 0.1 shard_map.69
  28.8 1.6 %collective-permute-start.9 = (f32[2,128]{1,0:T(2,128)S(1)}, f32[2,128]{1,0:T(2,128)S(1)}, u32[]{:S(2)}, u32[]{:S(2)}) collective-permute-start(f32[2,128]{1,0:T(2,128)S(1)} %get-tuple-element.22), channel_id=1, source_target_pairs={{0,2},{1,3},{2,0},{3,1},{4,6},{5,7},{6,4},{7,5},{8,10},{9,11},{10,... | collective-permute-start | bytes 3080 | tf_op jit(solution)/shard_map/ppermute | solution.py:45
  30.3 0.3 collective-permute-start.11
  30.6 1.8 %collective-permute-done.9.refs_0_ = f32[2,128]{1,0:T(2,128)S(1)} collective-permute-done((f32[2,128]{1,0:T(2,128)S(1)}, f32[2,128]{1,0:T(2,128)S(1)}, u32[]{:S(2)}, u32[]{:S(2)}) %collective-permute-start.9) | collective-permute-done | bytes 1056 | tf_op jit(solution)/shard_map/ppermute | solution.py:45
  32.4 0.9 %collective-permute-done.11.refs_3_ = f32[2,128]{1,0:T(2,128)S(1)} collective-permute-done((f32[2,128]{1,0:T(2,128)S(1)}, f32[2,128]{1,0:T(2,128)S(1)}, u32[]{:S(2)}, u32[]{:S(2)}) %collective-permute-start.11) | collective-permute-done | bytes 1056 | tf_op jit(solution)/shard_map/ppermute | solution.py:45
  33.3 0.7 %shard_map.70 = f32[2,4096]{1,0:T(2,128)} custom-call(f32[2,128]{1,0:T(2,128)S(1)} %collective-permute-done.9.refs_0_, f32[2,2048]{1,0:T(2,128)S(1)} %get-tuple-element.23.refs_1_, f32[2,2176]{1,0:T(2,128)S(1)} %collective-permute-done.10.refs_2_, f32[2,128]{1,0:T(2,128)S(1)} %collective-permute-done.11.refs_3_, f32[2,128]{1,0:T(2,128)S(1)} %get-tuple-element.26.refs_4_), custom_call_target="tpu_custom_call" | custom-call | tf_op jit(solution)/shard_map/pallas_call | solution.py:282
  (7 shorter events, 0.0 us)
Async XLA Ops:
  3.2 8.5 %collective-permute-start = (f32[1,4,1024]{2,1,0:T(4,128)S(1)}, f32[1,4,1024]{2,1,0:T(4,128)S(1)}, u32[]{:S(2)}, u32[]{:S(2)}) collective-permute-start(f32[1,4,1024]{2,1,0:T(4,128)S(1)} %get-tuple-element.18), channel_id=1, source_target_pairs={{0,8},{4,12},{8,0},{12,4},{1,9},{5,13},{9,1},{13,5},{2,10},{6,14},... | collective-permute-start | bytes 49160 | tf_op jit(solution)/shard_map/ppermute | solution.py:45
  7.4 5.5 %collective-permute-start.1 = (f32[1,4,1024]{2,1,0:T(4,128)S(1)}, f32[1,4,1024]{2,1,0:T(4,128)S(1)}, u32[]{:S(2)}, u32[]{:S(2)}) collective-permute-start(f32[1,4,1024]{2,1,0:T(4,128)S(1)} %get-tuple-element.19), channel_id=1, source_target_pairs={{0,12},{4,8},{8,4},{12,0},{1,13},{5,9},{9,5},{13,1},{2,14},{6,10},... | collective-permute-start | bytes 49160 | tf_op jit(solution)/shard_map/ppermute | solution.py:45
  8.7 4.2 %collective-permute-start.2 = (f32[1,4,1024]{2,1,0:T(4,128)S(1)}, f32[1,4,1024]{2,1,0:T(4,128)S(1)}, u32[]{:S(2)}, u32[]{:S(2)}) collective-permute-start(f32[1,4,1024]{2,1,0:T(4,128)S(1)} %get-tuple-element.20), channel_id=1, source_target_pairs={{0,4},{4,0},{8,12},{12,8},{1,5},{5,1},{9,13},{13,9},{2,6},{6,2},{1... | collective-permute-start | bytes 49160 | tf_op jit(solution)/shard_map/ppermute | solution.py:45
  12.9 5.0 %collective-permute-start.5 = (bf16[1,4,1024]{2,1,0:T(4,128)(2,1)S(1)}, bf16[1,4,1024]{2,1,0:T(4,128)(2,1)S(1)}, u32[]{:S(2)}, u32[]{:S(2)}) collective-permute-start(bf16[1,4,1024]{2,1,0:T(4,128)(2,1)S(1)} %shard_map.66.after_ref.refs_0_), channel_id=1, source_target_pairs={{0,2},{1,3},{2,0},{3,1},{4,6},{5,7},{6,4},{7,5},{8,10},{9,11},{10,... | collective-permute-start | bytes 24584 | tf_op jit(solution)/shard_map/ppermute | solution.py:45
  14.5 3.5 %collective-permute-start.4 = (bf16[1,4,1024]{2,1,0:T(4,128)(2,1)S(1)}, bf16[1,4,1024]{2,1,0:T(4,128)(2,1)S(1)}, u32[]{:S(2)}, u32[]{:S(2)}) collective-permute-start(bf16[1,4,1024]{2,1,0:T(4,128)(2,1)S(1)} %shard_map.66.after_ref.refs_0_), channel_id=1, source_target_pairs={{0,1},{1,0},{2,3},{3,2},{4,5},{5,4},{6,7},{7,6},{8,9},{9,8},{10,11... | collective-permute-start | bytes 24584 | tf_op jit(solution)/shard_map/ppermute | solution.py:45
  14.5 3.5 %collective-permute-start.3 = (bf16[1,4,1024]{2,1,0:T(4,128)(2,1)S(1)}, bf16[1,4,1024]{2,1,0:T(4,128)(2,1)S(1)}, u32[]{:S(2)}, u32[]{:S(2)}) collective-permute-start(bf16[1,4,1024]{2,1,0:T(4,128)(2,1)S(1)} %shard_map.66.after_ref.refs_0_), channel_id=1, source_target_pairs={{0,3},{1,2},{2,1},{3,0},{4,7},{5,6},{6,5},{7,4},{8,11},{9,10},{10,... | collective-permute-start | bytes 24584 | tf_op jit(solution)/shard_map/ppermute | solution.py:45
  21.2 5.7 %collective-permute-start.8 = (f32[4,2048]{1,0:T(4,128)S(1)}, f32[4,2048]{1,0:T(4,128)S(1)}, u32[]{:S(2)}, u32[]{:S(2)}) collective-permute-start(f32[4,2048]{1,0:T(4,128)S(1)} %shard_map.68.refs_0_), channel_id=1, source_target_pairs={{0,8},{4,12},{8,0},{12,4},{1,9},{5,13},{9,1},{13,5},{2,10},{6,14},... | collective-permute-start | bytes 98312 | tf_op jit(solution)/shard_map/ppermute | solution.py:45
  22.9 5.7 %collective-permute-start.7 = (f32[4,2048]{1,0:T(4,128)S(1)}, f32[4,2048]{1,0:T(4,128)S(1)}, u32[]{:S(2)}, u32[]{:S(2)}) collective-permute-start(f32[4,2048]{1,0:T(4,128)S(1)} %shard_map.68.refs_0_), channel_id=1, source_target_pairs={{0,12},{4,8},{8,4},{12,0},{1,13},{5,9},{9,5},{13,1},{2,14},{6,10},... | collective-permute-start | bytes 98312 | tf_op jit(solution)/shard_map/ppermute | solution.py:45
  24.3 4.4 %collective-permute-start.6 = (f32[4,2048]{1,0:T(4,128)S(1)}, f32[4,2048]{1,0:T(4,128)S(1)}, u32[]{:S(2)}, u32[]{:S(2)}) collective-permute-start(f32[4,2048]{1,0:T(4,128)S(1)} %shard_map.68.refs_0_), channel_id=1, source_target_pairs={{0,4},{4,0},{8,12},{12,8},{1,5},{5,1},{9,13},{13,9},{2,6},{6,2},{1... | collective-permute-start | bytes 98312 | tf_op jit(solution)/shard_map/ppermute | solution.py:45
  28.7 4.6 %collective-permute-start.10 = (f32[2,2176]{1,0:T(2,128)S(1)}, f32[2,2176]{1,0:T(2,128)S(1)}, u32[]{:S(2)}, u32[]{:S(2)}) collective-permute-start(f32[2,2176]{1,0:T(2,128)S(1)} %get-tuple-element.24), channel_id=1, source_target_pairs={{0,1},{1,0},{2,3},{3,2},{4,5},{5,4},{6,7},{7,6},{8,9},{9,8},{10,11... | collective-permute-start | bytes 52232 | tf_op jit(solution)/shard_map/ppermute | solution.py:45
  28.8 3.6 %collective-permute-start.9 = (f32[2,128]{1,0:T(2,128)S(1)}, f32[2,128]{1,0:T(2,128)S(1)}, u32[]{:S(2)}, u32[]{:S(2)}) collective-permute-start(f32[2,128]{1,0:T(2,128)S(1)} %get-tuple-element.22), channel_id=1, source_target_pairs={{0,2},{1,3},{2,0},{3,1},{4,6},{5,7},{6,4},{7,5},{8,10},{9,11},{10,... | collective-permute-start | bytes 3080 | tf_op jit(solution)/shard_map/ppermute | solution.py:45
  30.3 3.0 %collective-permute-start.11 = (f32[2,128]{1,0:T(2,128)S(1)}, f32[2,128]{1,0:T(2,128)S(1)}, u32[]{:S(2)}, u32[]{:S(2)}) collective-permute-start(f32[2,128]{1,0:T(2,128)S(1)} %get-tuple-element.25), channel_id=1, source_target_pairs={{0,3},{1,2},{2,1},{3,0},{4,7},{5,6},{6,5},{7,4},{8,11},{9,10},{10,... | collective-permute-start | bytes 3080 | tf_op jit(solution)/shard_map/ppermute | solution.py:45

commit v6 on v5

--- a/solution.py
+++ b/solution.py
@@ -298,7 +298,7 @@
     )
     shares = [share, load(projection, 1, ex_count, ranks)]
     grad_rows = sum_rows(
-        [blocks[0]] + [swap(blocks[s], ("ctx",), (s,)) for s in ctx_steps], jnp.bfloat16, shares[1]
+        [blocks[0]] + [swap(blocks[s], ("ctx",), (s,)) for s in reversed(ctx_steps)], jnp.bfloat16, shares[1]
     )
     shares.append(load(projection, 2, ex_count, grad_rows))
     sources = [grad_rows] + [swap(grad_rows, ("feat", "ex"), s) for s in chip_steps]

time: 34.2 us -> 34.6 us (1.012)
  waiting for transfers between devices: 7.77 us -> 8.12 us
    ppermute x12, waiting for transfers between devices: 7.77 us -> 8.12 us  [swap(): return lax.ppermute(value, tuple(axes) if len(axes) > 1 else axes[0], pairs)]
  transfers between devices with their start and end apart: 12 -> 12, of which waited for: 5 -> 7; matrix products, arithmetic and copies ran while one was open for 0% -> 0% of each run, Pallas kernels for 16% -> 16%
where the time goes in v6:
time: 34.6 us; the launch traced here: 34.4 us
  starting transfers between devices  13.3 us (38%)
  Pallas kernels  12.2 us (35%)
  waiting for transfers between devices  8.12 us (23%)
  between operations  0.73 us (2%)
    ppermute x12, starting transfers between devices, swap(): return lax.ppermute(value, tuple(axes) if len(axes) > 1 else axes[0], pairs)  13.3 us
    ppermute x12, waiting for transfers between devices, swap(): return lax.ppermute(value, tuple(axes) if len(axes) > 1 else axes[0], pairs)  8.12 us
    pallas_call x2, Pallas kernels, load(): pl.pallas_call(functools.partial(load_body, number), out_shape=pltpu.VMEM...  5.58 us
    pallas_call x1, Pallas kernels, project(): pl.pallas_call(functools.partial(project_body, len(sources)), out_shape=j...  3.2 us
    pallas_call x1, Pallas kernels, gradient(): pl.pallas_call(functools.partial(gradient_body, chunks, counts), out_shap...  2.58 us
    pallas_call x1, Pallas kernels, scale(): pl.pallas_call(functools.partial(scale_body, len(near), len(rows), column...  0.71 us
  transfers between devices with their start and end apart: 12, of which 7 were waited for; matrix products, arithmetic and copies ran while one was open for 0% of the time, Pallas kernels for 16%

profile of v6, /device:TPU:0, one launch (start us, length us, event | category | flops | bytes accessed | tf_op | source)
XLA Modules:
  0.0 34.4 jit_solution(13645518230025639846)
XLA Ops:
  0.7 2.6 %shard_map.64 = (f32[1,4,1024]{2,1,0:T(4,128)S(1)}, f32[1,4,1024]{2,1,0:T(4,128)S(1)}, f32[1,4,1024]{2,1,0:T(4,128)S(1)}, f32[1,4,1024]{2,1,0:T(4,128)S(1)}, s32...) custom-call(bf16[1,128,8192]{2,1,0:T(8,128)(2,1)} %hidden_hbm.1, bf16[16,8192]{1,0:T(8,128)(2,1)} %bitcast.1, ...), custom_call_target="tpu_custom_call" | custom-call | tf_op jit(solution)/shard_map/pallas_call | solution.py:149
  3.2 3.1 %collective-permute-start = (f32[1,4,1024]{2,1,0:T(4,128)S(1)}, f32[1,4,1024]{2,1,0:T(4,128)S(1)}, u32[]{:S(2)}, u32[]{:S(2)}) collective-permute-start(f32[1,4,1024]{2,1,0:T(4,128)S(1)} %get-tuple-element.18), channel_id=1, source_target_pairs={{0,4},{4,0},{8,12},{12,8},{1,5},{5,1},{9,13},{13,9},{2,6},{6,2},{1... | collective-permute-start | bytes 49160 | tf_op jit(solution)/shard_map/ppermute | solution.py:45
  6.4 2.5 %collective-permute-start.1 = (f32[1,4,1024]{2,1,0:T(4,128)S(1)}, f32[1,4,1024]{2,1,0:T(4,128)S(1)}, u32[]{:S(2)}, u32[]{:S(2)}) collective-permute-start(f32[1,4,1024]{2,1,0:T(4,128)S(1)} %get-tuple-element.19), channel_id=1, source_target_pairs={{0,12},{4,8},{8,4},{12,0},{1,13},{5,9},{9,5},{13,1},{2,14},{6,10},... | collective-permute-start | bytes 49160 | tf_op jit(solution)/shard_map/ppermute | solution.py:45
  8.8 0.1 collective-permute-start.2
  8.9 2.8 %shard_map.65.refs_4_.refs_5_ = bf16[1536,2048]{1,0:T(8,128)(2,1)S(1)} custom-call(s32[4,128]{1,0:T(4,128)S(1)} %get-tuple-element.16.after_ref.ranks_ref, bf16[4096,4096]{1,0:T(8,128)(2,1)} %projection_hbm.7), custom_call_target="tpu_custom_call" | custom-call | tf_op jit(solution)/shard_map/pallas_call | solution.py:84
  11.8 0.4 %collective-permute-done.1.refs_2_ = f32[1,4,1024]{2,1,0:T(4,128)S(1)} collective-permute-done((f32[1,4,1024]{2,1,0:T(4,128)S(1)}, f32[1,4,1024]{2,1,0:T(4,128)S(1)}, u32[]{:S(2)}, u32[]{:S(2)}) %collective-permute-start.1) | collective-permute-done | bytes 16416 | tf_op jit(solution)/shard_map/ppermute | solution.py:45
  12.1 1.4 %collective-permute-done.2.refs_3_ = f32[1,4,1024]{2,1,0:T(4,128)S(1)} collective-permute-done((f32[1,4,1024]{2,1,0:T(4,128)S(1)}, f32[1,4,1024]{2,1,0:T(4,128)S(1)}, u32[]{:S(2)}, u32[]{:S(2)}) %collective-permute-start.2) | collective-permute-done | bytes 16416 | tf_op jit(solution)/shard_map/ppermute | solution.py:45
  13.5 1.6 %collective-permute-start.5 = (bf16[1,4,1024]{2,1,0:T(4,128)(2,1)S(1)}, bf16[1,4,1024]{2,1,0:T(4,128)(2,1)S(1)}, u32[]{:S(2)}, u32[]{:S(2)}) collective-permute-start(bf16[1,4,1024]{2,1,0:T(4,128)(2,1)S(1)} %shard_map.66.after_ref.refs_0_), channel_id=1, source_target_pairs={{0,2},{1,3},{2,0},{3,1},{4,6},{5,7},{6,4},{7,5},{8,10},{9,11},{10,... | collective-permute-start | bytes 24584 | tf_op jit(solution)/shard_map/ppermute | solution.py:45
  15.1 0.6 %collective-permute-start.3 = (bf16[1,4,1024]{2,1,0:T(4,128)(2,1)S(1)}, bf16[1,4,1024]{2,1,0:T(4,128)(2,1)S(1)}, u32[]{:S(2)}, u32[]{:S(2)}) collective-permute-start(bf16[1,4,1024]{2,1,0:T(4,128)(2,1)S(1)} %shard_map.66.after_ref.refs_0_), channel_id=1, source_target_pairs={{0,3},{1,2},{2,1},{3,0},{4,7},{5,6},{6,5},{7,4},{8,11},{9,10},{10,... | collective-permute-start | bytes 24584 | tf_op jit(solution)/shard_map/ppermute | solution.py:45
  15.7 2.8 %shard_map.67.refs_6_ = bf16[1536,2048]{1,0:T(8,128)(2,1)S(1)} custom-call(bf16[1,4,1024]{2,1,0:T(4,128)(2,1)S(1)} %shard_map.66.after_ref.refs_0_, bf16[4096,4096]{1,0:T(8,128)(2,1)} %projection_hbm.7), custom_call_target="tpu_custom_call" | custom-call | tf_op jit(solution)/shard_map/pallas_call | solution.py:84
  18.5 0.0 collective-permute-done.5.refs_3_
  18.5 3.2 %shard_map.68.refs_0_ = f32[4,2048]{1,0:T(4,128)S(1)} custom-call(s32[4,128]{1,0:T(4,128)S(1)} %get-tuple-element.16.after_ref.ranks_ref, bf16[4096,4096]{1,0:T(8,128)(2,1)} %projection_hbm.7, bf16[1,4,1024]{2,1,0:T(4,128)(2,1)S(1)} %shard_map.66.after_ref.refs_0_, bf16[1,4,1024]{2,1,0:T(4,128)(2,1)S(1)} %collective-permute-done.3.refs_1_, ...), custom_call_target="tpu_custom_call" | custom-call | tf_op jit(solution)/shard_map/pallas_call | solution.py:216
  21.7 1.2 %collective-permute-start.8 = (f32[4,2048]{1,0:T(4,128)S(1)}, f32[4,2048]{1,0:T(4,128)S(1)}, u32[]{:S(2)}, u32[]{:S(2)}) collective-permute-start(f32[4,2048]{1,0:T(4,128)S(1)} %shard_map.68.refs_0_), channel_id=1, source_target_pairs={{0,8},{4,12},{8,0},{12,4},{1,9},{5,13},{9,1},{13,5},{2,10},{6,14},... | collective-permute-start | bytes 98312 | tf_op jit(solution)/shard_map/ppermute | solution.py:45
  22.9 2.0 %collective-permute-start.7 = (f32[4,2048]{1,0:T(4,128)S(1)}, f32[4,2048]{1,0:T(4,128)S(1)}, u32[]{:S(2)}, u32[]{:S(2)}) collective-permute-start(f32[4,2048]{1,0:T(4,128)S(1)} %shard_map.68.refs_0_), channel_id=1, source_target_pairs={{0,12},{4,8},{8,4},{12,0},{1,13},{5,9},{9,5},{13,1},{2,14},{6,10},... | collective-permute-start | bytes 98312 | tf_op jit(solution)/shard_map/ppermute | solution.py:45
  24.9 0.4 %collective-permute-start.6 = (f32[4,2048]{1,0:T(4,128)S(1)}, f32[4,2048]{1,0:T(4,128)S(1)}, u32[]{:S(2)}, u32[]{:S(2)}) collective-permute-start(f32[4,2048]{1,0:T(4,128)S(1)} %shard_map.68.refs_0_), channel_id=1, source_target_pairs={{0,4},{4,0},{8,12},{12,8},{1,5},{5,1},{9,13},{13,9},{2,6},{6,2},{1... | collective-permute-start | bytes 98312 | tf_op jit(solution)/shard_map/ppermute | solution.py:45
  25.3 2.3 %collective-permute-done.8.refs_3_ = f32[4,2048]{1,0:T(4,128)S(1)} collective-permute-done((f32[4,2048]{1,0:T(4,128)S(1)}, f32[4,2048]{1,0:T(4,128)S(1)}, u32[]{:S(2)}, u32[]{:S(2)}) %collective-permute-start.8) | collective-permute-done | bytes 32800 | tf_op jit(solution)/shard_map/ppermute | solution.py:45
  27.6 1.1 %collective-permute-done.7.refs_2_ = f32[4,2048]{1,0:T(4,128)S(1)} collective-permute-done((f32[4,2048]{1,0:T(4,128)S(1)}, f32[4,2048]{1,0:T(4,128)S(1)}, u32[]{:S(2)}, u32[]{:S(2)}) %collective-permute-start.7) | collective-permute-done | bytes 32800 | tf_op jit(solution)/shard_map/ppermute | solution.py:45
  28.7 0.3 collective-permute-done.6.refs_1_
  29.0 0.1 shard_map.69
  29.1 1.6 %collective-permute-start.9 = (f32[2,128]{1,0:T(2,128)S(1)}, f32[2,128]{1,0:T(2,128)S(1)}, u32[]{:S(2)}, u32[]{:S(2)}) collective-permute-start(f32[2,128]{1,0:T(2,128)S(1)} %get-tuple-element.22), channel_id=1, source_target_pairs={{0,2},{1,3},{2,0},{3,1},{4,6},{5,7},{6,4},{7,5},{8,10},{9,11},{10,... | collective-permute-start | bytes 3080 | tf_op jit(solution)/shard_map/ppermute | solution.py:45
  30.7 0.3 collective-permute-start.11
  31.0 1.8 %collective-permute-done.9.refs_0_ = f32[2,128]{1,0:T(2,128)S(1)} collective-permute-done((f32[2,128]{1,0:T(2,128)S(1)}, f32[2,128]{1,0:T(2,128)S(1)}, u32[]{:S(2)}, u32[]{:S(2)}) %collective-permute-start.9) | collective-permute-done | bytes 1056 | tf_op jit(solution)/shard_map/ppermute | solution.py:45
  32.7 0.9 %collective-permute-done.11.refs_3_ = f32[2,128]{1,0:T(2,128)S(1)} collective-permute-done((f32[2,128]{1,0:T(2,128)S(1)}, f32[2,128]{1,0:T(2,128)S(1)}, u32[]{:S(2)}, u32[]{:S(2)}) %collective-permute-start.11) | collective-permute-done | bytes 1056 | tf_op jit(solution)/shard_map/ppermute | solution.py:45
  33.7 0.7 %shard_map.70 = f32[2,4096]{1,0:T(2,128)} custom-call(f32[2,128]{1,0:T(2,128)S(1)} %collective-permute-done.9.refs_0_, f32[2,2048]{1,0:T(2,128)S(1)} %get-tuple-element.23.refs_1_, f32[2,2176]{1,0:T(2,128)S(1)} %collective-permute-done.10.refs_2_, f32[2,128]{1,0:T(2,128)S(1)} %collective-permute-done.11.refs_3_, f32[2,128]{1,0:T(2,128)S(1)} %get-tuple-element.26.refs_4_), custom_call_target="tpu_custom_call" | custom-call | tf_op jit(solution)/shard_map/pallas_call | solution.py:282
  (7 shorter events, 0.0 us)
Async XLA Ops:
  3.2 8.5 %collective-permute-start = (f32[1,4,1024]{2,1,0:T(4,128)S(1)}, f32[1,4,1024]{2,1,0:T(4,128)S(1)}, u32[]{:S(2)}, u32[]{:S(2)}) collective-permute-start(f32[1,4,1024]{2,1,0:T(4,128)S(1)} %get-tuple-element.18), channel_id=1, source_target_pairs={{0,4},{4,0},{8,12},{12,8},{1,5},{5,1},{9,13},{13,9},{2,6},{6,2},{1... | collective-permute-start | bytes 49160 | tf_op jit(solution)/shard_map/ppermute | solution.py:45
  6.4 5.8 %collective-permute-start.1 = (f32[1,4,1024]{2,1,0:T(4,128)S(1)}, f32[1,4,1024]{2,1,0:T(4,128)S(1)}, u32[]{:S(2)}, u32[]{:S(2)}) collective-permute-start(f32[1,4,1024]{2,1,0:T(4,128)S(1)} %get-tuple-element.19), channel_id=1, source_target_pairs={{0,12},{4,8},{8,4},{12,0},{1,13},{5,9},{9,5},{13,1},{2,14},{6,10},... | collective-permute-start | bytes 49160 | tf_op jit(solution)/shard_map/ppermute | solution.py:45
  8.8 4.6 %collective-permute-start.2 = (f32[1,4,1024]{2,1,0:T(4,128)S(1)}, f32[1,4,1024]{2,1,0:T(4,128)S(1)}, u32[]{:S(2)}, u32[]{:S(2)}) collective-permute-start(f32[1,4,1024]{2,1,0:T(4,128)S(1)} %get-tuple-element.20), channel_id=1, source_target_pairs={{0,8},{4,12},{8,0},{12,4},{1,9},{5,13},{9,1},{13,5},{2,10},{6,14},... | collective-permute-start | bytes 49160 | tf_op jit(solution)/shard_map/ppermute | solution.py:45
  13.5 5.0 %collective-permute-start.5 = (bf16[1,4,1024]{2,1,0:T(4,128)(2,1)S(1)}, bf16[1,4,1024]{2,1,0:T(4,128)(2,1)S(1)}, u32[]{:S(2)}, u32[]{:S(2)}) collective-permute-start(bf16[1,4,1024]{2,1,0:T(4,128)(2,1)S(1)} %shard_map.66.after_ref.refs_0_), channel_id=1, source_target_pairs={{0,2},{1,3},{2,0},{3,1},{4,6},{5,7},{6,4},{7,5},{8,10},{9,11},{10,... | collective-permute-start | bytes 24584 | tf_op jit(solution)/shard_map/ppermute | solution.py:45
  15.1 3.5 %collective-permute-start.4 = (bf16[1,4,1024]{2,1,0:T(4,128)(2,1)S(1)}, bf16[1,4,1024]{2,1,0:T(4,128)(2,1)S(1)}, u32[]{:S(2)}, u32[]{:S(2)}) collective-permute-start(bf16[1,4,1024]{2,1,0:T(4,128)(2,1)S(1)} %shard_map.66.after_ref.refs_0_), channel_id=1, source_target_pairs={{0,1},{1,0},{2,3},{3,2},{4,5},{5,4},{6,7},{7,6},{8,9},{9,8},{10,11... | collective-permute-start | bytes 24584 | tf_op jit(solution)/shard_map/ppermute | solution.py:45
  15.1 3.5 %collective-permute-start.3 = (bf16[1,4,1024]{2,1,0:T(4,128)(2,1)S(1)}, bf16[1,4,1024]{2,1,0:T(4,128)(2,1)S(1)}, u32[]{:S(2)}, u32[]{:S(2)}) collective-permute-start(bf16[1,4,1024]{2,1,0:T(4,128)(2,1)S(1)} %shard_map.66.after_ref.refs_0_), channel_id=1, source_target_pairs={{0,3},{1,2},{2,1},{3,0},{4,7},{5,6},{6,5},{7,4},{8,11},{9,10},{10,... | collective-permute-start | bytes 24584 | tf_op jit(solution)/shard_map/ppermute | solution.py:45
  21.7 5.8 %collective-permute-start.8 = (f32[4,2048]{1,0:T(4,128)S(1)}, f32[4,2048]{1,0:T(4,128)S(1)}, u32[]{:S(2)}, u32[]{:S(2)}) collective-permute-start(f32[4,2048]{1,0:T(4,128)S(1)} %shard_map.68.refs_0_), channel_id=1, source_target_pairs={{0,8},{4,12},{8,0},{12,4},{1,9},{5,13},{9,1},{13,5},{2,10},{6,14},... | collective-permute-start | bytes 98312 | tf_op jit(solution)/shard_map/ppermute | solution.py:45
  22.9 5.7 %collective-permute-start.7 = (f32[4,2048]{1,0:T(4,128)S(1)}, f32[4,2048]{1,0:T(4,128)S(1)}, u32[]{:S(2)}, u32[]{:S(2)}) collective-permute-start(f32[4,2048]{1,0:T(4,128)S(1)} %shard_map.68.refs_0_), channel_id=1, source_target_pairs={{0,12},{4,8},{8,4},{12,0},{1,13},{5,9},{9,5},{13,1},{2,14},{6,10},... | collective-permute-start | bytes 98312 | tf_op jit(solution)/shard_map/ppermute | solution.py:45
  24.9 4.1 %collective-permute-start.6 = (f32[4,2048]{1,0:T(4,128)S(1)}, f32[4,2048]{1,0:T(4,128)S(1)}, u32[]{:S(2)}, u32[]{:S(2)}) collective-permute-start(f32[4,2048]{1,0:T(4,128)S(1)} %shard_map.68.refs_0_), channel_id=1, source_target_pairs={{0,4},{4,0},{8,12},{12,8},{1,5},{5,1},{9,13},{13,9},{2,6},{6,2},{1... | collective-permute-start | bytes 98312 | tf_op jit(solution)/shard_map/ppermute | solution.py:45
  29.1 4.6 %collective-permute-start.10 = (f32[2,2176]{1,0:T(2,128)S(1)}, f32[2,2176]{1,0:T(2,128)S(1)}, u32[]{:S(2)}, u32[]{:S(2)}) collective-permute-start(f32[2,2176]{1,0:T(2,128)S(1)} %get-tuple-element.24), channel_id=1, source_target_pairs={{0,1},{1,0},{2,3},{3,2},{4,5},{5,4},{6,7},{7,6},{8,9},{9,8},{10,11... | collective-permute-start | bytes 52232 | tf_op jit(solution)/shard_map/ppermute | solution.py:45
  29.1 3.6 %collective-permute-start.9 = (f32[2,128]{1,0:T(2,128)S(1)}, f32[2,128]{1,0:T(2,128)S(1)}, u32[]{:S(2)}, u32[]{:S(2)}) collective-permute-start(f32[2,128]{1,0:T(2,128)S(1)} %get-tuple-element.22), channel_id=1, source_target_pairs={{0,2},{1,3},{2,0},{3,1},{4,6},{5,7},{6,4},{7,5},{8,10},{9,11},{10,... | collective-permute-start | bytes 3080 | tf_op jit(solution)/shard_map/ppermute | solution.py:45
  30.7 3.0 %collective-permute-start.11 = (f32[2,128]{1,0:T(2,128)S(1)}, f32[2,128]{1,0:T(2,128)S(1)}, u32[]{:S(2)}, u32[]{:S(2)}) collective-permute-start(f32[2,128]{1,0:T(2,128)S(1)} %get-tuple-element.25), channel_id=1, source_target_pairs={{0,3},{1,2},{2,1},{3,0},{4,7},{5,6},{6,5},{7,4},{8,11},{9,10},{10,... | collective-permute-start | bytes 3080 | tf_op jit(solution)/shard_map/ppermute | solution.py:45

commit v7 on v6

v7 whole, which is shorter than its diff:
```python
import functools
import itertools

import jax
import jax.numpy as jnp
from jax import lax
from jax.experimental import pallas as pl
from jax.experimental.pallas import tpu as pltpu
from jax.sharding import PartitionSpec as P

MIB = 1 << 20
VMEM = pl.BlockSpec(memory_space=pltpu.VMEM)
HBM = pl.BlockSpec(memory_space=pltpu.HBM)


def is_power(count):
    return count & (count - 1) == 0


def place_at(index, count, step, sign=1):
    if is_power(count):
        return index ^ step
    return (index + sign * step + count) % count


def step_to(index, target, count):
    if is_power(count):
        return index ^ target
    return lax.rem(target - index + count, count)


def exchange_steps(feat_count, ex_count):
    steps = itertools.product(range(feat_count), range(ex_count))
    return sorted(steps, key=lambda s: (any(s), not all(s), s))


def swap(value, axes, steps):
    sizes = [lax.axis_size(a) for a in axes]
    flat = lambda place: functools.reduce(lambda total, p: total * p[1] + p[0], zip(place, sizes), 0)
    pairs = [
        (flat(place), flat([place_at(i, n, s) for i, n, s in zip(place, sizes, steps)]))
        for place in itertools.product(*map(range, sizes))
    ]
    return lax.ppermute(value, tuple(axes) if len(axes) > 1 else axes[0], pairs)


def params(mib, **more):
    return pltpu.CompilerParams(vmem_limit_bytes=int(mib * MIB), **more)


def lane_dot(a, b):
    return lax.dot_general(a, b, (((1,), (1,)), ((), ())), preferred_element_type=jnp.float32)


def hbm(value):
    return pltpu.with_memory_space_constraint(value, pltpu.HBM)


def gradient_body(chunks, ctx_count, hidden_hbm, factor_hbm, cotangent_hbm, lengths, *refs):
    outs, (hidden, factor, cotangent, blocks, sems) = refs[:ctx_count], refs[ctx_count:]
    own, tokens, width = hidden.shape
    part = width // chunks
    copies = [pltpu.make_async_copy(factor_hbm, factor, sems.at[0])]
    for k in range(chunks):
        columns = pl.ds(k * part, part)
        copies.append(
            pltpu.make_async_copy(hidden_hbm.at[:, :, columns], hidden.at[:, :, columns], sems.at[1 + k])
        )
    copies.append(pltpu.make_async_copy(cotangent_hbm, cotangent, sems.at[1 + chunks]))
    for copy in copies:
        copy.start()
    copies[0].wait()
    down = [None] * own
    for k in range(chunks):
        copies[1 + k].wait()
        for e in range(own):
            product = lane_dot(factor[:, k * part : (k + 1) * part], hidden[e, :, k * part : (k + 1) * part])
            down[e] = product if k == 0 else down[e] + product
    copies[-1].wait()
    place = lax.axis_index("ctx")
    for e in range(own):
        rows = down[e].astype(jnp.bfloat16)
        position = place * tokens + lax.broadcasted_iota(jnp.int32, rows.shape, 1)
        rows = jnp.where(position < lengths[e], rows.astype(jnp.float32), 0.0).astype(jnp.bfloat16)
        grad = jnp.dot(rows, cotangent[e], preferred_element_type=jnp.float32)
        share = grad.shape[0] // ctx_count
        for c in range(ctx_count):
            blocks[c, e] = grad[c * share : (c + 1) * share]
    for step in range(ctx_count):
        outs[step][...] = blocks[place_at(place, ctx_count, step)]


def gradient(hidden, factor, cotangent, lengths, ctx_count):
    own, tokens, width = hidden.shape
    rank, model = factor.shape[0], cotangent.shape[2]
    shape = (own, rank // ctx_count, model)
    chunks = 2
    return pl.pallas_call(
        functools.partial(gradient_body, chunks, ctx_count),
        out_shape=[jax.ShapeDtypeStruct(shape, jnp.float32)] * ctx_count,
        in_specs=[HBM] * 3 + [pl.BlockSpec(memory_space=pltpu.SMEM)],
        out_specs=[VMEM] * ctx_count,
        scratch_shapes=[
            pltpu.VMEM(hidden.shape, hidden.dtype),
            pltpu.VMEM(factor.shape, factor.dtype),
            pltpu.VMEM(cotangent.shape, cotangent.dtype),
            pltpu.VMEM((ctx_count,) + shape, jnp.float32),
            pltpu.SemaphoreType.DMA((chunks + 2,)),
        ],
        compiler_params=params(4),
    )(*map(hbm, (hidden, factor, cotangent)), lengths)


def sum_body(*refs):
    total = refs[0][...]
    for ref in refs[1:-1]:
        total = total + ref[...]
    refs[-1][...] = total.astype(refs[-1].dtype)


def sum_rows(parts, dtype):
    return pl.pallas_call(
        sum_body,
        out_shape=jax.ShapeDtypeStruct(parts[0].shape, dtype),
        in_specs=[VMEM] * len(parts),
        out_specs=VMEM,
        compiler_params=params(2),
    )(*parts)


def project_body(feat_count, ex_count, order_ref, held_ref, *refs):
    sources, (out, rows_ref) = refs[:-2], refs[-2:]
    count, width = out.shape
    own, share, model = sources[0].shape
    feat, ex = lax.axis_index("feat"), lax.axis_index("ex")
    per_ex = own * feat_count
    order = order_ref[...]
    slot = lax.broadcasted_iota(jnp.int32, order.shape, 1)
    ranks = []
    for steps in exchange_steps(feat_count, ex_count):
        from_feat, from_ex = place_at(feat, feat_count, steps[0], -1), place_at(ex, ex_count, steps[1], -1)
        for e in range(own):
            chosen = slot == (from_feat * ex_count + from_ex) * own + e
            wanted = jnp.sum(jnp.where(chosen, order, 0), axis=1, keepdims=True)
            target = sum((wanted >= j * per_ex).astype(jnp.int32) for j in range(1, ex_count))
            ranks.append(step_to(ex, target, ex_count) * per_ex + wanted - target * per_ex)
    row = lax.broadcasted_iota(jnp.int32, (rows_ref.shape[0], model), 0)
    for r in range(share):
        rows = jnp.zeros(row.shape, jnp.float32)
        for k, source in enumerate(sources):
            for e in range(own):
                values = source[e, r : r + 1].astype(jnp.float32)
                rows = rows + jnp.where(row == ranks[k * own + e], values, 0.0)
        rows_ref[:, r * model : (r + 1) * model] = rows.astype(jnp.bfloat16)
    columns = pl.ds(pl.multiple_of(ex * width, 128), width)
    out[...] = jnp.dot(rows_ref[...], held_ref[:, columns], preferred_element_type=jnp.float32)[:count]


def project(sources, order, held, feat_count, ex_count):
    depth, width = held.shape
    count = len(sources) * sources[0].shape[0]
    padded = max(8, count)
    return pl.pallas_call(
        functools.partial(project_body, feat_count, ex_count),
        out_shape=jax.ShapeDtypeStruct((count, width // ex_count), jnp.float32),
        in_specs=[VMEM] * (len(sources) + 2),
        out_specs=VMEM,
        scratch_shapes=[pltpu.VMEM((padded, depth), jnp.bfloat16)],
        compiler_params=params(2 + 60 / 1024),
    )(order.reshape(1, -1), pltpu.with_memory_space_constraint(held, pltpu.VMEM), *sources)


def total_body(ex_count, *refs):
    parts = refs[: -2 * ex_count - 1]
    near, *others, own_rows, own_squares = refs[-2 * ex_count - 1 :]
    total = parts[0][...]
    for part in parts[1:]:
        total = total + part[...]
    squares = jnp.sum(total * total, axis=1, keepdims=True)
    per_ex, width = own_rows.shape
    own_rows[...] = total[:per_ex]
    for step in range(ex_count):
        rows = slice(step * per_ex, (step + 1) * per_ex)
        spread = jnp.broadcast_to(squares[rows], (per_ex, 128))
        if step == 0:
            near[...] = spread
            own_squares[...] = spread
        else:
            others[2 * step - 2][:, :width] = total[rows]
            others[2 * step - 2][:, width:] = spread
            others[2 * step - 1][...] = spread


def totals(parts, ex_count):
    count, width = parts[0].shape
    per_ex = count // ex_count
    shape = lambda columns: jax.ShapeDtypeStruct((per_ex, columns), jnp.float32)
    near, *others, own_rows, own_squares = pl.pallas_call(
        functools.partial(total_body, ex_count),
        out_shape=[shape(128)] + [shape(width + 128), shape(128)] * (ex_count - 1) + [shape(width), shape(128)],
        in_specs=[VMEM] * len(parts),
        out_specs=[VMEM] * (2 * ex_count + 1),
        compiler_params=params(1),
    )(*parts)
    return [own_rows, *others[::2]], [near, *others[1::2]], own_squares


def scale_body(near_count, ex_count, columns, *refs):
    rows, squares, out = refs[near_count : near_count + ex_count], refs[:near_count] + refs[near_count + ex_count : -1], refs[-1]
    width = rows[0].shape[1]
    total = squares[0][...]
    for square in squares[1:]:
        total = total + square[...]
    for row in rows[1:]:
        total = total + row[:, width:]
    norm = jnp.sqrt(total[:, :1] / columns + 1e-06)
    for step in range(ex_count):
        place = place_at(lax.axis_index("ex"), ex_count, step, -1)
        out[:, pl.ds(pl.multiple_of(place * width, 128), width)] = rows[step][:, :width] / norm


def scale(near, rows, squares, columns):
    per_ex, width = rows[0].shape
    operands = (*near, *rows, *squares)
    return pl.pallas_call(
        functools.partial(scale_body, len(near), len(rows), columns),
        out_shape=jax.ShapeDtypeStruct((per_ex, width * len(rows)), jnp.float32),
        in_specs=[VMEM] * len(operands),
        out_specs=VMEM,
        compiler_params=params(1),
    )(*operands)


def per_device(hidden, cotangent, adapter_down_factor, projection, lengths, slot_example_order):
    ctx_count, feat_count, ex_count = tuple(map(lax.axis_size, ("ctx", "feat", "ex")))
    ctx_steps = sorted(range(1, ctx_count), key=lambda s: (s == 1, s))
    chip_steps = exchange_steps(feat_count, ex_count)[1:]

    blocks = gradient(hidden, adapter_down_factor.T, cotangent, lengths, ctx_count)
    later, first = lax.optimization_barrier((projection, blocks[0]))
    held = lax.ppermute(later, "ex", [(i, i) for i in range(ex_count)])
    grad_rows = sum_rows([first] + [swap(blocks[s], ("ctx",), (s,)) for s in ctx_steps], jnp.bfloat16)
    sources = [grad_rows] + [swap(grad_rows, ("feat", "ex"), s) for s in chip_steps]
    product = project(sources, slot_example_order, held, feat_count, ex_count)
    rows, squares, own_squares = totals([product] + [swap(product, ("ctx",), (s,)) for s in reversed(ctx_steps)], ex_count)
    taken = [rows[0]] + [swap(rows[s], ("ex",), (s,)) for s in range(1, ex_count)]
    near, far = (
        [swap(squares[e], ("feat", "ex"), (f, e)) for f, e in chip_steps if f and bool(e) == both] for both in (False, True)
    )
    return scale(near, taken, [*far, own_squares], projection.shape[1] * feat_count)


def solution(mesh):
    in_specs = (
        P(("group", "feat", "ex"), "ctx", None),
        P(("group", "feat", "ex"), "ctx", None),
        P(),
        P("ctx", "feat"),
        P(("group", "feat", "ex")),
        P("group"),
    )
    out_specs = P(("group", "ex"), "feat")
    return jax.shard_map(
        per_device, mesh=mesh, in_specs=in_specs, out_specs=out_specs, check_vma=False
    )
```

time: 34.6 us -> 42.7 us (1.23)
  starting transfers between devices: 13.3 us -> 23.8 us
  Pallas kernels: 12.2 us -> 5.71 us
  waiting for transfers between devices: 8.12 us -> 11.7 us
  local copies, waits for them, and re-layouts: 0 us -> 0.66 us
    ppermute x0 -> x1, starting transfers between devices: none -> 10.5 us  [per_device(): held = lax.ppermute(later, 'ex', [(i, i) for i in range(ex_count)])]
    pallas_call x4 -> x2, Pallas kernels: 11.4 us -> 4.89 us  [the longest x1 2.55 us: gradient(): pl.pallas_call(functools.partial(gradient_body, chunks, ctx_count), out_s...]
    ppermute x12, waiting for transfers between devices: 8.12 us -> 11.7 us  [swap(): return lax.ppermute(value, tuple(axes) if len(axes) > 1 else axes[0], pairs)]
    unnamed x0 -> x2, local copies, waits for them, and re-layouts: none -> 0.66 us
  transfers between devices with their start and end apart: 12 -> 13, of which waited for: 7 -> 8; matrix products, arithmetic and copies ran while one was open for 0% -> 0% of each run, Pallas kernels for 16% -> 0%
where the time goes in v7:
time: 42.7 us; the launch traced here: 42.5 us
  starting transfers between devices  23.8 us (56%)
  waiting for transfers between devices  11.7 us (27%)
  Pallas kernels  5.71 us (13%)
  between operations  0.68 us (2%)
  local copies, waits for them, and re-layouts  0.66 us (2%)
    ppermute x12, starting transfers between devices, swap(): return lax.ppermute(value, tuple(axes) if len(axes) > 1 else axes[0], pairs)  13.2 us
    ppermute x12, waiting for transfers between devices, swap(): return lax.ppermute(value, tuple(axes) if len(axes) > 1 else axes[0], pairs)  11.7 us
    ppermute x1, starting transfers between devices, per_device(): held = lax.ppermute(later, 'ex', [(i, i) for i in range(ex_count)])  10.5 us
    pallas_call x1, Pallas kernels, gradient(): pl.pallas_call(functools.partial(gradient_body, chunks, ctx_count), out_s...  2.55 us
    pallas_call x1, Pallas kernels, project(): pl.pallas_call(functools.partial(project_body, feat_count, ex_count), out...  2.34 us
  transfers between devices with their start and end apart: 13, of which 8 were waited for; matrix products, arithmetic and copies ran while one was open for 0% of the time, Pallas kernels for 0%

profile of v7, /device:TPU:0, one launch (start us, length us, event | category | flops | bytes accessed | tf_op | source)
XLA Modules:
  0.0 42.5 jit_solution(14969195925645410071)
XLA Ops:
  0.7 2.5 %shard_map.64 = (f32[1,4,1024]{2,1,0:T(4,128)S(1)}, f32[1,4,1024]{2,1,0:T(4,128)S(1)}, f32[1,4,1024]{2,1,0:T(4,128)S(1)}, f32[1,4,1024]{2,1,0:T(4,128)S(1)}) custom-call(bf16[1,128,8192]{2,1,0:T(8,128)(2,1)} %hidden_hbm.1, bf16[16,8192]{1,0:T(8,128)(2,1)} %bitcast.3, bf16[1,128,1024]{2,1,0:T(8,128)(2,1)} %cotangent_hbm.1, s32[1]{0:T(128)S(6)} %copy.7.lengths), custom_call_target="tpu_custom_call" | custom-call | tf_op jit(solution)/shard_map/pallas_call | solution.py:98
  3.2 10.5 %collective-permute-start = (bf16[4096,4096]{1,0:T(8,128)(2,1)}, bf16[4096,4096]{1,0:T(8,128)(2,1)S(1)}, u32[]{:S(2)}, u32[]{:S(2)}) collective-permute-start(bf16[4096,4096]{1,0:T(8,128)(2,1)} %param.9), channel_id=1, source_target_pairs={{0,0},{1,1},{2,2},{3,3},{4,4},{5,5},{6,6},{7,7},{8,8},{9,9},{10,10... | collective-permute-start | bytes 100663304 | tf_op jit(solution)/shard_map/ppermute | solution.py:241
  13.8 4.1 %collective-permute-start.1 = (f32[1,4,1024]{2,1,0:T(4,128)S(1)}, f32[1,4,1024]{2,1,0:T(4,128)S(1)}, u32[]{:S(2)}, u32[]{:S(2)}) collective-permute-start(f32[1,4,1024]{2,1,0:T(4,128)S(1)} %get-tuple-element.19), channel_id=1, source_target_pairs={{0,8},{4,12},{8,0},{12,4},{1,9},{5,13},{9,1},{13,5},{2,10},{6,14},... | collective-permute-start | bytes 49160 | tf_op jit(solution)/shard_map/ppermute | solution.py:44
  17.8 1.3 %collective-permute-start.2 = (f32[1,4,1024]{2,1,0:T(4,128)S(1)}, f32[1,4,1024]{2,1,0:T(4,128)S(1)}, u32[]{:S(2)}, u32[]{:S(2)}) collective-permute-start(f32[1,4,1024]{2,1,0:T(4,128)S(1)} %get-tuple-element.20), channel_id=1, source_target_pairs={{0,12},{4,8},{8,4},{12,0},{1,13},{5,9},{9,5},{13,1},{2,14},{6,10},... | collective-permute-start | bytes 49160 | tf_op jit(solution)/shard_map/ppermute | solution.py:44
  19.2 0.2 collective-permute-start.3
  19.4 0.1 collective-permute-done.1.refs_1_
  19.5 3.8 %collective-permute-done.2.refs_2_ = f32[1,4,1024]{2,1,0:T(4,128)S(1)} collective-permute-done((f32[1,4,1024]{2,1,0:T(4,128)S(1)}, f32[1,4,1024]{2,1,0:T(4,128)S(1)}, u32[]{:S(2)}, u32[]{:S(2)}) %collective-permute-start.2) | collective-permute-done | bytes 16416 | tf_op jit(solution)/shard_map/ppermute | solution.py:44
  23.4 1.6 %collective-permute-start.6 = (bf16[1,4,1024]{2,1,0:T(4,128)(2,1)S(1)}, bf16[1,4,1024]{2,1,0:T(4,128)(2,1)S(1)}, u32[]{:S(2)}, u32[]{:S(2)}) collective-permute-start(bf16[1,4,1024]{2,1,0:T(4,128)(2,1)S(1)} %shard_map.65.refs_0_), channel_id=1, source_target_pairs={{0,2},{1,3},{2,0},{3,1},{4,6},{5,7},{6,4},{7,5},{8,10},{9,11},{10,... | collective-permute-start | bytes 24584 | tf_op jit(solution)/shard_map/ppermute | solution.py:44
  24.9 0.6 %collective-permute-start.4 = (bf16[1,4,1024]{2,1,0:T(4,128)(2,1)S(1)}, bf16[1,4,1024]{2,1,0:T(4,128)(2,1)S(1)}, u32[]{:S(2)}, u32[]{:S(2)}) collective-permute-start(bf16[1,4,1024]{2,1,0:T(4,128)(2,1)S(1)} %shard_map.65.refs_0_), channel_id=1, source_target_pairs={{0,3},{1,2},{2,1},{3,0},{4,7},{5,6},{6,5},{7,4},{8,11},{9,10},{10,... | collective-permute-start | bytes 24584 | tf_op jit(solution)/shard_map/ppermute | solution.py:44
  25.6 1.5 %collective-permute-done.6.refs_3_ = bf16[1,4,1024]{2,1,0:T(4,128)(2,1)S(1)} collective-permute-done((bf16[1,4,1024]{2,1,0:T(4,128)(2,1)S(1)}, bf16[1,4,1024]{2,1,0:T(4,128)(2,1)S(1)}, u32[]{:S(2)}, u32[]{:S(2)}) %collective-permute-start.6) | collective-permute-done | bytes 8224 | tf_op jit(solution)/shard_map/ppermute | solution.py:44
  27.1 0.9 %collective-permute-done.4.refs_1_ = bf16[1,4,1024]{2,1,0:T(4,128)(2,1)S(1)} collective-permute-done((bf16[1,4,1024]{2,1,0:T(4,128)(2,1)S(1)}, bf16[1,4,1024]{2,1,0:T(4,128)(2,1)S(1)}, u32[]{:S(2)}, u32[]{:S(2)}) %collective-permute-start.4) | collective-permute-done | bytes 8224 | tf_op jit(solution)/shard_map/ppermute | solution.py:44
  28.0 0.7 %copy-done = s32[4]{0:T(128)S(1)} copy-done((s32[4]{0:T(128)S(1)}, s32[4]{0:T(128)}, u32[]{:S(2)}) %copy-start) | copy-done | bytes 40
  28.7 2.3 %shard_map.66.refs_0_ = f32[4,2048]{1,0:T(4,128)S(1)} custom-call(s32[1,4]{1,0:T(1,128)S(1)} %bitcast.2, bf16[4096,4096]{1,0:T(8,128)(2,1)S(1)} %collective-permute-done.held_ref, bf16[1,4,1024]{2,1,0:T(4,128)(2,1)S(1)} %shard_map.65.refs_0_, bf16[1,4,1024]{2,1,0:T(4,128)(2,1)S(1)} %collective-permute-done.4.refs_1_, ...), custom_call_target="tpu_custom_call" | custom-call | tf_op jit(solution)/shard_map/pallas_call | solution.py:163
  31.0 1.2 %collective-permute-start.9 = (f32[4,2048]{1,0:T(4,128)S(1)}, f32[4,2048]{1,0:T(4,128)S(1)}, u32[]{:S(2)}, u32[]{:S(2)}) collective-permute-start(f32[4,2048]{1,0:T(4,128)S(1)} %shard_map.66.refs_0_), channel_id=1, source_target_pairs={{0,8},{4,12},{8,0},{12,4},{1,9},{5,13},{9,1},{13,5},{2,10},{6,14},... | collective-permute-start | bytes 98312 | tf_op jit(solution)/shard_map/ppermute | solution.py:44
  32.3 0.9 %collective-permute-start.8 = (f32[4,2048]{1,0:T(4,128)S(1)}, f32[4,2048]{1,0:T(4,128)S(1)}, u32[]{:S(2)}, u32[]{:S(2)}) collective-permute-start(f32[4,2048]{1,0:T(4,128)S(1)} %shard_map.66.refs_0_), channel_id=1, source_target_pairs={{0,12},{4,8},{8,4},{12,0},{1,13},{5,9},{9,5},{13,1},{2,14},{6,10},... | collective-permute-start | bytes 98312 | tf_op jit(solution)/shard_map/ppermute | solution.py:44
  33.2 1.3 %collective-permute-start.7 = (f32[4,2048]{1,0:T(4,128)S(1)}, f32[4,2048]{1,0:T(4,128)S(1)}, u32[]{:S(2)}, u32[]{:S(2)}) collective-permute-start(f32[4,2048]{1,0:T(4,128)S(1)} %shard_map.66.refs_0_), channel_id=1, source_target_pairs={{0,4},{4,0},{8,12},{12,8},{1,5},{5,1},{9,13},{13,9},{2,6},{6,2},{1... | collective-permute-start | bytes 98312 | tf_op jit(solution)/shard_map/ppermute | solution.py:44
  34.5 1.3 %collective-permute-done.9.refs_3_ = f32[4,2048]{1,0:T(4,128)S(1)} collective-permute-done((f32[4,2048]{1,0:T(4,128)S(1)}, f32[4,2048]{1,0:T(4,128)S(1)}, u32[]{:S(2)}, u32[]{:S(2)}) %collective-permute-start.9) | collective-permute-done | bytes 32800 | tf_op jit(solution)/shard_map/ppermute | solution.py:44
  35.8 2.1 %collective-permute-done.8.refs_2_ = f32[4,2048]{1,0:T(4,128)S(1)} collective-permute-done((f32[4,2048]{1,0:T(4,128)S(1)}, f32[4,2048]{1,0:T(4,128)S(1)}, u32[]{:S(2)}, u32[]{:S(2)}) %collective-permute-start.8) | collective-permute-done | bytes 32800 | tf_op jit(solution)/shard_map/ppermute | solution.py:44
  38.0 0.1 shard_map.67
  38.1 0.7 %collective-permute-start.10 = (f32[2,128]{1,0:T(2,128)S(1)}, f32[2,128]{1,0:T(2,128)S(1)}, u32[]{:S(2)}, u32[]{:S(2)}) collective-permute-start(f32[2,128]{1,0:T(2,128)S(1)} %get-tuple-element.22), channel_id=1, source_target_pairs={{0,2},{1,3},{2,0},{3,1},{4,6},{5,7},{6,4},{7,5},{8,10},{9,11},{10,... | collective-permute-start | bytes 3080 | tf_op jit(solution)/shard_map/ppermute | solution.py:44
  38.8 1.2 %collective-permute-start.12 = (f32[2,128]{1,0:T(2,128)S(1)}, f32[2,128]{1,0:T(2,128)S(1)}, u32[]{:S(2)}, u32[]{:S(2)}) collective-permute-start(f32[2,128]{1,0:T(2,128)S(1)} %get-tuple-element.25), channel_id=1, source_target_pairs={{0,3},{1,2},{2,1},{3,0},{4,7},{5,6},{6,5},{7,4},{8,11},{9,10},{10,... | collective-permute-start | bytes 3080 | tf_op jit(solution)/shard_map/ppermute | solution.py:44
  39.9 1.8 %collective-permute-done.10.refs_0_ = f32[2,128]{1,0:T(2,128)S(1)} collective-permute-done((f32[2,128]{1,0:T(2,128)S(1)}, f32[2,128]{1,0:T(2,128)S(1)}, u32[]{:S(2)}, u32[]{:S(2)}) %collective-permute-start.10) | collective-permute-done | bytes 1056 | tf_op jit(solution)/shard_map/ppermute | solution.py:44
  41.7 0.1 collective-permute-done.12.refs_3_
  41.8 0.7 %shard_map.68 = f32[2,4096]{1,0:T(2,128)} custom-call(f32[2,128]{1,0:T(2,128)S(1)} %collective-permute-done.10.refs_0_, f32[2,2048]{1,0:T(2,128)S(1)} %get-tuple-element.23.refs_1_, f32[2,2176]{1,0:T(2,128)S(1)} %collective-permute-done.11.refs_2_, f32[2,128]{1,0:T(2,128)S(1)} %collective-permute-done.12.refs_3_, f32[2,128]{1,0:T(2,128)S(1)} %get-tuple-element.26.refs_4_), custom_call_target="tpu_custom_call" | custom-call | tf_op jit(solution)/shard_map/pallas_call | solution.py:225
  (9 shorter events, 0.0 us)
Async XLA Ops:
  3.2 24.8 %collective-permute-start = (bf16[4096,4096]{1,0:T(8,128)(2,1)}, bf16[4096,4096]{1,0:T(8,128)(2,1)S(1)}, u32[]{:S(2)}, u32[]{:S(2)}) collective-permute-start(bf16[4096,4096]{1,0:T(8,128)(2,1)} %param.9), channel_id=1, source_target_pairs={{0,0},{1,1},{2,2},{3,3},{4,4},{5,5},{6,6},{7,7},{8,8},{9,9},{10,10... | collective-permute-start | bytes 100663304 | tf_op jit(solution)/shard_map/ppermute | solution.py:241
  13.8 5.8 %collective-permute-start.1 = (f32[1,4,1024]{2,1,0:T(4,128)S(1)}, f32[1,4,1024]{2,1,0:T(4,128)S(1)}, u32[]{:S(2)}, u32[]{:S(2)}) collective-permute-start(f32[1,4,1024]{2,1,0:T(4,128)S(1)} %get-tuple-element.19), channel_id=1, source_target_pairs={{0,8},{4,12},{8,0},{12,4},{1,9},{5,13},{9,1},{13,5},{2,10},{6,14},... | collective-permute-start | bytes 49160 | tf_op jit(solution)/shard_map/ppermute | solution.py:44
  17.8 5.5 %collective-permute-start.2 = (f32[1,4,1024]{2,1,0:T(4,128)S(1)}, f32[1,4,1024]{2,1,0:T(4,128)S(1)}, u32[]{:S(2)}, u32[]{:S(2)}) collective-permute-start(f32[1,4,1024]{2,1,0:T(4,128)S(1)} %get-tuple-element.20), channel_id=1, source_target_pairs={{0,12},{4,8},{8,4},{12,0},{1,13},{5,9},{9,5},{13,1},{2,14},{6,10},... | collective-permute-start | bytes 49160 | tf_op jit(solution)/shard_map/ppermute | solution.py:44
  19.2 4.2 %collective-permute-start.3 = (f32[1,4,1024]{2,1,0:T(4,128)S(1)}, f32[1,4,1024]{2,1,0:T(4,128)S(1)}, u32[]{:S(2)}, u32[]{:S(2)}) collective-permute-start(f32[1,4,1024]{2,1,0:T(4,128)S(1)} %get-tuple-element.21), channel_id=1, source_target_pairs={{0,4},{4,0},{8,12},{12,8},{1,5},{5,1},{9,13},{13,9},{2,6},{6,2},{1... | collective-permute-start | bytes 49160 | tf_op jit(solution)/shard_map/ppermute | solution.py:44
  23.4 3.7 %collective-permute-start.6 = (bf16[1,4,1024]{2,1,0:T(4,128)(2,1)S(1)}, bf16[1,4,1024]{2,1,0:T(4,128)(2,1)S(1)}, u32[]{:S(2)}, u32[]{:S(2)}) collective-permute-start(bf16[1,4,1024]{2,1,0:T(4,128)(2,1)S(1)} %shard_map.65.refs_0_), channel_id=1, source_target_pairs={{0,2},{1,3},{2,0},{3,1},{4,6},{5,7},{6,4},{7,5},{8,10},{9,11},{10,... | collective-permute-start | bytes 24584 | tf_op jit(solution)/shard_map/ppermute | solution.py:44
  24.9 2.2 %collective-permute-start.5 = (bf16[1,4,1024]{2,1,0:T(4,128)(2,1)S(1)}, bf16[1,4,1024]{2,1,0:T(4,128)(2,1)S(1)}, u32[]{:S(2)}, u32[]{:S(2)}) collective-permute-start(bf16[1,4,1024]{2,1,0:T(4,128)(2,1)S(1)} %shard_map.65.refs_0_), channel_id=1, source_target_pairs={{0,1},{1,0},{2,3},{3,2},{4,5},{5,4},{6,7},{7,6},{8,9},{9,8},{10,11... | collective-permute-start | bytes 24584 | tf_op jit(solution)/shard_map/ppermute | solution.py:44
  24.9 3.1 %collective-permute-start.4 = (bf16[1,4,1024]{2,1,0:T(4,128)(2,1)S(1)}, bf16[1,4,1024]{2,1,0:T(4,128)(2,1)S(1)}, u32[]{:S(2)}, u32[]{:S(2)}) collective-permute-start(bf16[1,4,1024]{2,1,0:T(4,128)(2,1)S(1)} %shard_map.65.refs_0_), channel_id=1, source_target_pairs={{0,3},{1,2},{2,1},{3,0},{4,7},{5,6},{6,5},{7,4},{8,11},{9,10},{10,... | collective-permute-start | bytes 24584 | tf_op jit(solution)/shard_map/ppermute | solution.py:44
  28.0 0.7 %copy-start = (s32[4]{0:T(128)S(1)}, s32[4]{0:T(128)}, u32[]{:S(2)}) copy-start(s32[4]{0:T(128)} %param.11) | copy-start | bytes 52
  31.0 4.8 %collective-permute-start.9 = (f32[4,2048]{1,0:T(4,128)S(1)}, f32[4,2048]{1,0:T(4,128)S(1)}, u32[]{:S(2)}, u32[]{:S(2)}) collective-permute-start(f32[4,2048]{1,0:T(4,128)S(1)} %shard_map.66.refs_0_), channel_id=1, source_target_pairs={{0,8},{4,12},{8,0},{12,4},{1,9},{5,13},{9,1},{13,5},{2,10},{6,14},... | collective-permute-start | bytes 98312 | tf_op jit(solution)/shard_map/ppermute | solution.py:44
  32.3 5.7 %collective-permute-start.8 = (f32[4,2048]{1,0:T(4,128)S(1)}, f32[4,2048]{1,0:T(4,128)S(1)}, u32[]{:S(2)}, u32[]{:S(2)}) collective-permute-start(f32[4,2048]{1,0:T(4,128)S(1)} %shard_map.66.refs_0_), channel_id=1, source_target_pairs={{0,12},{4,8},{8,4},{12,0},{1,13},{5,9},{9,5},{13,1},{2,14},{6,10},... | collective-permute-start | bytes 98312 | tf_op jit(solution)/shard_map/ppermute | solution.py:44
  33.2 4.8 %collective-permute-start.7 = (f32[4,2048]{1,0:T(4,128)S(1)}, f32[4,2048]{1,0:T(4,128)S(1)}, u32[]{:S(2)}, u32[]{:S(2)}) collective-permute-start(f32[4,2048]{1,0:T(4,128)S(1)} %shard_map.66.refs_0_), channel_id=1, source_target_pairs={{0,4},{4,0},{8,12},{12,8},{1,5},{5,1},{9,13},{13,9},{2,6},{6,2},{1... | collective-permute-start | bytes 98312 | tf_op jit(solution)/shard_map/ppermute | solution.py:44
  38.1 3.7 %collective-permute-start.11 = (f32[2,2176]{1,0:T(2,128)S(1)}, f32[2,2176]{1,0:T(2,128)S(1)}, u32[]{:S(2)}, u32[]{:S(2)}) collective-permute-start(f32[2,2176]{1,0:T(2,128)S(1)} %get-tuple-element.24), channel_id=1, source_target_pairs={{0,1},{1,0},{2,3},{3,2},{4,5},{5,4},{6,7},{7,6},{8,9},{9,8},{10,11... | collective-permute-start | bytes 52232 | tf_op jit(solution)/shard_map/ppermute | solution.py:44
  38.1 3.6 %collective-permute-start.10 = (f32[2,128]{1,0:T(2,128)S(1)}, f32[2,128]{1,0:T(2,128)S(1)}, u32[]{:S(2)}, u32[]{:S(2)}) collective-permute-start(f32[2,128]{1,0:T(2,128)S(1)} %get-tuple-element.22), channel_id=1, source_target_pairs={{0,2},{1,3},{2,0},{3,1},{4,6},{5,7},{6,4},{7,5},{8,10},{9,11},{10,... | collective-permute-start | bytes 3080 | tf_op jit(solution)/shard_map/ppermute | solution.py:44
  38.8 3.0 %collective-permute-start.12 = (f32[2,128]{1,0:T(2,128)S(1)}, f32[2,128]{1,0:T(2,128)S(1)}, u32[]{:S(2)}, u32[]{:S(2)}) collective-permute-start(f32[2,128]{1,0:T(2,128)S(1)} %get-tuple-element.25), channel_id=1, source_target_pairs={{0,3},{1,2},{2,1},{3,0},{4,7},{5,6},{6,5},{7,4},{8,11},{9,10},{10,... | collective-permute-start | bytes 3080 | tf_op jit(solution)/shard_map/ppermute | solution.py:44

commit v8 on v5

--- a/solution.py
+++ b/solution.py
@@ -9,7 +9,7 @@
 from jax.sharding import PartitionSpec as P
 
 MIB = 1 << 20
-SHARES = (1, 3, 3, 1)
+SHARES = (1, 4, 3)
 VMEM = pl.BlockSpec(memory_space=pltpu.VMEM)
 HBM = pl.BlockSpec(memory_space=pltpu.HBM)
 
@@ -185,10 +185,8 @@
     )(*parts, pltpu.with_memory_space_constraint(after, pltpu.VMEM))
 
 
-def project_body(source_count, ranks_ref, projection_hbm, *refs):
-    sources, shares, (out, last_share, rows_ref, sem) = refs[:source_count], refs[source_count:-4], refs[-4:]
-    copy = share_copy(projection_hbm, last_share, sem, len(shares))
-    copy.start()
+def project_body(source_count, ranks_ref, *refs):
+    sources, shares, (out, rows_ref) = refs[:source_count], refs[source_count:-2], refs[-2:]
     padded, count = rows_ref.shape[0], out.shape[0]
     own, share, model = sources[0].shape
     row = lax.broadcasted_iota(jnp.int32, (padded, model), 0)
@@ -200,10 +198,8 @@
                 values = source[e, r : r + 1].astype(jnp.float32)
                 rows = rows + jnp.where(row == ranks[k * own + e : k * own + e + 1], values, 0.0)
         rows_ref[:, r * model : (r + 1) * model] = rows.astype(jnp.bfloat16)
-    for number, weights in enumerate((*shares, last_share)):
-        first, depth = share_rows(projection_hbm.shape[0], number)
-        if number == len(shares):
-            copy.wait()
+    for number, weights in enumerate(shares):
+        first, depth = share_rows(rows_ref.shape[1], number)
         part = jnp.dot(rows_ref[:, first : first + depth], weights[...], preferred_element_type=jnp.float32)
         total = part if number == 0 else total + part
     out[...] = total[:count]
@@ -216,15 +212,13 @@
     return pl.pallas_call(
         functools.partial(project_body, len(sources)),
         out_shape=jax.ShapeDtypeStruct((count, width // ex_count), jnp.float32),
-        in_specs=[VMEM, HBM] + [VMEM] * (len(sources) + len(shares)),
+        in_specs=[VMEM] * (1 + len(sources) + len(shares)),
         out_specs=VMEM,
         scratch_shapes=[
-            pltpu.VMEM(share_shape(projection, len(shares), ex_count), projection.dtype),
             pltpu.VMEM((padded, depth), jnp.bfloat16),
-            pltpu.SemaphoreType.DMA,
         ],
         compiler_params=params(8),
-    )(ranks, hbm(projection), *sources, *[pltpu.with_memory_space_constraint(v, pltpu.VMEM) for v in shares])
+    )(ranks, *sources, *[pltpu.with_memory_space_constraint(v, pltpu.VMEM) for v in shares])
 
 
 def total_body(ex_count, *refs):

time: 34.2 us -> 33.8 us (0.988)
    pallas_call x1, Pallas kernels: 3.2 us -> 2.28 us  [project(): pl.pallas_call(functools.partial(project_body, len(sources)), out_shape=j...]
    pallas_call x2, Pallas kernels: 5.58 us -> 6.18 us  [load(): pl.pallas_call(functools.partial(load_body, number), out_shape=pltpu.VMEM...]
  transfers between devices with their start and end apart: 12 -> 12, of which waited for: 5 -> 5; matrix products, arithmetic and copies ran while one was open for 0% -> 0% of each run, Pallas kernels for 16% -> 18%
where the time goes in v8:
time: 33.8 us; the launch traced here: 33.6 us
  starting transfers between devices  13.4 us (40%)
  Pallas kernels  11.9 us (35%)
  waiting for transfers between devices  7.63 us (23%)
  between operations  0.73 us (2%)
    ppermute x12, starting transfers between devices, swap(): return lax.ppermute(value, tuple(axes) if len(axes) > 1 else axes[0], pairs)  13.4 us
    ppermute x12, waiting for transfers between devices, swap(): return lax.ppermute(value, tuple(axes) if len(axes) > 1 else axes[0], pairs)  7.63 us
    pallas_call x2, Pallas kernels, load(): pl.pallas_call(functools.partial(load_body, number), out_shape=pltpu.VMEM...  6.18 us
    pallas_call x1, Pallas kernels, gradient(): pl.pallas_call(functools.partial(gradient_body, chunks, counts), out_shap...  2.58 us
    pallas_call x1, Pallas kernels, project(): pl.pallas_call(functools.partial(project_body, len(sources)), out_shape=j...  2.28 us
    pallas_call x1, Pallas kernels, scale(): pl.pallas_call(functools.partial(scale_body, len(near), len(rows), column...  0.71 us
  transfers between devices with their start and end apart: 12, of which 5 were waited for; matrix products, arithmetic and copies ran while one was open for 0% of the time, Pallas kernels for 18%

profile of v8, /device:TPU:0, one launch (start us, length us, event | category | flops | bytes accessed | tf_op | source)
XLA Modules:
  0.0 33.6 jit_solution(16210917260630460861)
XLA Ops:
  0.7 2.6 %shard_map.64 = (f32[1,4,1024]{2,1,0:T(4,128)S(1)}, f32[1,4,1024]{2,1,0:T(4,128)S(1)}, f32[1,4,1024]{2,1,0:T(4,128)S(1)}, f32[1,4,1024]{2,1,0:T(4,128)S(1)}, s32...) custom-call(bf16[1,128,8192]{2,1,0:T(8,128)(2,1)} %hidden_hbm.1, bf16[16,8192]{1,0:T(8,128)(2,1)} %bitcast.1, ...), custom_call_target="tpu_custom_call" | custom-call | tf_op jit(solution)/shard_map/pallas_call | solution.py:149
  3.2 4.1 %collective-permute-start = (f32[1,4,1024]{2,1,0:T(4,128)S(1)}, f32[1,4,1024]{2,1,0:T(4,128)S(1)}, u32[]{:S(2)}, u32[]{:S(2)}) collective-permute-start(f32[1,4,1024]{2,1,0:T(4,128)S(1)} %get-tuple-element.18), channel_id=1, source_target_pairs={{0,8},{4,12},{8,0},{12,4},{1,9},{5,13},{9,1},{13,5},{2,10},{6,14},... | collective-permute-start | bytes 49160 | tf_op jit(solution)/shard_map/ppermute | solution.py:45
  7.4 1.3 %collective-permute-start.1 = (f32[1,4,1024]{2,1,0:T(4,128)S(1)}, f32[1,4,1024]{2,1,0:T(4,128)S(1)}, u32[]{:S(2)}, u32[]{:S(2)}) collective-permute-start(f32[1,4,1024]{2,1,0:T(4,128)S(1)} %get-tuple-element.19), channel_id=1, source_target_pairs={{0,12},{4,8},{8,4},{12,0},{1,13},{5,9},{9,5},{13,1},{2,14},{6,10},... | collective-permute-start | bytes 49160 | tf_op jit(solution)/shard_map/ppermute | solution.py:45
  8.7 0.2 collective-permute-start.2
  8.9 3.4 %shard_map.65.refs_4_.refs_5_ = bf16[2048,2048]{1,0:T(8,128)(2,1)S(1)} custom-call(s32[4,128]{1,0:T(4,128)S(1)} %get-tuple-element.16.after_ref.ranks_ref, bf16[4096,4096]{1,0:T(8,128)(2,1)} %projection_hbm.5), custom_call_target="tpu_custom_call" | custom-call | tf_op jit(solution)/shard_map/pallas_call | solution.py:84
  12.3 0.0 collective-permute-done.refs_1_
  12.4 0.5 %collective-permute-done.1.refs_2_ = f32[1,4,1024]{2,1,0:T(4,128)S(1)} collective-permute-done((f32[1,4,1024]{2,1,0:T(4,128)S(1)}, f32[1,4,1024]{2,1,0:T(4,128)S(1)}, u32[]{:S(2)}, u32[]{:S(2)}) %collective-permute-start.1) | collective-permute-done | bytes 16416 | tf_op jit(solution)/shard_map/ppermute | solution.py:45
  12.9 0.0 collective-permute-done.2.refs_3_
  12.9 1.6 %collective-permute-start.5 = (bf16[1,4,1024]{2,1,0:T(4,128)(2,1)S(1)}, bf16[1,4,1024]{2,1,0:T(4,128)(2,1)S(1)}, u32[]{:S(2)}, u32[]{:S(2)}) collective-permute-start(bf16[1,4,1024]{2,1,0:T(4,128)(2,1)S(1)} %shard_map.66.after_ref.refs_0_), channel_id=1, source_target_pairs={{0,2},{1,3},{2,0},{3,1},{4,6},{5,7},{6,4},{7,5},{8,10},{9,11},{10,... | collective-permute-start | bytes 24584 | tf_op jit(solution)/shard_map/ppermute | solution.py:45
  14.5 0.0 collective-permute-start.4
  14.5 0.6 %collective-permute-start.3 = (bf16[1,4,1024]{2,1,0:T(4,128)(2,1)S(1)}, bf16[1,4,1024]{2,1,0:T(4,128)(2,1)S(1)}, u32[]{:S(2)}, u32[]{:S(2)}) collective-permute-start(bf16[1,4,1024]{2,1,0:T(4,128)(2,1)S(1)} %shard_map.66.after_ref.refs_0_), channel_id=1, source_target_pairs={{0,3},{1,2},{2,1},{3,0},{4,7},{5,6},{6,5},{7,4},{8,11},{9,10},{10,... | collective-permute-start | bytes 24584 | tf_op jit(solution)/shard_map/ppermute | solution.py:45
  15.1 2.8 %shard_map.67.refs_6_ = bf16[1536,2048]{1,0:T(8,128)(2,1)S(1)} custom-call(bf16[1,4,1024]{2,1,0:T(4,128)(2,1)S(1)} %shard_map.66.after_ref.refs_0_, bf16[4096,4096]{1,0:T(8,128)(2,1)} %projection_hbm.5), custom_call_target="tpu_custom_call" | custom-call | tf_op jit(solution)/shard_map/pallas_call | solution.py:84
  17.9 0.0 collective-permute-done.5.refs_3_
  18.0 2.3 %shard_map.68.refs_0_ = f32[4,2048]{1,0:T(4,128)S(1)} custom-call(s32[4,128]{1,0:T(4,128)S(1)} %get-tuple-element.16.after_ref.ranks_ref, bf16[1,4,1024]{2,1,0:T(4,128)(2,1)S(1)} %shard_map.66.after_ref.refs_0_, bf16[1,4,1024]{2,1,0:T(4,128)(2,1)S(1)} %collective-permute-done.3.refs_1_, bf16[1,4,1024]{2,1,0:T(4,128)(2,1)S(1)} %collective-permute-done.4.refs_2_, ...), custom_call_target="tpu_custom_call" | custom-call | tf_op jit(solution)/shard_map/pallas_call | solution.py:212
  20.2 2.3 %collective-permute-start.8 = (f32[4,2048]{1,0:T(4,128)S(1)}, f32[4,2048]{1,0:T(4,128)S(1)}, u32[]{:S(2)}, u32[]{:S(2)}) collective-permute-start(f32[4,2048]{1,0:T(4,128)S(1)} %shard_map.68.refs_0_), channel_id=1, source_target_pairs={{0,8},{4,12},{8,0},{12,4},{1,9},{5,13},{9,1},{13,5},{2,10},{6,14},... | collective-permute-start | bytes 98312 | tf_op jit(solution)/shard_map/ppermute | solution.py:45
  22.5 1.3 %collective-permute-start.7 = (f32[4,2048]{1,0:T(4,128)S(1)}, f32[4,2048]{1,0:T(4,128)S(1)}, u32[]{:S(2)}, u32[]{:S(2)}) collective-permute-start(f32[4,2048]{1,0:T(4,128)S(1)} %shard_map.68.refs_0_), channel_id=1, source_target_pairs={{0,12},{4,8},{8,4},{12,0},{1,13},{5,9},{9,5},{13,1},{2,14},{6,10},... | collective-permute-start | bytes 98312 | tf_op jit(solution)/shard_map/ppermute | solution.py:45
  23.9 1.6 %collective-permute-done.8.refs_3_ = f32[4,2048]{1,0:T(4,128)S(1)} collective-permute-done((f32[4,2048]{1,0:T(4,128)S(1)}, f32[4,2048]{1,0:T(4,128)S(1)}, u32[]{:S(2)}, u32[]{:S(2)}) %collective-permute-start.8) | collective-permute-done | bytes 32800 | tf_op jit(solution)/shard_map/ppermute | solution.py:45
  25.5 2.8 %collective-permute-done.7.refs_2_ = f32[4,2048]{1,0:T(4,128)S(1)} collective-permute-done((f32[4,2048]{1,0:T(4,128)S(1)}, f32[4,2048]{1,0:T(4,128)S(1)}, u32[]{:S(2)}, u32[]{:S(2)}) %collective-permute-start.7) | collective-permute-done | bytes 32800 | tf_op jit(solution)/shard_map/ppermute | solution.py:45
  28.3 0.1 shard_map.69
  28.4 1.6 %collective-permute-start.9 = (f32[2,128]{1,0:T(2,128)S(1)}, f32[2,128]{1,0:T(2,128)S(1)}, u32[]{:S(2)}, u32[]{:S(2)}) collective-permute-start(f32[2,128]{1,0:T(2,128)S(1)} %get-tuple-element.22), channel_id=1, source_target_pairs={{0,2},{1,3},{2,0},{3,1},{4,6},{5,7},{6,4},{7,5},{8,10},{9,11},{10,... | collective-permute-start | bytes 3080 | tf_op jit(solution)/shard_map/ppermute | solution.py:45
  29.9 0.3 collective-permute-start.11
  30.2 1.8 %collective-permute-done.9.refs_0_ = f32[2,128]{1,0:T(2,128)S(1)} collective-permute-done((f32[2,128]{1,0:T(2,128)S(1)}, f32[2,128]{1,0:T(2,128)S(1)}, u32[]{:S(2)}, u32[]{:S(2)}) %collective-permute-start.9) | collective-permute-done | bytes 1056 | tf_op jit(solution)/shard_map/ppermute | solution.py:45
  32.0 0.9 %collective-permute-done.11.refs_3_ = f32[2,128]{1,0:T(2,128)S(1)} collective-permute-done((f32[2,128]{1,0:T(2,128)S(1)}, f32[2,128]{1,0:T(2,128)S(1)}, u32[]{:S(2)}, u32[]{:S(2)}) %collective-permute-start.11) | collective-permute-done | bytes 1056 | tf_op jit(solution)/shard_map/ppermute | solution.py:45
  32.9 0.7 %shard_map.70 = f32[2,4096]{1,0:T(2,128)} custom-call(f32[2,128]{1,0:T(2,128)S(1)} %collective-permute-done.9.refs_0_, f32[2,2048]{1,0:T(2,128)S(1)} %get-tuple-element.23.refs_1_, f32[2,2176]{1,0:T(2,128)S(1)} %collective-permute-done.10.refs_2_, f32[2,128]{1,0:T(2,128)S(1)} %collective-permute-done.11.refs_3_, f32[2,128]{1,0:T(2,128)S(1)} %get-tuple-element.26.refs_4_), custom_call_target="tpu_custom_call" | custom-call | tf_op jit(solution)/shard_map/pallas_call | solution.py:276
  (7 shorter events, 0.0 us)
Async XLA Ops:
  3.2 9.1 %collective-permute-start = (f32[1,4,1024]{2,1,0:T(4,128)S(1)}, f32[1,4,1024]{2,1,0:T(4,128)S(1)}, u32[]{:S(2)}, u32[]{:S(2)}) collective-permute-start(f32[1,4,1024]{2,1,0:T(4,128)S(1)} %get-tuple-element.18), channel_id=1, source_target_pairs={{0,8},{4,12},{8,0},{12,4},{1,9},{5,13},{9,1},{13,5},{2,10},{6,14},... | collective-permute-start | bytes 49160 | tf_op jit(solution)/shard_map/ppermute | solution.py:45
  7.4 5.5 %collective-permute-start.1 = (f32[1,4,1024]{2,1,0:T(4,128)S(1)}, f32[1,4,1024]{2,1,0:T(4,128)S(1)}, u32[]{:S(2)}, u32[]{:S(2)}) collective-permute-start(f32[1,4,1024]{2,1,0:T(4,128)S(1)} %get-tuple-element.19), channel_id=1, source_target_pairs={{0,12},{4,8},{8,4},{12,0},{1,13},{5,9},{9,5},{13,1},{2,14},{6,10},... | collective-permute-start | bytes 49160 | tf_op jit(solution)/shard_map/ppermute | solution.py:45
  8.7 4.2 %collective-permute-start.2 = (f32[1,4,1024]{2,1,0:T(4,128)S(1)}, f32[1,4,1024]{2,1,0:T(4,128)S(1)}, u32[]{:S(2)}, u32[]{:S(2)}) collective-permute-start(f32[1,4,1024]{2,1,0:T(4,128)S(1)} %get-tuple-element.20), channel_id=1, source_target_pairs={{0,4},{4,0},{8,12},{12,8},{1,5},{5,1},{9,13},{13,9},{2,6},{6,2},{1... | collective-permute-start | bytes 49160 | tf_op jit(solution)/shard_map/ppermute | solution.py:45
  12.9 5.0 %collective-permute-start.5 = (bf16[1,4,1024]{2,1,0:T(4,128)(2,1)S(1)}, bf16[1,4,1024]{2,1,0:T(4,128)(2,1)S(1)}, u32[]{:S(2)}, u32[]{:S(2)}) collective-permute-start(bf16[1,4,1024]{2,1,0:T(4,128)(2,1)S(1)} %shard_map.66.after_ref.refs_0_), channel_id=1, source_target_pairs={{0,2},{1,3},{2,0},{3,1},{4,6},{5,7},{6,4},{7,5},{8,10},{9,11},{10,... | collective-permute-start | bytes 24584 | tf_op jit(solution)/shard_map/ppermute | solution.py:45
  14.5 3.5 %collective-permute-start.4 = (bf16[1,4,1024]{2,1,0:T(4,128)(2,1)S(1)}, bf16[1,4,1024]{2,1,0:T(4,128)(2,1)S(1)}, u32[]{:S(2)}, u32[]{:S(2)}) collective-permute-start(bf16[1,4,1024]{2,1,0:T(4,128)(2,1)S(1)} %shard_map.66.after_ref.refs_0_), channel_id=1, source_target_pairs={{0,1},{1,0},{2,3},{3,2},{4,5},{5,4},{6,7},{7,6},{8,9},{9,8},{10,11... | collective-permute-start | bytes 24584 | tf_op jit(solution)/shard_map/ppermute | solution.py:45
  14.5 3.5 %collective-permute-start.3 = (bf16[1,4,1024]{2,1,0:T(4,128)(2,1)S(1)}, bf16[1,4,1024]{2,1,0:T(4,128)(2,1)S(1)}, u32[]{:S(2)}, u32[]{:S(2)}) collective-permute-start(bf16[1,4,1024]{2,1,0:T(4,128)(2,1)S(1)} %shard_map.66.after_ref.refs_0_), channel_id=1, source_target_pairs={{0,3},{1,2},{2,1},{3,0},{4,7},{5,6},{6,5},{7,4},{8,11},{9,10},{10,... | collective-permute-start | bytes 24584 | tf_op jit(solution)/shard_map/ppermute | solution.py:45
  20.2 5.2 %collective-permute-start.8 = (f32[4,2048]{1,0:T(4,128)S(1)}, f32[4,2048]{1,0:T(4,128)S(1)}, u32[]{:S(2)}, u32[]{:S(2)}) collective-permute-start(f32[4,2048]{1,0:T(4,128)S(1)} %shard_map.68.refs_0_), channel_id=1, source_target_pairs={{0,8},{4,12},{8,0},{12,4},{1,9},{5,13},{9,1},{13,5},{2,10},{6,14},... | collective-permute-start | bytes 98312 | tf_op jit(solution)/shard_map/ppermute | solution.py:45
  22.5 5.7 %collective-permute-start.7 = (f32[4,2048]{1,0:T(4,128)S(1)}, f32[4,2048]{1,0:T(4,128)S(1)}, u32[]{:S(2)}, u32[]{:S(2)}) collective-permute-start(f32[4,2048]{1,0:T(4,128)S(1)} %shard_map.68.refs_0_), channel_id=1, source_target_pairs={{0,12},{4,8},{8,4},{12,0},{1,13},{5,9},{9,5},{13,1},{2,14},{6,10},... | collective-permute-start | bytes 98312 | tf_op jit(solution)/shard_map/ppermute | solution.py:45
  23.9 4.4 %collective-permute-start.6 = (f32[4,2048]{1,0:T(4,128)S(1)}, f32[4,2048]{1,0:T(4,128)S(1)}, u32[]{:S(2)}, u32[]{:S(2)}) collective-permute-start(f32[4,2048]{1,0:T(4,128)S(1)} %shard_map.68.refs_0_), channel_id=1, source_target_pairs={{0,4},{4,0},{8,12},{12,8},{1,5},{5,1},{9,13},{13,9},{2,6},{6,2},{1... | collective-permute-start | bytes 98312 | tf_op jit(solution)/shard_map/ppermute | solution.py:45
  28.4 4.6 %collective-permute-start.10 = (f32[2,2176]{1,0:T(2,128)S(1)}, f32[2,2176]{1,0:T(2,128)S(1)}, u32[]{:S(2)}, u32[]{:S(2)}) collective-permute-start(f32[2,2176]{1,0:T(2,128)S(1)} %get-tuple-element.24), channel_id=1, source_target_pairs={{0,1},{1,0},{2,3},{3,2},{4,5},{5,4},{6,7},{7,6},{8,9},{9,8},{10,11... | collective-permute-start | bytes 52232 | tf_op jit(solution)/shard_map/ppermute | solution.py:45
  28.4 3.6 %collective-permute-start.9 = (f32[2,128]{1,0:T(2,128)S(1)}, f32[2,128]{1,0:T(2,128)S(1)}, u32[]{:S(2)}, u32[]{:S(2)}) collective-permute-start(f32[2,128]{1,0:T(2,128)S(1)} %get-tuple-element.22), channel_id=1, source_target_pairs={{0,2},{1,3},{2,0},{3,1},{4,6},{5,7},{6,4},{7,5},{8,10},{9,11},{10,... | collective-permute-start | bytes 3080 | tf_op jit(solution)/shard_map/ppermute | solution.py:45
  29.9 3.0 %collective-permute-start.11 = (f32[2,128]{1,0:T(2,128)S(1)}, f32[2,128]{1,0:T(2,128)S(1)}, u32[]{:S(2)}, u32[]{:S(2)}) collective-permute-start(f32[2,128]{1,0:T(2,128)S(1)} %get-tuple-element.25), channel_id=1, source_target_pairs={{0,3},{1,2},{2,1},{3,0},{4,7},{5,6},{6,5},{7,4},{8,11},{9,10},{10,... | collective-permute-start | bytes 3080 | tf_op jit(solution)/shard_map/ppermute | solution.py:45

commit v9 on v8

--- a/solution.py
+++ b/solution.py
@@ -9,7 +9,7 @@
 from jax.sharding import PartitionSpec as P
 
 MIB = 1 << 20
-SHARES = (1, 4, 3)
+SHARES = (2, 3, 3)
 VMEM = pl.BlockSpec(memory_space=pltpu.VMEM)
 HBM = pl.BlockSpec(memory_space=pltpu.HBM)
 

time: 33.8 us -> 33.7 us (level)
    pallas_call x2, Pallas kernels: 6.18 us -> 5.58 us  [load(): pl.pallas_call(functools.partial(load_body, number), out_shape=pltpu.VMEM...]
    pallas_call x1, Pallas kernels: 2.58 us -> 3.05 us  [gradient(): pl.pallas_call(functools.partial(gradient_body, chunks, counts), out_shap...]
  transfers between devices with their start and end apart: 12 -> 12, of which waited for: 5 -> 5; matrix products, arithmetic and copies ran while one was open for 0% -> 0% of each run, Pallas kernels for 18% -> 17%
where the time goes in v9:
time: 33.7 us; the launch traced here: 33.5 us
  starting transfers between devices  13.3 us (39%)
  Pallas kernels  11.7 us (35%)
  waiting for transfers between devices  7.77 us (23%)
  between operations  0.73 us (2%)
    ppermute x12, starting transfers between devices, swap(): return lax.ppermute(value, tuple(axes) if len(axes) > 1 else axes[0], pairs)  13.3 us
    ppermute x12, waiting for transfers between devices, swap(): return lax.ppermute(value, tuple(axes) if len(axes) > 1 else axes[0], pairs)  7.77 us
    pallas_call x2, Pallas kernels, load(): pl.pallas_call(functools.partial(load_body, number), out_shape=pltpu.VMEM...  5.58 us
    pallas_call x1, Pallas kernels, gradient(): pl.pallas_call(functools.partial(gradient_body, chunks, counts), out_shap...  3.05 us
    pallas_call x1, Pallas kernels, project(): pl.pallas_call(functools.partial(project_body, len(sources)), out_shape=j...  2.28 us
    pallas_call x1, Pallas kernels, scale(): pl.pallas_call(functools.partial(scale_body, len(near), len(rows), column...  0.71 us
  transfers between devices with their start and end apart: 12, of which 5 were waited for; matrix products, arithmetic and copies ran while one was open for 0% of the time, Pallas kernels for 17%

profile of v9, /device:TPU:0, one launch (start us, length us, event | category | flops | bytes accessed | tf_op | source)
XLA Modules:
  0.0 33.5 jit_solution(4466662699538318930)
XLA Ops:
  0.7 3.1 %shard_map.64 = (f32[1,4,1024]{2,1,0:T(4,128)S(1)}, f32[1,4,1024]{2,1,0:T(4,128)S(1)}, f32[1,4,1024]{2,1,0:T(4,128)S(1)}, f32[1,4,1024]{2,1,0:T(4,128)S(1)}, s32...) custom-call(bf16[1,128,8192]{2,1,0:T(8,128)(2,1)} %hidden_hbm.1, bf16[16,8192]{1,0:T(8,128)(2,1)} %bitcast.1, ...), custom_call_target="tpu_custom_call" | custom-call | tf_op jit(solution)/shard_map/pallas_call | solution.py:149
  3.7 4.1 %collective-permute-start = (f32[1,4,1024]{2,1,0:T(4,128)S(1)}, f32[1,4,1024]{2,1,0:T(4,128)S(1)}, u32[]{:S(2)}, u32[]{:S(2)}) collective-permute-start(f32[1,4,1024]{2,1,0:T(4,128)S(1)} %get-tuple-element.18), channel_id=1, source_target_pairs={{0,8},{4,12},{8,0},{12,4},{1,9},{5,13},{9,1},{13,5},{2,10},{6,14},... | collective-permute-start | bytes 49160 | tf_op jit(solution)/shard_map/ppermute | solution.py:45
  7.8 1.3 %collective-permute-start.1 = (f32[1,4,1024]{2,1,0:T(4,128)S(1)}, f32[1,4,1024]{2,1,0:T(4,128)S(1)}, u32[]{:S(2)}, u32[]{:S(2)}) collective-permute-start(f32[1,4,1024]{2,1,0:T(4,128)S(1)} %get-tuple-element.19), channel_id=1, source_target_pairs={{0,12},{4,8},{8,4},{12,0},{1,13},{5,9},{9,5},{13,1},{2,14},{6,10},... | collective-permute-start | bytes 49160 | tf_op jit(solution)/shard_map/ppermute | solution.py:45
  9.2 0.2 collective-permute-start.2
  9.4 2.8 %shard_map.65.refs_4_.refs_5_ = bf16[1536,2048]{1,0:T(8,128)(2,1)S(1)} custom-call(s32[4,128]{1,0:T(4,128)S(1)} %get-tuple-element.16.after_ref.ranks_ref, bf16[4096,4096]{1,0:T(8,128)(2,1)} %projection_hbm.5), custom_call_target="tpu_custom_call" | custom-call | tf_op jit(solution)/shard_map/pallas_call | solution.py:84
  12.2 0.0 collective-permute-done.refs_1_
  12.2 1.1 %collective-permute-done.1.refs_2_ = f32[1,4,1024]{2,1,0:T(4,128)S(1)} collective-permute-done((f32[1,4,1024]{2,1,0:T(4,128)S(1)}, f32[1,4,1024]{2,1,0:T(4,128)S(1)}, u32[]{:S(2)}, u32[]{:S(2)}) %collective-permute-start.1) | collective-permute-done | bytes 16416 | tf_op jit(solution)/shard_map/ppermute | solution.py:45
  13.4 0.0 collective-permute-done.2.refs_3_
  13.4 1.6 %collective-permute-start.5 = (bf16[1,4,1024]{2,1,0:T(4,128)(2,1)S(1)}, bf16[1,4,1024]{2,1,0:T(4,128)(2,1)S(1)}, u32[]{:S(2)}, u32[]{:S(2)}) collective-permute-start(bf16[1,4,1024]{2,1,0:T(4,128)(2,1)S(1)} %shard_map.66.after_ref.refs_0_), channel_id=1, source_target_pairs={{0,2},{1,3},{2,0},{3,1},{4,6},{5,7},{6,4},{7,5},{8,10},{9,11},{10,... | collective-permute-start | bytes 24584 | tf_op jit(solution)/shard_map/ppermute | solution.py:45
  15.0 0.0 collective-permute-start.4
  15.0 0.6 %collective-permute-start.3 = (bf16[1,4,1024]{2,1,0:T(4,128)(2,1)S(1)}, bf16[1,4,1024]{2,1,0:T(4,128)(2,1)S(1)}, u32[]{:S(2)}, u32[]{:S(2)}) collective-permute-start(bf16[1,4,1024]{2,1,0:T(4,128)(2,1)S(1)} %shard_map.66.after_ref.refs_0_), channel_id=1, source_target_pairs={{0,3},{1,2},{2,1},{3,0},{4,7},{5,6},{6,5},{7,4},{8,11},{9,10},{10,... | collective-permute-start | bytes 24584 | tf_op jit(solution)/shard_map/ppermute | solution.py:45
  15.6 2.8 %shard_map.67.refs_6_ = bf16[1536,2048]{1,0:T(8,128)(2,1)S(1)} custom-call(bf16[1,4,1024]{2,1,0:T(4,128)(2,1)S(1)} %shard_map.66.after_ref.refs_0_, bf16[4096,4096]{1,0:T(8,128)(2,1)} %projection_hbm.5), custom_call_target="tpu_custom_call" | custom-call | tf_op jit(solution)/shard_map/pallas_call | solution.py:84
  18.4 2.3 %shard_map.68.refs_0_ = f32[4,2048]{1,0:T(4,128)S(1)} custom-call(s32[4,128]{1,0:T(4,128)S(1)} %get-tuple-element.16.after_ref.ranks_ref, bf16[1,4,1024]{2,1,0:T(4,128)(2,1)S(1)} %shard_map.66.after_ref.refs_0_, bf16[1,4,1024]{2,1,0:T(4,128)(2,1)S(1)} %collective-permute-done.3.refs_1_, bf16[1,4,1024]{2,1,0:T(4,128)(2,1)S(1)} %collective-permute-done.4.refs_2_, ...), custom_call_target="tpu_custom_call" | custom-call | tf_op jit(solution)/shard_map/pallas_call | solution.py:212
  20.7 1.7 %collective-permute-start.8 = (f32[4,2048]{1,0:T(4,128)S(1)}, f32[4,2048]{1,0:T(4,128)S(1)}, u32[]{:S(2)}, u32[]{:S(2)}) collective-permute-start(f32[4,2048]{1,0:T(4,128)S(1)} %shard_map.68.refs_0_), channel_id=1, source_target_pairs={{0,8},{4,12},{8,0},{12,4},{1,9},{5,13},{9,1},{13,5},{2,10},{6,14},... | collective-permute-start | bytes 98312 | tf_op jit(solution)/shard_map/ppermute | solution.py:45
  22.4 1.3 %collective-permute-start.7 = (f32[4,2048]{1,0:T(4,128)S(1)}, f32[4,2048]{1,0:T(4,128)S(1)}, u32[]{:S(2)}, u32[]{:S(2)}) collective-permute-start(f32[4,2048]{1,0:T(4,128)S(1)} %shard_map.68.refs_0_), channel_id=1, source_target_pairs={{0,12},{4,8},{8,4},{12,0},{1,13},{5,9},{9,5},{13,1},{2,14},{6,10},... | collective-permute-start | bytes 98312 | tf_op jit(solution)/shard_map/ppermute | solution.py:45
  23.8 0.5 %collective-permute-start.6 = (f32[4,2048]{1,0:T(4,128)S(1)}, f32[4,2048]{1,0:T(4,128)S(1)}, u32[]{:S(2)}, u32[]{:S(2)}) collective-permute-start(f32[4,2048]{1,0:T(4,128)S(1)} %shard_map.68.refs_0_), channel_id=1, source_target_pairs={{0,4},{4,0},{8,12},{12,8},{1,5},{5,1},{9,13},{13,9},{2,6},{6,2},{1... | collective-permute-start | bytes 98312 | tf_op jit(solution)/shard_map/ppermute | solution.py:45
  24.2 2.1 %collective-permute-done.8.refs_3_ = f32[4,2048]{1,0:T(4,128)S(1)} collective-permute-done((f32[4,2048]{1,0:T(4,128)S(1)}, f32[4,2048]{1,0:T(4,128)S(1)}, u32[]{:S(2)}, u32[]{:S(2)}) %collective-permute-start.8) | collective-permute-done | bytes 32800 | tf_op jit(solution)/shard_map/ppermute | solution.py:45
  26.3 1.8 %collective-permute-done.7.refs_2_ = f32[4,2048]{1,0:T(4,128)S(1)} collective-permute-done((f32[4,2048]{1,0:T(4,128)S(1)}, f32[4,2048]{1,0:T(4,128)S(1)}, u32[]{:S(2)}, u32[]{:S(2)}) %collective-permute-start.7) | collective-permute-done | bytes 32800 | tf_op jit(solution)/shard_map/ppermute | solution.py:45
  28.1 0.1 shard_map.69
  28.2 1.6 %collective-permute-start.9 = (f32[2,128]{1,0:T(2,128)S(1)}, f32[2,128]{1,0:T(2,128)S(1)}, u32[]{:S(2)}, u32[]{:S(2)}) collective-permute-start(f32[2,128]{1,0:T(2,128)S(1)} %get-tuple-element.22), channel_id=1, source_target_pairs={{0,2},{1,3},{2,0},{3,1},{4,6},{5,7},{6,4},{7,5},{8,10},{9,11},{10,... | collective-permute-start | bytes 3080 | tf_op jit(solution)/shard_map/ppermute | solution.py:45
  29.8 0.3 collective-permute-start.11
  30.1 1.8 %collective-permute-done.9.refs_0_ = f32[2,128]{1,0:T(2,128)S(1)} collective-permute-done((f32[2,128]{1,0:T(2,128)S(1)}, f32[2,128]{1,0:T(2,128)S(1)}, u32[]{:S(2)}, u32[]{:S(2)}) %collective-permute-start.9) | collective-permute-done | bytes 1056 | tf_op jit(solution)/shard_map/ppermute | solution.py:45
  31.9 0.9 %collective-permute-done.11.refs_3_ = f32[2,128]{1,0:T(2,128)S(1)} collective-permute-done((f32[2,128]{1,0:T(2,128)S(1)}, f32[2,128]{1,0:T(2,128)S(1)}, u32[]{:S(2)}, u32[]{:S(2)}) %collective-permute-start.11) | collective-permute-done | bytes 1056 | tf_op jit(solution)/shard_map/ppermute | solution.py:45
  32.8 0.7 %shard_map.70 = f32[2,4096]{1,0:T(2,128)} custom-call(f32[2,128]{1,0:T(2,128)S(1)} %collective-permute-done.9.refs_0_, f32[2,2048]{1,0:T(2,128)S(1)} %get-tuple-element.23.refs_1_, f32[2,2176]{1,0:T(2,128)S(1)} %collective-permute-done.10.refs_2_, f32[2,128]{1,0:T(2,128)S(1)} %collective-permute-done.11.refs_3_, f32[2,128]{1,0:T(2,128)S(1)} %get-tuple-element.26.refs_4_), custom_call_target="tpu_custom_call" | custom-call | tf_op jit(solution)/shard_map/pallas_call | solution.py:276
  (7 shorter events, 0.0 us)
Async XLA Ops:
  3.7 8.5 %collective-permute-start = (f32[1,4,1024]{2,1,0:T(4,128)S(1)}, f32[1,4,1024]{2,1,0:T(4,128)S(1)}, u32[]{:S(2)}, u32[]{:S(2)}) collective-permute-start(f32[1,4,1024]{2,1,0:T(4,128)S(1)} %get-tuple-element.18), channel_id=1, source_target_pairs={{0,8},{4,12},{8,0},{12,4},{1,9},{5,13},{9,1},{13,5},{2,10},{6,14},... | collective-permute-start | bytes 49160 | tf_op jit(solution)/shard_map/ppermute | solution.py:45
  7.8 5.5 %collective-permute-start.1 = (f32[1,4,1024]{2,1,0:T(4,128)S(1)}, f32[1,4,1024]{2,1,0:T(4,128)S(1)}, u32[]{:S(2)}, u32[]{:S(2)}) collective-permute-start(f32[1,4,1024]{2,1,0:T(4,128)S(1)} %get-tuple-element.19), channel_id=1, source_target_pairs={{0,12},{4,8},{8,4},{12,0},{1,13},{5,9},{9,5},{13,1},{2,14},{6,10},... | collective-permute-start | bytes 49160 | tf_op jit(solution)/shard_map/ppermute | solution.py:45
  9.2 4.2 %collective-permute-start.2 = (f32[1,4,1024]{2,1,0:T(4,128)S(1)}, f32[1,4,1024]{2,1,0:T(4,128)S(1)}, u32[]{:S(2)}, u32[]{:S(2)}) collective-permute-start(f32[1,4,1024]{2,1,0:T(4,128)S(1)} %get-tuple-element.20), channel_id=1, source_target_pairs={{0,4},{4,0},{8,12},{12,8},{1,5},{5,1},{9,13},{13,9},{2,6},{6,2},{1... | collective-permute-start | bytes 49160 | tf_op jit(solution)/shard_map/ppermute | solution.py:45
  13.4 5.0 %collective-permute-start.5 = (bf16[1,4,1024]{2,1,0:T(4,128)(2,1)S(1)}, bf16[1,4,1024]{2,1,0:T(4,128)(2,1)S(1)}, u32[]{:S(2)}, u32[]{:S(2)}) collective-permute-start(bf16[1,4,1024]{2,1,0:T(4,128)(2,1)S(1)} %shard_map.66.after_ref.refs_0_), channel_id=1, source_target_pairs={{0,2},{1,3},{2,0},{3,1},{4,6},{5,7},{6,4},{7,5},{8,10},{9,11},{10,... | collective-permute-start | bytes 24584 | tf_op jit(solution)/shard_map/ppermute | solution.py:45
  15.0 3.5 %collective-permute-start.4 = (bf16[1,4,1024]{2,1,0:T(4,128)(2,1)S(1)}, bf16[1,4,1024]{2,1,0:T(4,128)(2,1)S(1)}, u32[]{:S(2)}, u32[]{:S(2)}) collective-permute-start(bf16[1,4,1024]{2,1,0:T(4,128)(2,1)S(1)} %shard_map.66.after_ref.refs_0_), channel_id=1, source_target_pairs={{0,1},{1,0},{2,3},{3,2},{4,5},{5,4},{6,7},{7,6},{8,9},{9,8},{10,11... | collective-permute-start | bytes 24584 | tf_op jit(solution)/shard_map/ppermute | solution.py:45
  15.0 3.5 %collective-permute-start.3 = (bf16[1,4,1024]{2,1,0:T(4,128)(2,1)S(1)}, bf16[1,4,1024]{2,1,0:T(4,128)(2,1)S(1)}, u32[]{:S(2)}, u32[]{:S(2)}) collective-permute-start(bf16[1,4,1024]{2,1,0:T(4,128)(2,1)S(1)} %shard_map.66.after_ref.refs_0_), channel_id=1, source_target_pairs={{0,3},{1,2},{2,1},{3,0},{4,7},{5,6},{6,5},{7,4},{8,11},{9,10},{10,... | collective-permute-start | bytes 24584 | tf_op jit(solution)/shard_map/ppermute | solution.py:45
  20.7 5.6 %collective-permute-start.8 = (f32[4,2048]{1,0:T(4,128)S(1)}, f32[4,2048]{1,0:T(4,128)S(1)}, u32[]{:S(2)}, u32[]{:S(2)}) collective-permute-start(f32[4,2048]{1,0:T(4,128)S(1)} %shard_map.68.refs_0_), channel_id=1, source_target_pairs={{0,8},{4,12},{8,0},{12,4},{1,9},{5,13},{9,1},{13,5},{2,10},{6,14},... | collective-permute-start | bytes 98312 | tf_op jit(solution)/shard_map/ppermute | solution.py:45
  22.4 5.7 %collective-permute-start.7 = (f32[4,2048]{1,0:T(4,128)S(1)}, f32[4,2048]{1,0:T(4,128)S(1)}, u32[]{:S(2)}, u32[]{:S(2)}) collective-permute-start(f32[4,2048]{1,0:T(4,128)S(1)} %shard_map.68.refs_0_), channel_id=1, source_target_pairs={{0,12},{4,8},{8,4},{12,0},{1,13},{5,9},{9,5},{13,1},{2,14},{6,10},... | collective-permute-start | bytes 98312 | tf_op jit(solution)/shard_map/ppermute | solution.py:45
  23.8 4.4 %collective-permute-start.6 = (f32[4,2048]{1,0:T(4,128)S(1)}, f32[4,2048]{1,0:T(4,128)S(1)}, u32[]{:S(2)}, u32[]{:S(2)}) collective-permute-start(f32[4,2048]{1,0:T(4,128)S(1)} %shard_map.68.refs_0_), channel_id=1, source_target_pairs={{0,4},{4,0},{8,12},{12,8},{1,5},{5,1},{9,13},{13,9},{2,6},{6,2},{1... | collective-permute-start | bytes 98312 | tf_op jit(solution)/shard_map/ppermute | solution.py:45
  28.2 4.6 %collective-permute-start.10 = (f32[2,2176]{1,0:T(2,128)S(1)}, f32[2,2176]{1,0:T(2,128)S(1)}, u32[]{:S(2)}, u32[]{:S(2)}) collective-permute-start(f32[2,2176]{1,0:T(2,128)S(1)} %get-tuple-element.24), channel_id=1, source_target_pairs={{0,1},{1,0},{2,3},{3,2},{4,5},{5,4},{6,7},{7,6},{8,9},{9,8},{10,11... | collective-permute-start | bytes 52232 | tf_op jit(solution)/shard_map/ppermute | solution.py:45
  28.2 3.6 %collective-permute-start.9 = (f32[2,128]{1,0:T(2,128)S(1)}, f32[2,128]{1,0:T(2,128)S(1)}, u32[]{:S(2)}, u32[]{:S(2)}) collective-permute-start(f32[2,128]{1,0:T(2,128)S(1)} %get-tuple-element.22), channel_id=1, source_target_pairs={{0,2},{1,3},{2,0},{3,1},{4,6},{5,7},{6,4},{7,5},{8,10},{9,11},{10,... | collective-permute-start | bytes 3080 | tf_op jit(solution)/shard_map/ppermute | solution.py:45
  29.8 3.0 %collective-permute-start.11 = (f32[2,128]{1,0:T(2,128)S(1)}, f32[2,128]{1,0:T(2,128)S(1)}, u32[]{:S(2)}, u32[]{:S(2)}) collective-permute-start(f32[2,128]{1,0:T(2,128)S(1)} %get-tuple-element.25), channel_id=1, source_target_pairs={{0,3},{1,2},{2,1},{3,0},{4,7},{5,6},{6,5},{7,4},{8,11},{9,10},{10,... | collective-permute-start | bytes 3080 | tf_op jit(solution)/shard_map/ppermute | solution.py:45

commit v10 on v9

--- a/solution.py
+++ b/solution.py
@@ -9,7 +9,7 @@
 from jax.sharding import PartitionSpec as P
 
 MIB = 1 << 20
-SHARES = (2, 3, 3)
+SHARES = (3, 2, 3)
 VMEM = pl.BlockSpec(memory_space=pltpu.VMEM)
 HBM = pl.BlockSpec(memory_space=pltpu.HBM)
 

time: 33.7 us -> 33.8 us (level)
    pallas_call x1, Pallas kernels: 3.05 us -> 3.65 us  [gradient(): pl.pallas_call(functools.partial(gradient_body, chunks, counts), out_shap...]
    pallas_call x2, Pallas kernels: 5.58 us -> 5.05 us  [load(): pl.pallas_call(functools.partial(load_body, number), out_shape=pltpu.VMEM...]
  transfers between devices with their start and end apart: 12 -> 12, of which waited for: 5 -> 5; matrix products, arithmetic and copies ran while one was open for 0% -> 0% of each run, Pallas kernels for 17% -> 15%
where the time goes in v10:
time: 33.8 us; the launch traced here: 33.7 us
  starting transfers between devices  13.3 us (39%)
  Pallas kernels  11.8 us (35%)
  waiting for transfers between devices  7.86 us (23%)
  between operations  0.73 us (2%)
    ppermute x12, starting transfers between devices, swap(): return lax.ppermute(value, tuple(axes) if len(axes) > 1 else axes[0], pairs)  13.3 us
    ppermute x12, waiting for transfers between devices, swap(): return lax.ppermute(value, tuple(axes) if len(axes) > 1 else axes[0], pairs)  7.86 us
    pallas_call x2, Pallas kernels, load(): pl.pallas_call(functools.partial(load_body, number), out_shape=pltpu.VMEM...  5.05 us
    pallas_call x1, Pallas kernels, gradient(): pl.pallas_call(functools.partial(gradient_body, chunks, counts), out_shap...  3.65 us
    pallas_call x1, Pallas kernels, project(): pl.pallas_call(functools.partial(project_body, len(sources)), out_shape=j...  2.28 us
    pallas_call x1, Pallas kernels, scale(): pl.pallas_call(functools.partial(scale_body, len(near), len(rows), column...  0.71 us
  transfers between devices with their start and end apart: 12, of which 5 were waited for; matrix products, arithmetic and copies ran while one was open for 0% of the time, Pallas kernels for 15%

profile of v10, /device:TPU:0, one launch (start us, length us, event | category | flops | bytes accessed | tf_op | source)
XLA Modules:
  0.0 33.7 jit_solution(14816626374166025608)
XLA Ops:
  0.7 3.6 %shard_map.64 = (f32[1,4,1024]{2,1,0:T(4,128)S(1)}, f32[1,4,1024]{2,1,0:T(4,128)S(1)}, f32[1,4,1024]{2,1,0:T(4,128)S(1)}, f32[1,4,1024]{2,1,0:T(4,128)S(1)}, s32...) custom-call(bf16[1,128,8192]{2,1,0:T(8,128)(2,1)} %hidden_hbm.1, bf16[16,8192]{1,0:T(8,128)(2,1)} %bitcast.1, ...), custom_call_target="tpu_custom_call" | custom-call | tf_op jit(solution)/shard_map/pallas_call | solution.py:149
  4.3 4.1 %collective-permute-start = (f32[1,4,1024]{2,1,0:T(4,128)S(1)}, f32[1,4,1024]{2,1,0:T(4,128)S(1)}, u32[]{:S(2)}, u32[]{:S(2)}) collective-permute-start(f32[1,4,1024]{2,1,0:T(4,128)S(1)} %get-tuple-element.18), channel_id=1, source_target_pairs={{0,8},{4,12},{8,0},{12,4},{1,9},{5,13},{9,1},{13,5},{2,10},{6,14},... | collective-permute-start | bytes 49160 | tf_op jit(solution)/shard_map/ppermute | solution.py:45
  8.4 1.3 %collective-permute-start.1 = (f32[1,4,1024]{2,1,0:T(4,128)S(1)}, f32[1,4,1024]{2,1,0:T(4,128)S(1)}, u32[]{:S(2)}, u32[]{:S(2)}) collective-permute-start(f32[1,4,1024]{2,1,0:T(4,128)S(1)} %get-tuple-element.19), channel_id=1, source_target_pairs={{0,12},{4,8},{8,4},{12,0},{1,13},{5,9},{9,5},{13,1},{2,14},{6,10},... | collective-permute-start | bytes 49160 | tf_op jit(solution)/shard_map/ppermute | solution.py:45
  9.8 0.2 collective-permute-start.2
  10.0 2.3 %shard_map.65.refs_4_.refs_5_ = bf16[1024,2048]{1,0:T(8,128)(2,1)S(1)} custom-call(s32[4,128]{1,0:T(4,128)S(1)} %get-tuple-element.16.after_ref.ranks_ref, bf16[4096,4096]{1,0:T(8,128)(2,1)} %projection_hbm.5), custom_call_target="tpu_custom_call" | custom-call | tf_op jit(solution)/shard_map/pallas_call | solution.py:84
  12.3 0.0 collective-permute-done.refs_1_
  12.3 1.7 %collective-permute-done.1.refs_2_ = f32[1,4,1024]{2,1,0:T(4,128)S(1)} collective-permute-done((f32[1,4,1024]{2,1,0:T(4,128)S(1)}, f32[1,4,1024]{2,1,0:T(4,128)S(1)}, u32[]{:S(2)}, u32[]{:S(2)}) %collective-permute-start.1) | collective-permute-done | bytes 16416 | tf_op jit(solution)/shard_map/ppermute | solution.py:45
  14.0 0.0 collective-permute-done.2.refs_3_
  14.0 1.6 %collective-permute-start.5 = (bf16[1,4,1024]{2,1,0:T(4,128)(2,1)S(1)}, bf16[1,4,1024]{2,1,0:T(4,128)(2,1)S(1)}, u32[]{:S(2)}, u32[]{:S(2)}) collective-permute-start(bf16[1,4,1024]{2,1,0:T(4,128)(2,1)S(1)} %shard_map.66.after_ref.refs_0_), channel_id=1, source_target_pairs={{0,2},{1,3},{2,0},{3,1},{4,6},{5,7},{6,4},{7,5},{8,10},{9,11},{10,... | collective-permute-start | bytes 24584 | tf_op jit(solution)/shard_map/ppermute | solution.py:45
  15.6 0.0 collective-permute-start.4
  15.6 0.6 %collective-permute-start.3 = (bf16[1,4,1024]{2,1,0:T(4,128)(2,1)S(1)}, bf16[1,4,1024]{2,1,0:T(4,128)(2,1)S(1)}, u32[]{:S(2)}, u32[]{:S(2)}) collective-permute-start(bf16[1,4,1024]{2,1,0:T(4,128)(2,1)S(1)} %shard_map.66.after_ref.refs_0_), channel_id=1, source_target_pairs={{0,3},{1,2},{2,1},{3,0},{4,7},{5,6},{6,5},{7,4},{8,11},{9,10},{10,... | collective-permute-start | bytes 24584 | tf_op jit(solution)/shard_map/ppermute | solution.py:45
  16.2 2.8 %shard_map.67.refs_6_ = bf16[1536,2048]{1,0:T(8,128)(2,1)S(1)} custom-call(bf16[1,4,1024]{2,1,0:T(4,128)(2,1)S(1)} %shard_map.66.after_ref.refs_0_, bf16[4096,4096]{1,0:T(8,128)(2,1)} %projection_hbm.5), custom_call_target="tpu_custom_call" | custom-call | tf_op jit(solution)/shard_map/pallas_call | solution.py:84
  19.0 2.3 %shard_map.68.refs_0_ = f32[4,2048]{1,0:T(4,128)S(1)} custom-call(s32[4,128]{1,0:T(4,128)S(1)} %get-tuple-element.16.after_ref.ranks_ref, bf16[1,4,1024]{2,1,0:T(4,128)(2,1)S(1)} %shard_map.66.after_ref.refs_0_, bf16[1,4,1024]{2,1,0:T(4,128)(2,1)S(1)} %collective-permute-done.3.refs_1_, bf16[1,4,1024]{2,1,0:T(4,128)(2,1)S(1)} %collective-permute-done.4.refs_2_, ...), custom_call_target="tpu_custom_call" | custom-call | tf_op jit(solution)/shard_map/pallas_call | solution.py:212
  21.3 1.2 %collective-permute-start.8 = (f32[4,2048]{1,0:T(4,128)S(1)}, f32[4,2048]{1,0:T(4,128)S(1)}, u32[]{:S(2)}, u32[]{:S(2)}) collective-permute-start(f32[4,2048]{1,0:T(4,128)S(1)} %shard_map.68.refs_0_), channel_id=1, source_target_pairs={{0,8},{4,12},{8,0},{12,4},{1,9},{5,13},{9,1},{13,5},{2,10},{6,14},... | collective-permute-start | bytes 98312 | tf_op jit(solution)/shard_map/ppermute | solution.py:45
  22.6 1.3 %collective-permute-start.7 = (f32[4,2048]{1,0:T(4,128)S(1)}, f32[4,2048]{1,0:T(4,128)S(1)}, u32[]{:S(2)}, u32[]{:S(2)}) collective-permute-start(f32[4,2048]{1,0:T(4,128)S(1)} %shard_map.68.refs_0_), channel_id=1, source_target_pairs={{0,12},{4,8},{8,4},{12,0},{1,13},{5,9},{9,5},{13,1},{2,14},{6,10},... | collective-permute-start | bytes 98312 | tf_op jit(solution)/shard_map/ppermute | solution.py:45
  23.8 1.0 %collective-permute-start.6 = (f32[4,2048]{1,0:T(4,128)S(1)}, f32[4,2048]{1,0:T(4,128)S(1)}, u32[]{:S(2)}, u32[]{:S(2)}) collective-permute-start(f32[4,2048]{1,0:T(4,128)S(1)} %shard_map.68.refs_0_), channel_id=1, source_target_pairs={{0,4},{4,0},{8,12},{12,8},{1,5},{5,1},{9,13},{13,9},{2,6},{6,2},{1... | collective-permute-start | bytes 98312 | tf_op jit(solution)/shard_map/ppermute | solution.py:45
  24.8 1.7 %collective-permute-done.8.refs_3_ = f32[4,2048]{1,0:T(4,128)S(1)} collective-permute-done((f32[4,2048]{1,0:T(4,128)S(1)}, f32[4,2048]{1,0:T(4,128)S(1)}, u32[]{:S(2)}, u32[]{:S(2)}) %collective-permute-start.8) | collective-permute-done | bytes 32800 | tf_op jit(solution)/shard_map/ppermute | solution.py:45
  26.6 1.7 %collective-permute-done.7.refs_2_ = f32[4,2048]{1,0:T(4,128)S(1)} collective-permute-done((f32[4,2048]{1,0:T(4,128)S(1)}, f32[4,2048]{1,0:T(4,128)S(1)}, u32[]{:S(2)}, u32[]{:S(2)}) %collective-permute-start.7) | collective-permute-done | bytes 32800 | tf_op jit(solution)/shard_map/ppermute | solution.py:45
  28.3 0.1 shard_map.69
  28.4 1.6 %collective-permute-start.9 = (f32[2,128]{1,0:T(2,128)S(1)}, f32[2,128]{1,0:T(2,128)S(1)}, u32[]{:S(2)}, u32[]{:S(2)}) collective-permute-start(f32[2,128]{1,0:T(2,128)S(1)} %get-tuple-element.22), channel_id=1, source_target_pairs={{0,2},{1,3},{2,0},{3,1},{4,6},{5,7},{6,4},{7,5},{8,10},{9,11},{10,... | collective-permute-start | bytes 3080 | tf_op jit(solution)/shard_map/ppermute | solution.py:45
  29.9 0.3 collective-permute-start.11
  30.2 1.8 %collective-permute-done.9.refs_0_ = f32[2,128]{1,0:T(2,128)S(1)} collective-permute-done((f32[2,128]{1,0:T(2,128)S(1)}, f32[2,128]{1,0:T(2,128)S(1)}, u32[]{:S(2)}, u32[]{:S(2)}) %collective-permute-start.9) | collective-permute-done | bytes 1056 | tf_op jit(solution)/shard_map/ppermute | solution.py:45
  32.0 0.9 %collective-permute-done.11.refs_3_ = f32[2,128]{1,0:T(2,128)S(1)} collective-permute-done((f32[2,128]{1,0:T(2,128)S(1)}, f32[2,128]{1,0:T(2,128)S(1)}, u32[]{:S(2)}, u32[]{:S(2)}) %collective-permute-start.11) | collective-permute-done | bytes 1056 | tf_op jit(solution)/shard_map/ppermute | solution.py:45
  32.9 0.7 %shard_map.70 = f32[2,4096]{1,0:T(2,128)} custom-call(f32[2,128]{1,0:T(2,128)S(1)} %collective-permute-done.9.refs_0_, f32[2,2048]{1,0:T(2,128)S(1)} %get-tuple-element.23.refs_1_, f32[2,2176]{1,0:T(2,128)S(1)} %collective-permute-done.10.refs_2_, f32[2,128]{1,0:T(2,128)S(1)} %collective-permute-done.11.refs_3_, f32[2,128]{1,0:T(2,128)S(1)} %get-tuple-element.26.refs_4_), custom_call_target="tpu_custom_call" | custom-call | tf_op jit(solution)/shard_map/pallas_call | solution.py:276
  (7 shorter events, 0.0 us)
Async XLA Ops:
  4.3 8.0 %collective-permute-start = (f32[1,4,1024]{2,1,0:T(4,128)S(1)}, f32[1,4,1024]{2,1,0:T(4,128)S(1)}, u32[]{:S(2)}, u32[]{:S(2)}) collective-permute-start(f32[1,4,1024]{2,1,0:T(4,128)S(1)} %get-tuple-element.18), channel_id=1, source_target_pairs={{0,8},{4,12},{8,0},{12,4},{1,9},{5,13},{9,1},{13,5},{2,10},{6,14},... | collective-permute-start | bytes 49160 | tf_op jit(solution)/shard_map/ppermute | solution.py:45
  8.4 5.5 %collective-permute-start.1 = (f32[1,4,1024]{2,1,0:T(4,128)S(1)}, f32[1,4,1024]{2,1,0:T(4,128)S(1)}, u32[]{:S(2)}, u32[]{:S(2)}) collective-permute-start(f32[1,4,1024]{2,1,0:T(4,128)S(1)} %get-tuple-element.19), channel_id=1, source_target_pairs={{0,12},{4,8},{8,4},{12,0},{1,13},{5,9},{9,5},{13,1},{2,14},{6,10},... | collective-permute-start | bytes 49160 | tf_op jit(solution)/shard_map/ppermute | solution.py:45
  9.8 4.2 %collective-permute-start.2 = (f32[1,4,1024]{2,1,0:T(4,128)S(1)}, f32[1,4,1024]{2,1,0:T(4,128)S(1)}, u32[]{:S(2)}, u32[]{:S(2)}) collective-permute-start(f32[1,4,1024]{2,1,0:T(4,128)S(1)} %get-tuple-element.20), channel_id=1, source_target_pairs={{0,4},{4,0},{8,12},{12,8},{1,5},{5,1},{9,13},{13,9},{2,6},{6,2},{1... | collective-permute-start | bytes 49160 | tf_op jit(solution)/shard_map/ppermute | solution.py:45
  14.0 5.0 %collective-permute-start.5 = (bf16[1,4,1024]{2,1,0:T(4,128)(2,1)S(1)}, bf16[1,4,1024]{2,1,0:T(4,128)(2,1)S(1)}, u32[]{:S(2)}, u32[]{:S(2)}) collective-permute-start(bf16[1,4,1024]{2,1,0:T(4,128)(2,1)S(1)} %shard_map.66.after_ref.refs_0_), channel_id=1, source_target_pairs={{0,2},{1,3},{2,0},{3,1},{4,6},{5,7},{6,4},{7,5},{8,10},{9,11},{10,... | collective-permute-start | bytes 24584 | tf_op jit(solution)/shard_map/ppermute | solution.py:45
  15.6 3.5 %collective-permute-start.4 = (bf16[1,4,1024]{2,1,0:T(4,128)(2,1)S(1)}, bf16[1,4,1024]{2,1,0:T(4,128)(2,1)S(1)}, u32[]{:S(2)}, u32[]{:S(2)}) collective-permute-start(bf16[1,4,1024]{2,1,0:T(4,128)(2,1)S(1)} %shard_map.66.after_ref.refs_0_), channel_id=1, source_target_pairs={{0,1},{1,0},{2,3},{3,2},{4,5},{5,4},{6,7},{7,6},{8,9},{9,8},{10,11... | collective-permute-start | bytes 24584 | tf_op jit(solution)/shard_map/ppermute | solution.py:45
  15.6 3.5 %collective-permute-start.3 = (bf16[1,4,1024]{2,1,0:T(4,128)(2,1)S(1)}, bf16[1,4,1024]{2,1,0:T(4,128)(2,1)S(1)}, u32[]{:S(2)}, u32[]{:S(2)}) collective-permute-start(bf16[1,4,1024]{2,1,0:T(4,128)(2,1)S(1)} %shard_map.66.after_ref.refs_0_), channel_id=1, source_target_pairs={{0,3},{1,2},{2,1},{3,0},{4,7},{5,6},{6,5},{7,4},{8,11},{9,10},{10,... | collective-permute-start | bytes 24584 | tf_op jit(solution)/shard_map/ppermute | solution.py:45
  21.3 5.2 %collective-permute-start.8 = (f32[4,2048]{1,0:T(4,128)S(1)}, f32[4,2048]{1,0:T(4,128)S(1)}, u32[]{:S(2)}, u32[]{:S(2)}) collective-permute-start(f32[4,2048]{1,0:T(4,128)S(1)} %shard_map.68.refs_0_), channel_id=1, source_target_pairs={{0,8},{4,12},{8,0},{12,4},{1,9},{5,13},{9,1},{13,5},{2,10},{6,14},... | collective-permute-start | bytes 98312 | tf_op jit(solution)/shard_map/ppermute | solution.py:45
  22.6 5.7 %collective-permute-start.7 = (f32[4,2048]{1,0:T(4,128)S(1)}, f32[4,2048]{1,0:T(4,128)S(1)}, u32[]{:S(2)}, u32[]{:S(2)}) collective-permute-start(f32[4,2048]{1,0:T(4,128)S(1)} %shard_map.68.refs_0_), channel_id=1, source_target_pairs={{0,12},{4,8},{8,4},{12,0},{1,13},{5,9},{9,5},{13,1},{2,14},{6,10},... | collective-permute-start | bytes 98312 | tf_op jit(solution)/shard_map/ppermute | solution.py:45
  23.8 4.5 %collective-permute-start.6 = (f32[4,2048]{1,0:T(4,128)S(1)}, f32[4,2048]{1,0:T(4,128)S(1)}, u32[]{:S(2)}, u32[]{:S(2)}) collective-permute-start(f32[4,2048]{1,0:T(4,128)S(1)} %shard_map.68.refs_0_), channel_id=1, source_target_pairs={{0,4},{4,0},{8,12},{12,8},{1,5},{5,1},{9,13},{13,9},{2,6},{6,2},{1... | collective-permute-start | bytes 98312 | tf_op jit(solution)/shard_map/ppermute | solution.py:45
  28.4 4.6 %collective-permute-start.10 = (f32[2,2176]{1,0:T(2,128)S(1)}, f32[2,2176]{1,0:T(2,128)S(1)}, u32[]{:S(2)}, u32[]{:S(2)}) collective-permute-start(f32[2,2176]{1,0:T(2,128)S(1)} %get-tuple-element.24), channel_id=1, source_target_pairs={{0,1},{1,0},{2,3},{3,2},{4,5},{5,4},{6,7},{7,6},{8,9},{9,8},{10,11... | collective-permute-start | bytes 52232 | tf_op jit(solution)/shard_map/ppermute | solution.py:45
  28.4 3.6 %collective-permute-start.9 = (f32[2,128]{1,0:T(2,128)S(1)}, f32[2,128]{1,0:T(2,128)S(1)}, u32[]{:S(2)}, u32[]{:S(2)}) collective-permute-start(f32[2,128]{1,0:T(2,128)S(1)} %get-tuple-element.22), channel_id=1, source_target_pairs={{0,2},{1,3},{2,0},{3,1},{4,6},{5,7},{6,4},{7,5},{8,10},{9,11},{10,... | collective-permute-start | bytes 3080 | tf_op jit(solution)/shard_map/ppermute | solution.py:45
  29.9 3.0 %collective-permute-start.11 = (f32[2,128]{1,0:T(2,128)S(1)}, f32[2,128]{1,0:T(2,128)S(1)}, u32[]{:S(2)}, u32[]{:S(2)}) collective-permute-start(f32[2,128]{1,0:T(2,128)S(1)} %get-tuple-element.25), channel_id=1, source_target_pairs={{0,3},{1,2},{2,1},{3,0},{4,7},{5,6},{6,5},{7,4},{8,11},{9,10},{10,... | collective-permute-start | bytes 3080 | tf_op jit(solution)/shard_map/ppermute | solution.py:45
